TPU v7x, 32 devices: a whole 2x2x4 slice. The times are simulated.
32 devices in a mesh: blk: 8 (over y, x, core), uly: 4 (over z).
Axes of the slice: x: 2, y: 2, z: 4, core: 2. Of those that a mesh axis runs over, the one named last changes fastest.
Arguments:
- tokens: bfloat16 [4096, 2048], P(('blk', 'uly')), may hold values from -6 to 6
- segment_ids: int32 [4096], P(('blk', 'uly')), may hold values from 0 to 4, as said below
- layer_skip: int32 [5], replicated, may hold values from 0 to 1, as said below
- attn_gain: bfloat16 [2048], P(('blk', 'uly')), may hold values from 0.099609375 to 1.8984375
- w_query: bfloat16 [2048, 2048], P(('blk', 'uly')), may hold values from -0.125 to 0.125
- w_key: bfloat16 [2048, 512], P(('blk', 'uly')), may hold values from -0.125 to 0.125
- w_value: bfloat16 [2048, 512], P(('blk', 'uly')), may hold values from -0.125 to 0.125
- w_output: bfloat16 [2048, 2048], P(None, ('blk', 'uly')), may hold values from -0.5 to 0.5
- mlp_gain: bfloat16 [2048], P(('blk', 'uly')), may hold values from 0.099609375 to 1.8984375
- w_gate: bfloat16 [2048, 5632], P(('blk', 'uly')), may hold values from -0.125 to 0.125
- w_up: bfloat16 [2048, 5632], P(('blk', 'uly')), may hold values from -0.125 to 0.125
- w_down: bfloat16 [5632, 2048], P(None, ('blk', 'uly')), may hold values from -0.078125 to 0.078125
- cotangent: bfloat16 [4096, 2048], P(('blk', 'uly')), may hold values from -6 to 6
Outputs:
- output: bfloat16 [4096, 2048], P(('blk', 'uly'))
- grad_tokens: float32 [4096, 2048], P(('blk', 'uly'))
- grad_attn_gain: float32 [2048], P(('blk', 'uly'))
- grad_query: float32 [2048, 2048], P(('blk', 'uly'))
- grad_key: float32 [2048, 512], P(('blk', 'uly'))
- grad_value: float32 [2048, 512], P(('blk', 'uly'))
- grad_output: float32 [2048, 2048], P(None, ('blk', 'uly'))
- grad_mlp_gain: float32 [2048], P(('blk', 'uly'))
- grad_gate: float32 [2048, 5632], P(('blk', 'uly'))
- grad_up: float32 [2048, 5632], P(('blk', 'uly'))
- grad_down: float32 [5632, 2048], P(None, ('blk', 'uly'))
Inputs may be any that keep to these rules, and one draw needn't show every extreme that they name: `segment_ids`: Non-decreasing along the row; every number is used; documents 0 and 1 lie within the first 127 tokens, documents 3 and 4 within the last 127 tokens, and document 2 takes all tokens between them. `layer_skip`: document 2 never skips; exactly one of documents 0 and 1 skips.
All inputs are finite; a program needn't handle non-finite values.
Results may differ from a plain program's by a relative error of at most 0.02.
Values may be sent and summed in bfloat16 or wider, within the bound.
No kernel may reach another device: no remote copies, remote signals or barrier semaphores. Data moves between devices by JAX's collectives and lax.ppermute only.
A program may use at most 384 MiB of HBM per device.

v0:
```python
import jax
import jax.numpy as jnp
from jax import lax
from jax.sharding import PartitionSpec as P

HEADS = 16
KV_HEADS = 4
HEAD_DIM = 128


EPS = 1e-05
THETA = 10000.0


def passed_along(block, axis, distance):
    devices = range(lax.axis_size(axis))
    route = [(i - distance, i) for i in devices if i - distance in devices]
    return lax.ppermute(block, axis, route)


def from_behind(array, axis, by):
    devices = lax.axis_size(axis)
    return lax.ppermute(array, axis, [(i, (i + by) % devices) for i in range(devices)])


def angle_tables(start, count, head_dim):
    half = head_dim // 2
    spots = (start + lax.iota(jnp.int32, count)).astype(jnp.float32)
    rates = jnp.power(THETA, -lax.iota(jnp.int32, half).astype(jnp.float32) / half)
    angles = spots[:, None] * rates[None, :]
    return (jnp.cos(angles), jnp.sin(angles))


def rotate(values, cosine_table, sine_table):
    half = values.shape[-1] // 2
    first_half = values[..., :half]
    second_half = values[..., half:]
    cosine = cosine_table[:, None, :]
    sine_part = sine_table[:, None, :]
    return jnp.concatenate(
        [
            first_half * cosine - second_half * sine_part,
            second_half * cosine + first_half * sine_part,
        ],
        axis=-1,
    )


def rotate_back(values, cosine_table, sine_table):
    half = values.shape[-1] // 2
    first_half = values[..., :half]
    second_half = values[..., half:]
    cosine = cosine_table[:, None, :]
    sine_part = sine_table[:, None, :]
    return jnp.concatenate(
        [
            first_half * cosine + second_half * sine_part,
            second_half * cosine - first_half * sine_part,
        ],
        axis=-1,
    )


def outer_sum(left, right):
    return lax.dot_general(
        left, right, (((0,), (0,)), ((), ())), preferred_element_type=jnp.float32
    )


def times_transposed(left, right):
    return lax.dot_general(
        left, right, (((1,), (1,)), ((), ())), preferred_element_type=jnp.float32
    )


def gather_weights(gain, first, second, third):
    return (
        lax.all_gather(gain, ("blk", "uly"), axis=0, tiled=True),
        lax.all_gather(first, ("blk", "uly"), axis=0, tiled=True),
        lax.all_gather(second, ("blk", "uly"), axis=0, tiled=True),
        lax.all_gather(third, ("blk", "uly"), axis=1, tiled=True),
    )


def shift_pair(key_block, value_block):
    return passed_along((key_block, value_block), "blk", 1)


def pass_grads(grad_k, grad_v):
    return (
        from_behind(grad_k.astype(jnp.bfloat16), "blk", 1).astype(grad_k.dtype),
        from_behind(grad_v.astype(jnp.bfloat16), "blk", 1).astype(grad_v.dtype),
    )


def to_tokens(values):
    return lax.all_to_all(values, "uly", split_axis=0, concat_axis=1, tiled=True)


def per_device(
    tokens,
    segment_ids,
    layer_skip,
    attn_gain,
    w_query,
    w_key,
    w_value,
    w_output,
    mlp_gain,
    w_gate,
    w_up,
    w_down,
    cotangent,
):
    cycle_size = lax.axis_size("blk")
    group_size = lax.axis_size("uly")
    cycle_rank = lax.axis_index("blk")
    member = lax.axis_index("uly")
    tok_rows = tokens.shape[0]
    block_rows = group_size * tok_rows
    local_kv = KV_HEADS // group_size
    share = HEADS // KV_HEADS
    scale = HEAD_DIM ** (-0.5)
    kv_width = KV_HEADS * HEAD_DIM
    query_part = HEADS * HEAD_DIM // group_size
    kv_part = kv_width // group_size
    turns = cycle_size - 1
    segments = lax.all_gather(segment_ids, ("blk", "uly"), axis=0, tiled=True)
    first_row = (cycle_rank * group_size + member) * tok_rows
    doc_index = lax.iota(jnp.int32, layer_skip.shape[0])
    skipped = jnp.sum(
        jnp.where(segment_ids[:, None] == doc_index[None, :], layer_skip[None, :], 0), axis=1
    )
    keep = (1 - skipped).astype(jnp.float32)[:, None]
    key_value_shard = jnp.concatenate([w_key, w_value], axis=1)

    def attn_weights():
        return gather_weights(attn_gain, w_query, key_value_shard, w_output)

    def mlp_weights():
        return gather_weights(mlp_gain, w_gate, w_up, w_down)

    inputs = tokens.astype(jnp.float32)
    attn_set = attn_weights()
    gain_one = attn_set[0].astype(jnp.float32)
    scale_one = lax.rsqrt(jnp.mean(inputs * inputs, axis=-1, keepdims=True) + EPS)
    normed_one = (inputs * scale_one * gain_one).astype(jnp.bfloat16)
    query = jnp.dot(normed_one, attn_set[1], preferred_element_type=jnp.float32)
    key_value = jnp.dot(normed_one, attn_set[2], preferred_element_type=jnp.float32)
    key = key_value[:, :kv_width]
    value = key_value[:, kv_width:]
    cosine_table, sine_table = angle_tables(first_row, tok_rows, HEAD_DIM)
    query_rot = (
        rotate(query.reshape(tok_rows, HEADS, HEAD_DIM), cosine_table, sine_table)
        .astype(jnp.bfloat16)
        .reshape(tok_rows, HEADS * HEAD_DIM)
    )
    key_rot = (
        rotate(key.reshape(tok_rows, KV_HEADS, HEAD_DIM), cosine_table, sine_table)
        .astype(jnp.bfloat16)
        .reshape(tok_rows, kv_width)
    )
    value_low = value.astype(jnp.bfloat16)
    query_heads, key_heads, value_heads = (
        lax.all_to_all(query_rot, "uly", split_axis=1, concat_axis=0, tiled=True),
        lax.all_to_all(key_rot, "uly", split_axis=1, concat_axis=0, tiled=True),
        lax.all_to_all(value_low, "uly", split_axis=1, concat_axis=0, tiled=True),
    )
    queries = query_heads.reshape(block_rows, local_kv, share, HEAD_DIM)
    keys = key_heads.reshape(block_rows, local_kv, HEAD_DIM)
    values = value_heads.reshape(block_rows, local_kv, HEAD_DIM)
    row_ids = lax.iota(jnp.int32, block_rows)
    query_seg = lax.dynamic_slice_in_dim(segments, cycle_rank * block_rows, block_rows, 0)
    query_spot = cycle_rank * block_rows + row_ids

    def allowed_mask(key_index):
        safe_index = jnp.maximum(key_index, 0)
        key_seg = lax.dynamic_slice_in_dim(segments, safe_index * block_rows, block_rows, 0)
        key_spot = safe_index * block_rows + row_ids
        return (query_seg[:, None] == key_seg[None, :]) & (query_spot[:, None] >= key_spot[None, :])

    def is_active(key_index):
        safe_index = jnp.maximum(key_index, 0)
        return (key_index >= 0) & (
            segments[safe_index * block_rows + block_rows - 1] >= query_seg[0]
        )

    def masked_scores(key_block, key_index):
        raw = (
            jnp.einsum("qhgd,khd->qhgk", queries, key_block, preferred_element_type=jnp.float32)
            * scale
        )
        return jnp.where(allowed_mask(key_index)[:, None, None, :], raw, -1e30)

    def forward_block(state, key_block, value_block, key_index):
        top, total, accum = state
        scores = masked_scores(key_block, key_index)
        new_top = jnp.maximum(top, jnp.max(scores, axis=-1))
        weights = jnp.exp(scores - new_top[..., None])
        fade = jnp.exp(top - new_top)
        total = total * fade + jnp.sum(weights, axis=-1)
        accum = accum * fade[..., None] + jnp.einsum(
            "qhgk,khd->qhgd",
            weights.astype(jnp.bfloat16),
            value_block,
            preferred_element_type=jnp.float32,
        )
        return (new_top, total, accum)

    start_state = (
        jnp.full((block_rows, local_kv, share), -1e30, jnp.float32),
        jnp.zeros((block_rows, local_kv, share), jnp.float32),
        jnp.zeros((block_rows, local_kv, share, HEAD_DIM), jnp.float32),
    )
    state = forward_block(start_state, keys, values, cycle_rank)

    def forward_turn(turn, carry):
        state, key_block, value_block = carry
        key_block, value_block = shift_pair(key_block, value_block)
        key_index = cycle_rank - turn
        state = lax.cond(
            is_active(key_index),
            lambda: forward_block(state, key_block, value_block, key_index),
            lambda: state,
        )
        return (state, key_block, value_block)

    top, total, accum = lax.fori_loop(1, turns + 1, forward_turn, (state, keys, values))[0]
    attn_exact = accum / total[..., None]
    log_total = top + jnp.log(total)
    attn_low = attn_exact.astype(jnp.bfloat16).reshape(block_rows, query_part)
    attn_rows = to_tokens(attn_low)
    proj = jnp.dot(attn_rows, attn_set[3], preferred_element_type=jnp.float32)
    middle = inputs + keep * proj
    mlp_set = mlp_weights()
    gain_two = mlp_set[0].astype(jnp.float32)
    scale_two = lax.rsqrt(jnp.mean(middle * middle, axis=-1, keepdims=True) + EPS)
    normed_two = (middle * scale_two * gain_two).astype(jnp.bfloat16)
    gate = jnp.dot(normed_two, mlp_set[1], preferred_element_type=jnp.float32)
    up = jnp.dot(normed_two, mlp_set[2], preferred_element_type=jnp.float32)
    sigmoid_gate = jax.nn.sigmoid(gate)
    silu_gate = gate * sigmoid_gate
    hidden = (silu_gate * up).astype(jnp.bfloat16)
    ffn = jnp.dot(hidden, mlp_set[3], preferred_element_type=jnp.float32)
    output = (middle + keep * ffn).astype(jnp.bfloat16)
    mlp_back = mlp_weights()
    attn_back = attn_weights()
    grad_result = cotangent.astype(jnp.float32)
    grad_ffn = (keep * grad_result).astype(jnp.bfloat16)
    grad_down = lax.psum_scatter(
        outer_sum(hidden, grad_ffn), ("blk", "uly"), scatter_dimension=1, tiled=True
    )
    grad_hidden = times_transposed(grad_ffn, mlp_back[3])
    grad_gate_act = (grad_hidden * up * sigmoid_gate * (1.0 + gate * (1.0 - sigmoid_gate))).astype(
        jnp.bfloat16
    )
    grad_up_act = (grad_hidden * silu_gate).astype(jnp.bfloat16)
    grad_normed_two = times_transposed(grad_gate_act, mlp_back[1]) + times_transposed(
        grad_up_act, mlp_back[2]
    )
    gained_two = grad_normed_two * gain_two
    grad_gain_two = jnp.sum(grad_normed_two * middle * scale_two, axis=0)
    grad_middle = (
        grad_result
        + scale_two * gained_two
        - middle * scale_two**3 * jnp.mean(gained_two * middle, axis=-1, keepdims=True)
    )
    grad_mlp_gain, grad_gate, grad_up = (
        lax.psum_scatter(grad_gain_two, ("blk", "uly"), scatter_dimension=0, tiled=True),
        lax.psum_scatter(
            outer_sum(normed_two, grad_gate_act), ("blk", "uly"), scatter_dimension=0, tiled=True
        ),
        lax.psum_scatter(
            outer_sum(normed_two, grad_up_act), ("blk", "uly"), scatter_dimension=0, tiled=True
        ),
    )
    grad_proj = (keep * grad_middle).astype(jnp.bfloat16)
    grad_attn = times_transposed(grad_proj, attn_back[3]).astype(jnp.bfloat16)
    grad_heads = lax.all_to_all(grad_attn, "uly", split_axis=1, concat_axis=0, tiled=True)
    grad_attended = grad_heads.reshape(block_rows, local_kv, share, HEAD_DIM)
    delta = jnp.sum(grad_attended.astype(jnp.float32) * attn_exact, axis=-1)

    def backward_block(grads, key_block, value_block, key_index):
        grad_q, grad_k, grad_v = grads
        scores = masked_scores(key_block, key_index)
        probs = jnp.exp(scores - log_total[..., None])
        grad_probs = jnp.einsum(
            "qhgd,khd->qhgk", grad_attended, value_block, preferred_element_type=jnp.float32
        )
        grad_scores = (probs * (grad_probs - delta[..., None])).astype(jnp.bfloat16)
        grad_q = grad_q + jnp.einsum(
            "qhgk,khd->qhgd", grad_scores, key_block, preferred_element_type=jnp.float32
        )
        grad_k = grad_k + jnp.einsum(
            "qhgk,qhgd->khd", grad_scores, queries, preferred_element_type=jnp.float32
        )
        grad_v = grad_v + jnp.einsum(
            "qhgk,qhgd->khd",
            probs.astype(jnp.bfloat16),
            grad_attended,
            preferred_element_type=jnp.float32,
        )
        return (grad_q, grad_k, grad_v)

    zero_query = jnp.zeros((block_rows, local_kv, share, HEAD_DIM), jnp.float32)
    zero_pair = jnp.zeros((block_rows, local_kv, HEAD_DIM), jnp.float32)
    grad_q, grad_k, grad_v = backward_block(
        (zero_query, zero_pair, zero_pair), keys, values, cycle_rank
    )

    def backward_turn(turn, carry):
        grad_q, grad_k, grad_v, key_block, value_block = carry
        grad_k, grad_v = pass_grads(grad_k, grad_v)
        key_block, value_block = shift_pair(key_block, value_block)
        key_index = cycle_rank - turn
        grad_q, grad_k, grad_v = lax.cond(
            is_active(key_index),
            lambda: backward_block((grad_q, grad_k, grad_v), key_block, value_block, key_index),
            lambda: (grad_q, grad_k, grad_v),
        )
        return (grad_q, grad_k, grad_v, key_block, value_block)

    grad_q, grad_k, grad_v, key_last, value_last = lax.fori_loop(
        1, turns + 1, backward_turn, (grad_q, grad_k, grad_v, keys, values)
    )
    grad_k, grad_v = pass_grads(grad_k, grad_v)
    grad_query_rot = (grad_q * scale).astype(jnp.bfloat16).reshape(block_rows, query_part)
    grad_key_rot = (grad_k * scale).astype(jnp.bfloat16).reshape(block_rows, kv_part)
    grad_value_low = grad_v.astype(jnp.bfloat16).reshape(block_rows, kv_part)
    joined = jnp.concatenate([grad_query_rot, grad_key_rot, grad_value_low], axis=1)
    returned = to_tokens(joined).reshape(tok_rows, group_size, query_part + 2 * kv_part)
    back_query = returned[:, :, :query_part].reshape(tok_rows, HEADS * HEAD_DIM)
    back_key = returned[:, :, query_part : query_part + kv_part].reshape(tok_rows, kv_width)
    back_value = returned[:, :, query_part + kv_part :].reshape(tok_rows, kv_width)
    grad_query_tok = (
        rotate_back(
            back_query.astype(jnp.float32).reshape(tok_rows, HEADS, HEAD_DIM),
            cosine_table,
            sine_table,
        )
        .astype(jnp.bfloat16)
        .reshape(tok_rows, HEADS * HEAD_DIM)
    )
    grad_key_tok = (
        rotate_back(
            back_key.astype(jnp.float32).reshape(tok_rows, KV_HEADS, HEAD_DIM),
            cosine_table,
            sine_table,
        )
        .astype(jnp.bfloat16)
        .reshape(tok_rows, kv_width)
    )
    grad_normed_one = (
        times_transposed(grad_query_tok, attn_back[1])
        + times_transposed(grad_key_tok, attn_back[2][:, :kv_width])
        + times_transposed(back_value, attn_back[2][:, kv_width:])
    )
    gained_one = grad_normed_one * gain_one
    grad_gain_one = jnp.sum(grad_normed_one * inputs * scale_one, axis=0)
    grad_tokens = (
        grad_middle
        + scale_one * gained_one
        - inputs * scale_one**3 * jnp.mean(gained_one * inputs, axis=-1, keepdims=True)
    )
    grad_attn_gain, grad_query, grad_key, grad_value, grad_output = (
        lax.psum_scatter(grad_gain_one, ("blk", "uly"), scatter_dimension=0, tiled=True),
        lax.psum_scatter(
            outer_sum(normed_one, grad_query_tok), ("blk", "uly"), scatter_dimension=0, tiled=True
        ),
        lax.psum_scatter(
            outer_sum(normed_one, grad_key_tok), ("blk", "uly"), scatter_dimension=0, tiled=True
        ),
        lax.psum_scatter(
            outer_sum(normed_one, back_value), ("blk", "uly"), scatter_dimension=0, tiled=True
        ),
        lax.psum_scatter(
            outer_sum(attn_rows, grad_proj), ("blk", "uly"), scatter_dimension=1, tiled=True
        ),
    )
    return (
        output,
        grad_tokens,
        grad_attn_gain,
        grad_query,
        grad_key,
        grad_value,
        grad_output,
        grad_mlp_gain,
        grad_gate,
        grad_up,
        grad_down,
    )


def solution(mesh):
    placed = (
        P(("blk", "uly"), None),
        P(("blk", "uly")),
        P(),
        P(("blk", "uly")),
        P(("blk", "uly"), None),
        P(("blk", "uly"), None),
        P(("blk", "uly"), None),
        P(None, ("blk", "uly")),
        P(("blk", "uly")),
        P(("blk", "uly"), None),
        P(("blk", "uly"), None),
        P(None, ("blk", "uly")),
        P(("blk", "uly"), None),
    )
    return jax.shard_map(
        per_device,
        mesh=mesh,
        in_specs=placed,
        out_specs=(
            P(("blk", "uly"), None),
            P(("blk", "uly"), None),
            P(("blk", "uly")),
            P(("blk", "uly"), None),
            P(("blk", "uly"), None),
            P(("blk", "uly"), None),
            P(None, ("blk", "uly")),
            P(("blk", "uly")),
            P(("blk", "uly"), None),
            P(("blk", "uly"), None),
            P(None, ("blk", "uly")),
        ),
        check_vma=False,
    )
```

profile of v0, /device:TPU:0, one launch (start us, length us, event | category | flops | bytes accessed | tf_op | source)
XLA Modules:
  0.0 4945.1 jit_solution(9598329297964960772)
XLA Ops:
  13.8 42.2 all-reduce.5
  58.2 18.3 all-gather.8.cloned.1.call-done
  85.3 70.1 %all-gather.10.cloned.1.call-done = bf16[2048,2048]{1,0:T(8,128)(2,1)} async-done(((bf16[64,2048]{1,0:T(8,128)(2,1)}), bf16[2048,2048]{1,0:T(8,128)(2,1)}) %all-gather.10.cloned.1.call-update) | async-done | bytes 8388624 | tf_op jit(solution)/shard_map/all_gather | solution.py:79
  155.5 6.8 fusion.137
  167.3 8.8 all-to-all-done
  179.6 79.7 %all-gather = s32[32,1,128]{2,1,0:T(1,128)S(1)} all-gather(s32[1,1,128]{2,1,0:T(1,128)S(1)} %bitcast.355), channel_id=1, replica_groups=mesh['blk'=8,'uly'=4] {'blk','uly'}, dimensions={0}, use_global_device_ids=true | all-gather | bytes 16896 | tf_op jit(solution)/shard_map/all_gather | solution.py:128
  274.2 93.6 %while.52 = (s32[]{:T(128)}, f32[512,1,4]{0,2,1:T(4,128)S(1)}, f32[512,1,4]{0,2,1:T(4,128)S(1)}, f32[512,1,4,128]{3,0,2,1:T(8,128)S(1)}, bf16[512,1,128]{2,0,1:T...) while((s32[]{:T(128)}, f32[512,1,4]{0,2,1:T(4,128)S(1)}, ...), condition=%wide.region_9.10_spmd.clone, body=%wide.region_4.9_spmd.clone.sunk | while | flops 549723136 | bytes 18242116 | solution.py:228
  283.9 7.2 collective-permute-start
  293.7 6.7 collective-permute-start.1
  300.3 8.8 collective-permute-start
  313.6 5.3 collective-permute-start
  321.5 7.8 collective-permute-start.1
  336.2 6.7 collective-permute-start.1
  343.0 6.8 collective-permute-start
  352.3 8.6 collective-permute-start.1
  375.5 28.2 all-to-all-done.3
  404.7 6.9 multiply_reduce_fusion.3
  412.4 13.2 fusion.145
  425.7 128.0 %all-gather.14.cloned.1.call-done = bf16[2048,5632]{1,0:T(8,128)(2,1)} async-done(((bf16[64,5632]{1,0:T(8,128)(2,1)}), bf16[2048,5632]{1,0:T(8,128)(2,1)}) %all-gather.14.cloned.1.call-update) | async-done | bytes 23068688 | tf_op jit(solution)/shard_map/all_gather | solution.py:79
  553.7 12.3 fusion.144
  566.0 133.2 %all-gather.18.cloned.1.call-done = bf16[5632,2048]{0,1:T(8,128)(2,1)} async-done(((bf16[5632,64]{0,1:T(8,128)(2,1)}), bf16[5632,2048]{0,1:T(8,128)(2,1)}) %all-gather.18.cloned.1.call-update) | async-done | bytes 23068688 | tf_op jit(solution)/shard_map/all_gather | solution.py:81
  699.2 14.7 multiply_convert_fusion
  713.8 12.8 fusion.146
  726.7 13.9 multiply_reduce_fusion
  752.8 14.6 all-to-all-done.4
  769.3 5.0 multiply_reduce_fusion.1
  794.0 151.1 %while.53 = (s32[]{:T(128)}, f32[512,1,4,128]{3,0,2,1:T(8,128)S(1)}, f32[512,1,128]{2,0,1:T(8,128)S(1)}, f32[512,1,128]{2,0,1:T(8,128)}, bf16[512,1,128]{2,0,1:T...) while((s32[]{:T(128)}, ...), condition=%wide.region_16.17_spmd.clone, body=%wide.region_13.0_spmd.clone.sunk | while | flops 1354105856 | bytes 31636192 | solution.py:323
  811.9 8.8 collective-permute-start.2
  838.6 8.8 collective-permute-start.3
  864.6 11.4 collective-permute-start.5
  890.1 10.1 collective-permute-start.4
  922.9 8.8 collective-permute-start.2
  947.4 9.2 collective-permute-start.7
  962.4 20.4 all_to_all.90
  989.4 8.2 fusion.129
  1001.4 8.2 fusion.135
  1010.9 19.1 fusion.119
  1031.1 19.3 fusion.149
  1050.4 19.3 fusion.148
  1070.9 13.0 fusion.75
  1083.9 6.5 fusion.147
  1092.3 39.6 all-reduce.4
  1134.4 148.5 %reduce-scatter.10.cloned.1.call-done = f32[64,512]{1,0:T(8,128)} async-done(((f32[2048,512]{1,0:T(8,128)}), f32[64,512]{1,0:T(8,128)}) %reduce-scatter.10.cloned.1.call-update) | async-done | bytes 131088 | tf_op jit(solution)/shard_map/reduce_scatter | solution.py:370
  1282.9 366.1 %reduce-scatter.14.cloned.1.call-done = f32[2048,64]{0,1:T(8,128)} async-done(((f32[2048,2048]{0,1:T(8,128)}), f32[2048,64]{0,1:T(8,128)}) %reduce-scatter.14.cloned.1.call-update) | async-done | bytes 524304 | tf_op jit(solution)/shard_map/reduce_scatter | solution.py:376
  1649.0 364.9 %reduce-scatter.8.cloned.1.call-done = f32[64,2048]{1,0:T(8,128)} async-done(((f32[2048,2048]{1,0:T(8,128)}), f32[64,2048]{1,0:T(8,128)}) %reduce-scatter.8.cloned.1.call-update) | async-done | bytes 524304 | tf_op jit(solution)/shard_map/reduce_scatter | solution.py:367
  2013.9 973.2 %reduce-scatter.20.cloned.1.call-done = f32[5632,64]{0,1:T(8,128)} async-done(((f32[5632,2048]{0,1:T(8,128)}), f32[5632,64]{0,1:T(8,128)}) %reduce-scatter.20.cloned.1.call-update) | async-done | bytes 1441808 | tf_op jit(solution)/shard_map/reduce_scatter | solution.py:250
  2987.1 975.5 %reduce-scatter.18.cloned.1.call-done = f32[64,5632]{1,0:T(8,128)} async-done(((f32[2048,5632]{1,0:T(8,128)}), f32[64,5632]{1,0:T(8,128)}) %reduce-scatter.18.cloned.1.call-update) | async-done | bytes 1441808 | tf_op jit(solution)/shard_map/reduce_scatter | solution.py:273
  3962.7 975.7 %reduce-scatter.16.cloned.1.call-done = f32[64,5632]{1,0:T(8,128)} async-done(((f32[2048,5632]{1,0:T(8,128)}), f32[64,5632]{1,0:T(8,128)}) %reduce-scatter.16.cloned.1.call-update) | async-done | bytes 1441808 | tf_op jit(solution)/shard_map/reduce_scatter | solution.py:270
  (407 shorter events, 229.5 us)
Async XLA Ops:
  7.2 69.4 %all-gather.8.cloned.1.call-start = ((), (), s32[]{:S(2)}) async-start(), calls=%async_computation.13 | async-start | bytes 4325376 | tf_op jit(solution)/shard_map/all_gather | solution.py:80
  8.8 146.6 %all-gather.10.cloned.1.call-start = ((), (), s32[]{:S(2)}) async-start(), calls=%async_computation.14 | async-start | bytes 8650752 | tf_op jit(solution)/shard_map/all_gather | solution.py:79
  9.6 395.1 %all-gather.12.cloned.1.call-start = ((), (), s32[]{:S(2)}) async-start(), calls=%async_computation.15 | async-start | bytes 8650752 | tf_op jit(solution)/shard_map/all_gather | solution.py:81
  10.3 402.1 %all-gather.16.cloned.1.call-start = ((), (), s32[]{:S(2)}) async-start(), calls=%async_computation.17 | async-start | bytes 23789568 | tf_op jit(solution)/shard_map/all_gather | solution.py:80
  10.9 542.7 %all-gather.14.cloned.1.call-start = ((), (), s32[]{:S(2)}) async-start(), calls=%async_computation.16 | async-start | bytes 23789568 | tf_op jit(solution)/shard_map/all_gather | solution.py:79
  11.5 687.7 %all-gather.18.cloned.1.call-start = ((), (), s32[]{:S(2)}) async-start(), calls=%async_computation.18 | async-start | bytes 23789568 | tf_op jit(solution)/shard_map/all_gather | solution.py:81
  80.3 82.0 %all-to-all-start.2 = ((bf16[128,4,128]{2,0,1:T(8,128)(2,1)}), bf16[128,4,128]{2,0,1:T(8,128)(2,1)}, u32[]{:S(2)}, u32[]{:S(2)}) async-start(bf16[128,4,128]{2,0,1:T(8,128)(2,1)} %copy_bitcast_fusion.1), calls=%async_computation.2 | async-start | bytes 262144 | tf_op jit(solution)/shard_map/all_to_all | solution.py:167
  162.3 13.8 all-to-all-start
  176.1 85.5 %all-to-all-start.1 = ((bf16[128,4,512]{0,2,1:T(8,128)(2,1)}), bf16[128,4,512]{0,2,1:T(8,128)(2,1)S(1)}, u32[]{:S(2)}, u32[]{:S(2)}) async-start(bf16[128,4,512]{0,2,1:T(8,128)(2,1)} %bitcast.45), calls=%async_computation.1 | async-start | bytes 1048576 | tf_op jit(solution)/shard_map/all_to_all | solution.py:165
  279.4 14.2 collective-permute-start.1
  283.9 9.7 collective-permute-start
  293.7 17.9 collective-permute-start.1
  300.3 11.2 collective-permute-start
  311.6 9.8 collective-permute-start.1
  321.5 14.6 collective-permute-start.1
  336.2 16.0 collective-permute-start.1
  343.0 9.3 collective-permute-start
  352.3 15.4 collective-permute-start.1
  371.3 32.4 all-to-all-start.3
  748.0 19.4 all-to-all-start.4
  752.1 382.3 %reduce-scatter.12.cloned.1.call-start = ((), (), s32[]{:S(2)}) async-start(), calls=%async_computation.21 | async-start | bytes 4325376 | tf_op jit(solution)/shard_map/reduce_scatter | solution.py:373
  794.6 11.7 collective-permute-start.2
  796.3 11.1 collective-permute-start.3
  797.6 11.3 collective-permute-start.5
  811.9 19.6 collective-permute-start.2
  822.3 10.1 collective-permute-start.3
  823.0 11.1 collective-permute-start.5
  837.0 17.4 collective-permute-start.2
  838.6 16.7 collective-permute-start.3
  847.4 9.5 collective-permute-start.5
  859.8 20.6 collective-permute-start.2
  864.6 16.7 collective-permute-start.3
  864.6 18.3 collective-permute-start.5
  885.9 17.4 collective-permute-start.2
  887.5 16.7 collective-permute-start.3
  887.5 18.3 collective-permute-start.5
  890.1 15.8 collective-permute-start.4
  910.4 9.5 collective-permute-start.5
  922.9 17.4 collective-permute-start.2
  933.3 9.5 collective-permute-start.5
  947.4 13.7 collective-permute-start.6
  947.4 15.0 collective-permute-start.7
  985.9 297.0 %reduce-scatter.10.cloned.1.call-start = ((), (), s32[]{:S(2)}) async-start(), calls=%async_computation.20 | async-start | bytes 4325376 | tf_op jit(solution)/shard_map/reduce_scatter | solution.py:370
  989.3 659.7 %reduce-scatter.14.cloned.1.call-start = ((), (), s32[]{:S(2)}) async-start(), calls=%async_computation.22 | async-start | bytes 17301504 | tf_op jit(solution)/shard_map/reduce_scatter | solution.py:376
  997.6 1016.3 %reduce-scatter.8.cloned.1.call-start = ((), (), s32[]{:S(2)}) async-start(), calls=%async_computation.19 | async-start | bytes 17301504 | tf_op jit(solution)/shard_map/reduce_scatter | solution.py:367
  1009.6 1977.5 %reduce-scatter.20.cloned.1.call-start = ((), (), s32[]{:S(2)}) async-start(), calls=%async_computation.25 | async-start | bytes 47579136 | tf_op jit(solution)/shard_map/reduce_scatter | solution.py:250
  1030.0 2932.6 %reduce-scatter.18.cloned.1.call-start = ((), (), s32[]{:S(2)}) async-start(), calls=%async_computation.24 | async-start | bytes 47579136 | tf_op jit(solution)/shard_map/reduce_scatter | solution.py:273
  1050.3 3888.0 %reduce-scatter.16.cloned.1.call-start = ((), (), s32[]{:S(2)}) async-start(), calls=%async_computation.23 | async-start | bytes 47579136 | tf_op jit(solution)/shard_map/reduce_scatter | solution.py:270
  (62 other events, 2942.9 us)
Sparse Core Ops, SparseCore 0:
  11.6 64.9 all-gather.7
  79.5 75.9 all-gather.9
  158.4 80.5 all-gather.11
  241.7 167.1 all-gather.15
  411.6 141.9 all-gather.13
  556.3 142.7 all-gather.17
  986.0 147.4 reduce-scatter.11
  1136.4 146.4 reduce-scatter.9
  1285.8 363.2 reduce-scatter.13
  1651.7 362.1 reduce-scatter.7
  2016.8 970.2 reduce-scatter.19
  2989.9 972.7 reduce-scatter.17
  3965.6 972.7 reduce-scatter.15
where the time goes:
time: 4950 us
  waiting for transfers between devices  4210 us (85%)
  matrix products  205 us (4%)
  starting transfers between devices  185 us (4%)
  blocking collectives  182 us (4%)
  local copies, waits for them, and re-layouts  66.8 us (1%)
  other arithmetic  59.2 us (1%)
    reduce_scatter x1, waiting for transfers between devices, per_device(): lax.psum_scatter(outer_sum(normed_two, grad_gate_act), ('blk', 'uly'), sc...  976 us
    reduce_scatter x1, waiting for transfers between devices, per_device(): lax.psum_scatter(outer_sum(normed_two, grad_up_act), ('blk', 'uly'), scat...  976 us
    reduce_scatter x1, waiting for transfers between devices, per_device(): lax.psum_scatter(outer_sum(hidden, grad_ffn), ('blk', 'uly'), scatter_dim...  973 us
    reduce_scatter x1, waiting for transfers between devices, per_device(): lax.psum_scatter(outer_sum(attn_rows, grad_proj), ('blk', 'uly'), scatter...  366 us
    reduce_scatter x1, waiting for transfers between devices, per_device(): lax.psum_scatter(outer_sum(normed_one, grad_query_tok), ('blk', 'uly'), s...  365 us
    all_gather x2, waiting for transfers between devices, gather_weights(): lax.all_gather(first, ('blk', 'uly'), axis=0, tiled=True)  198 us
    reduce_scatter x1, waiting for transfers between devices, per_device(): lax.psum_scatter(outer_sum(normed_one, grad_key_tok), ('blk', 'uly'), sca...  149 us
    all_gather x2, waiting for transfers between devices, gather_weights(): lax.all_gather(third, ('blk', 'uly'), axis=1, tiled=True)  133 us
  transfers between devices with their start and end apart: 62, of which 15 were waited for; matrix products, arithmetic and copies ran while one was open for 4% of the time, Pallas kernels for 0%

commit v1 on v0

v1 whole, which is shorter than its diff:
```python
import functools

import jax
import jax.numpy as jnp
from jax import lax
from jax.experimental import pallas as pl
from jax.experimental.pallas import tpu as pltpu
from jax.sharding import Mesh
from jax.sharding import PartitionSpec as P

HEADS = 16
KV_HEADS = 4
HEAD_DIM = 128
SHARE = HEADS // KV_HEADS

EPS = 1e-05
THETA = 10000.0
LOG2E = 1.4426950408889634
SCALE = HEAD_DIM ** (-0.5)
FAR = 1e30

AXES = ("far", "x", "core", "zh", "zl")
TEAM = ("x", "zl")

BF = jnp.bfloat16
F32 = jnp.float32


def dot(left, right, left_dim=1, right_dim=0):
    return lax.dot_general(
        left, right, (((left_dim,), (right_dim,)), ((), ())), preferred_element_type=F32
    )


def turned(values, cosine, sine):
    return values * cosine + pltpu.roll(values, HEAD_DIM // 2, axis=1) * sine


def visible(kpos, qpos, qstart):
    return (kpos <= qpos) & (kpos >= qstart)


def is_mixed(starts, base, run):
    mixed = False
    for start in starts:
        inside = (start > base) & (start < base + run)
        mixed = inside if mixed is False else (mixed | inside)
    return mixed


def run_row(meta, sizes, number, run):
    far_n, zh_n = sizes
    far, core, zh = (meta[i] for i in range(3))
    zh_r = lax.rem(number, zh_n)
    core_r = lax.rem(number // zh_n, 2)
    x_r = lax.rem(number // (2 * zh_n), 2)
    far_r = number // (4 * zh_n)
    slot = ((core_r ^ core) * far_n + (far_r ^ far)) * zh_n + (zh_r ^ zh)
    return pl.multiple_of((slot * 2 + x_r) * run, run)


def natural_slot(meta, sizes, i):
    far_n, zh_n = sizes
    far, core, zh = (meta[k] for k in range(3))
    zh_i = i % zh_n if isinstance(i, int) else lax.rem(i, zh_n)
    far_i = i // zh_n % far_n if isinstance(i, int) else lax.rem(i // zh_n, far_n)
    core_i = i // (zh_n * far_n)
    return ((core_i ^ core) * far_n + (far_i ^ far)) * zh_n + (zh_i ^ zh)


def forward_kernel(
    docs, sizes, run, count, meta, q, cosine, sine, qpos, qstart, kown, klocal, *refs
):
    low = meta[3]
    high = low + 2 * sizes[1]
    first = meta[4]
    starts = [meta[5 + d] for d in range(docs)]
    factor = SCALE * LOG2E
    tile = 2 * run
    out, q_rot, lse, kv, sems, vt, vown, top, total, acc = refs[count:]
    copies = load_pieces(refs[:count], kv, sems, 0)
    for copy in copies:
        copy.wait()
    vown[...] = kv[:tile, HEAD_DIM:].T

    def flip(j, _):
        vt[j] = kv[pl.ds(run_row(meta, sizes, j, run), run), HEAD_DIM:].T
        return 0

    lax.fori_loop(first, high, flip, 0)

    heads = range(SHARE)
    keys = kv[:tile, :HEAD_DIM]
    own = visible(kown[...], qpos[...], qstart[...])
    for h in heads:
        lanes = slice(h * HEAD_DIM, (h + 1) * HEAD_DIM)
        q_head = turned(q[:, lanes], cosine[...], sine[...]).astype(BF)
        q_rot[:, lanes] = q_head
        raw = jnp.where(own, dot(keys, q_head, 1, 1), -FAR)
        peak = jnp.max(raw, axis=0, keepdims=True)
        weights = jnp.exp2(raw * factor - peak * factor)
        top[h : h + 1, :] = peak
        total[h : h + 1, :] = jnp.sum(weights, axis=0, keepdims=True)
        acc[h] = dot(vown[...], weights.astype(BF))

    def fold(j, masked):
        base = j * run
        keys = kv[pl.ds(run_row(meta, sizes, j, run), run), :HEAD_DIM]
        values = vt[j]
        seen = (qstart[...] <= base) & (qpos[...] >= base + run - 1)
        if masked:
            allowed = visible(klocal[...] + base, qpos[...], qstart[...])
        for h in heads:
            lanes = slice(h * HEAD_DIM, (h + 1) * HEAD_DIM)
            raw = dot(keys, q_rot[:, lanes], 1, 1)
            before = top[h : h + 1, :]
            if masked:
                raw = jnp.where(allowed, raw, -FAR)
                peak = jnp.maximum(before, jnp.max(raw, axis=0, keepdims=True))
                level = peak * factor
            else:
                new = jnp.max(raw, axis=0, keepdims=True)
                peak = jnp.maximum(before, jnp.where(seen, new, -FAR))
                level = jnp.where(seen, peak * factor, FAR)
            weights = jnp.exp2(raw * factor - level)
            fade = jnp.exp2((before - peak) * factor)
            top[h : h + 1, :] = peak
            total[h : h + 1, :] = total[h : h + 1, :] * fade + jnp.sum(
                weights, axis=0, keepdims=True
            )
            acc[h] = acc[h] * fade + dot(values, weights.astype(BF))

    def step(j, _):
        mixed = is_mixed(starts, j * run, run)
        other = j != low

        @pl.when(other & mixed)
        def _():
            fold(j, True)

        @pl.when(other & jnp.logical_not(mixed))
        def _():
            fold(j, False)

        return 0

    lax.fori_loop(first, high, step, 0)
    for h in heads:
        lanes = slice(h * HEAD_DIM, (h + 1) * HEAD_DIM)
        out[:, lanes] = (acc[h] / total[h : h + 1, :]).T.astype(BF)
    lse[...] = top[...] * factor + jnp.log2(total[...])


def load_natural(meta, sizes, source, target, sems, base):
    slots = 2 * sizes[0] * sizes[1]
    block = source.shape[0] // slots
    copies = []
    for i in range(slots):
        away = pl.ds(pl.multiple_of(natural_slot(meta, sizes, i) * block, block), block)
        copy = pltpu.make_async_copy(
            source.at[away, :], target.at[pl.ds(i * block, block), :], sems.at[base + i]
        )
        copy.start()
        copies.append(copy)
    return copies


def proj_kernel(sizes, meta, attn, w_out, proj, held, sems):
    for copy in load_natural(meta, sizes, w_out, held, sems, 0):
        copy.wait()
    for at in range(0, held.shape[0], 256):
        proj[:, at : at + 256] = dot(attn[...], held[at : at + 256, :], 1, 1).astype(BF)


def backward_kernel(
    docs, sizes, run, count, meta, q, o, g_proj, w_out, lse, cosine, sine, qpos, qstart, kown, klocal, *refs
):
    low = meta[3]
    high = low + 2 * sizes[1]
    first = meta[4]
    starts = [meta[5 + d] for d in range(docs)]
    factor = SCALE * LOG2E
    tile = 2 * run
    grad_q, grad_kv, kv, held, sems, dqt, delta, g = refs[count:]
    copies = load_pieces(refs[:count], kv, sems, 0)
    for copy in load_natural(meta, sizes, w_out, held, sems, count):
        copy.wait()
    total = dot(g_proj[...], held[...])
    for copy in copies:
        copy.wait()
    g[...] = total.astype(BF)
    dqt[...] = jnp.zeros_like(dqt)
    grad_kv[...] = jnp.zeros_like(grad_kv)

    def prepare(h, _):
        lanes = pl.ds(pl.multiple_of(h * HEAD_DIM, HEAD_DIM), HEAD_DIM)
        both = o[:, lanes].astype(F32) * g[:, lanes].astype(F32)
        delta[pl.ds(h, 1), :] = jnp.sum(both.T, axis=0, keepdims=True)
        return 0

    lax.fori_loop(0, SHARE, prepare, 0)

    def key_step(rows, count, kpos, base):
        k_tile = kv[rows, :HEAD_DIM]
        v_tile = kv[rows, HEAD_DIM:]
        kt = k_tile.T

        def head(h, carry):
            grad_k, grad_v = carry
            lanes = slice(h * HEAD_DIM, (h + 1) * HEAD_DIM)
            q_head = q[:, lanes]
            g_head = g[:, lanes]
            raw = dot(k_tile, q_head, 1, 1) * factor
            level = lse[h : h + 1, :]
            if kpos is not None:
                probs = jnp.exp2(raw - level)
                probs = jnp.where(visible(kpos, qpos[...], qstart[...]), probs, 0.0)
            else:
                seen = (qstart[...] <= base) & (qpos[...] >= base + run - 1)
                probs = jnp.exp2(raw - jnp.where(seen, level, FAR))
            slopes = dot(v_tile, g_head, 1, 1)
            grads = (probs * (slopes - delta[h : h + 1, :])).astype(BF)
            grad_v = grad_v + dot(probs.astype(BF), g_head)
            grad_k = grad_k + dot(grads, q_head)
            dqt[h] = dqt[h] + dot(kt, grads)
            return grad_k, grad_v

        zero = jnp.zeros((count, HEAD_DIM), F32)
        grad_k, grad_v = zero, zero
        for h in range(SHARE):
            grad_k, grad_v = head(h, (grad_k, grad_v))
        grad_kv[rows, :HEAD_DIM] = (grad_k * SCALE).astype(BF)
        grad_kv[rows, HEAD_DIM:] = grad_v.astype(BF)

    key_step(pl.ds(0, tile), tile, kown[...], 0)

    def step(j, _):
        base = j * run
        mixed = is_mixed(starts, base, run)
        other = j != low
        rows = pl.ds(run_row(meta, sizes, j, run), run)

        @pl.when(other & mixed)
        def _():
            key_step(rows, run, klocal[...] + base, base)

        @pl.when(other & jnp.logical_not(mixed))
        def _():
            key_step(rows, run, None, base)

        return 0

    lax.fori_loop(first, high, step, 0)

    def finish(h, _):
        lanes = pl.ds(pl.multiple_of(h * HEAD_DIM, HEAD_DIM), HEAD_DIM)
        rotated = (dqt[h] * SCALE).T.astype(BF).astype(F32)
        grad_q[:, lanes] = turned(rotated, cosine[...], -sine[...]).astype(BF)
        return 0

    lax.fori_loop(0, SHARE, finish, 0)


SMEM = pl.BlockSpec(memory_space=pltpu.SMEM)
VMEM = pl.BlockSpec(memory_space=pltpu.VMEM)
ANY = pl.BlockSpec(memory_space=pl.ANY)


def attention_forward(meta, docs, sizes, q, tables, kv):
    tile = q.shape[0]
    run = tile // 2
    span = sum(a.shape[0] for a in kv)
    pairs = tile * span // 2 * SHARE
    return pl.pallas_call(
        functools.partial(forward_kernel, docs, sizes, run, len(kv)),
        out_shape=(
            jax.ShapeDtypeStruct(q.shape, BF),
            jax.ShapeDtypeStruct(q.shape, BF),
            jax.ShapeDtypeStruct((SHARE, tile), F32),
        ),
        in_specs=[SMEM] + [VMEM] * (1 + len(tables)) + [ANY] * len(kv),
        out_specs=(VMEM, VMEM, VMEM),
        scratch_shapes=[
            pltpu.VMEM((span, 2 * HEAD_DIM), BF),
            pltpu.SemaphoreType.DMA((len(kv),)),
            pltpu.VMEM((span // run, HEAD_DIM, run), BF),
            pltpu.VMEM((HEAD_DIM, tile), BF),
            pltpu.VMEM((SHARE, tile), F32),
            pltpu.VMEM((SHARE, tile), F32),
            pltpu.VMEM((SHARE, HEAD_DIM, tile), F32),
        ],
        compiler_params=pltpu.CompilerParams(vmem_limit_bytes=56 << 20),
        cost_estimate=pl.CostEstimate(
            flops=pairs * HEAD_DIM * 4, bytes_accessed=4 << 20, transcendentals=pairs
        ),
        name="attention_forward",
    )(meta, q, *tables, *kv)


def attention_backward(meta, docs, sizes, q, o, g_proj, w_out, lse, tables, kv):
    tile = q.shape[0]
    run = tile // 2
    span = sum(a.shape[0] for a in kv)
    pairs = tile * span // 2 * SHARE
    return pl.pallas_call(
        functools.partial(backward_kernel, docs, sizes, run, len(kv)),
        out_shape=(
            jax.ShapeDtypeStruct(q.shape, BF),
            jax.ShapeDtypeStruct((span, 2 * HEAD_DIM), BF),
        ),
        in_specs=[SMEM, VMEM, VMEM, VMEM, ANY] + [VMEM] * (1 + len(tables)) + [ANY] * len(kv),
        out_specs=(VMEM, VMEM),
        scratch_shapes=[
            pltpu.VMEM((span, 2 * HEAD_DIM), BF),
            pltpu.VMEM(w_out.shape, BF),
            pltpu.SemaphoreType.DMA((len(kv) + 2 * sizes[0] * sizes[1],)),
            pltpu.VMEM((SHARE, HEAD_DIM, tile), F32),
            pltpu.VMEM((SHARE, tile), F32),
            pltpu.VMEM(q.shape, BF),
        ],
        compiler_params=pltpu.CompilerParams(vmem_limit_bytes=56 << 20),
        cost_estimate=pl.CostEstimate(
            flops=pairs * HEAD_DIM * 10, bytes_accessed=6 << 20, transcendentals=pairs
        ),
        name="attention_backward",
    )(meta, q, o, g_proj, w_out, lse, *tables, *kv)


def call(kernel, name, shapes, operands, specs=None, scratch=(), flops=1 << 20):
    nbytes = sum(a.size * a.dtype.itemsize for a in operands)
    return pl.pallas_call(
        kernel,
        out_shape=tuple(jax.ShapeDtypeStruct(s, d) for s, d in shapes),
        in_specs=specs or [VMEM] * len(operands),
        out_specs=(VMEM,) * len(shapes),
        scratch_shapes=list(scratch),
        compiler_params=pltpu.CompilerParams(vmem_limit_bytes=56 << 20),
        cost_estimate=pl.CostEstimate(flops=flops, bytes_accessed=nbytes, transcendentals=0),
        name=name,
    )(*operands)


def load_pieces(pieces, target, sems, base):
    copies = []
    place = 0
    for i, piece in enumerate(pieces):
        rows = piece.shape[0]
        copy = pltpu.make_async_copy(piece, target.at[pl.ds(place, rows), :], sems.at[base + i])
        copy.start()
        copies.append(copy)
        place += rows
    return copies


def pack_kernel(team, count, *refs):
    out = refs[count]
    place = 0
    for shard in refs[:count]:
        part = shard.shape[1] // team
        for t in range(team):
            out[t, :, place : place + part] = shard[:, t * part : (t + 1) * part]
        place += part


def pack(team, shards):
    width = sum(s.shape[1] for s in shards) // team
    kernel = functools.partial(pack_kernel, team, len(shards))
    return call(kernel, "pack", [((team, shards[0].shape[0], width), BF)], shards)[0]


def slots_kernel(chunk, scaled, copies, order, array, keep, own, sent):
    width = array.shape[1]
    for j in range(width // chunk):
        if chunk < width:
            block = array[:, pl.ds(pl.multiple_of(order[j] * chunk, chunk), chunk)]
        else:
            block = array[...]
        lanes = pl.ds(j * chunk, chunk)
        own[:, lanes] = block
        if scaled:
            block = (block.astype(F32) * keep[...]).astype(BF)
        for t in range(copies):
            sent[t, :, lanes] = block


def slots_and_copies(array, keep, scaled, copies):
    chunk, order = slot_order(array.shape[1], True)
    if order is None:
        array, order = to_slots(array), jnp.zeros((1,), jnp.int32)
    kernel = functools.partial(slots_kernel, chunk, scaled, copies)
    shapes = [(array.shape, BF), ((copies,) + array.shape, BF)]
    return call(kernel, "to_slots", shapes, [order, array, keep], [SMEM, VMEM, VMEM])


def natural_kernel(chunk, order, array, out):
    for j in range(array.shape[1] // chunk):
        out[:, j * chunk : (j + 1) * chunk] = array[
            :, pl.ds(pl.multiple_of(order[j] * chunk, chunk), chunk)
        ]


def to_natural(array):
    chunk, order = slot_order(array.shape[1], False)
    if order is None:
        return from_slots(array)
    kernel = functools.partial(natural_kernel, chunk)
    return call(kernel, "from_slots", [(array.shape, array.dtype)], [order, array], [SMEM, VMEM])[0]


def slot_order(width, forward):
    far_n, x_n, core_n, zh_n, _ = [lax.axis_size(a) for a in AXES]
    far, _, core, zh, _ = [lax.axis_index(a) for a in AXES]
    count = far_n * x_n * core_n * zh_n
    chunk = width // count
    if chunk % HEAD_DIM:
        return width, None
    j = lax.iota(jnp.int32, count)
    if forward:
        c, f, z, x = j // (far_n * zh_n * x_n), j // (zh_n * x_n) % far_n, j // x_n % zh_n, j % x_n
        return chunk, (((f ^ far) * x_n + x) * core_n + (c ^ core)) * zh_n + (z ^ zh)
    f, x, c, z = j // (x_n * core_n * zh_n), j // (core_n * zh_n) % x_n, j // zh_n % core_n, j % zh_n
    return chunk, (((c ^ core) * far_n + (f ^ far)) * zh_n + (z ^ zh)) * x_n + x


def project_kernel(count, ids, x, cosine, sine, *refs):
    pieces = refs[:count]
    normed, scale, q, kv, small, w, sems = refs[count:]
    copies = load_pieces(pieces, w, sems, 0)
    rows = x.shape[0]
    features = x.shape[1]
    step = 128

    def squares(i, _):
        at = pl.ds(pl.multiple_of(i * step, step), step)
        block = x[at, :].astype(F32)
        scale[at, :] = lax.rsqrt(jnp.sum(block * block, axis=1, keepdims=True) / features + EPS)
        return 0

    lax.fori_loop(0, rows // step, squares, 0)
    for copy in copies:
        copy.wait()
    width = w.shape[1] - HEAD_DIM
    turned_small = w[:, width:].astype(F32).T
    small[...] = turned_small[: small.shape[0], :]
    gain = small[ids : ids + 1, :]

    def norm(i, _):
        at = pl.ds(pl.multiple_of(i * step, step), step)
        normed[at, :] = (x[at, :].astype(F32) * scale[at, :] * gain).astype(BF)
        return 0

    lax.fori_loop(0, rows // step, norm, 0)
    for at in range(0, width - 2 * HEAD_DIM, 256):
        q[:, at : at + 256] = dot(normed[...], w[:, at : at + 256])
    both = dot(normed[...], w[:, width - 2 * HEAD_DIM : width])
    kv[:, :HEAD_DIM] = turned(both[:, :HEAD_DIM], cosine[...], sine[...]).astype(BF)
    kv[:, HEAD_DIM:] = both[:, HEAD_DIM:].astype(BF)


def project(tokens_all, cosine, sine, pieces, ids):
    rows, features = tokens_all.shape
    width = pieces[0].shape[1]
    held = -(-(ids + 2) // 8) * 8
    return call(
        functools.partial(project_kernel, len(pieces), ids),
        "project",
        [
            ((rows, features), BF),
            ((rows, 1), F32),
            ((rows, width - 3 * HEAD_DIM), F32),
            ((rows, 2 * HEAD_DIM), BF),
            ((held, features), F32),
        ],
        [tokens_all, cosine, sine, *pieces],
        [VMEM] * 3 + [ANY] * len(pieces),
        [pltpu.VMEM((features, width), BF), pltpu.SemaphoreType.DMA((len(pieces),))],
        2 * rows * features * width,
    )


def middle_kernel(parts, tokens, keep, gain, middle, sent):
    proj = total_of([parts[t] for t in range(parts.shape[0])])
    mid = tokens[...].astype(F32) + keep[...] * proj
    scale = lax.rsqrt(jnp.mean(mid * mid, axis=1, keepdims=True) + EPS)
    middle[...] = mid
    normed = (mid * scale * gain[...]).astype(BF)
    for t in range(sent.shape[0]):
        sent[t] = normed


def middle_grad_kernel(parts, middle, cotangent, keep, gain, grad_middle, sent, terms):
    grad = total_of([parts[t] for t in range(parts.shape[0])])
    mid = middle[...]
    scale = lax.rsqrt(jnp.mean(mid * mid, axis=1, keepdims=True) + EPS)
    gained = grad * gain[...]
    terms[...] = (grad * mid * scale).astype(BF)
    result = (
        cotangent[...].astype(F32)
        + scale * gained
        - mid * scale**3 * jnp.mean(gained * mid, axis=1, keepdims=True)
    )
    grad_middle[...] = result
    proj = (keep[...] * result).astype(BF)
    for t in range(sent.shape[0]):
        sent[t] = proj


def token_grad_kernel(parts, tokens, grad_middle, gain, out):
    grad = total_of([parts[t] for t in range(parts.shape[0])])
    x = tokens[...].astype(F32)
    scale = lax.rsqrt(jnp.mean(x * x, axis=1, keepdims=True) + EPS)
    gained = grad * gain[...]
    out[...] = (
        grad_middle[...]
        + scale * gained
        - x * scale**3 * jnp.mean(gained * x, axis=1, keepdims=True)
    )


def output_kernel(parts, middle, keep, out):
    ffn = total_of([parts[t] for t in range(parts.shape[0])])
    out[...] = (middle[...] + keep[...] * ffn).astype(BF)


def mlp_kernel(sizes, counts, meta, x, g, *refs):
    total = sum(counts)
    gate_pieces, up_pieces = refs[: counts[0]], refs[counts[0] : total]
    down = refs[total]
    hidden, grad_gate, grad_up, grad_x, ffn, w_g, w_u, w_d, sems = refs[total + 1 :]
    copies = load_pieces(gate_pieces, w_g, sems, 0)
    copies += load_pieces(up_pieces, w_u, sems, counts[0])
    late = load_natural(meta, sizes, down, w_d, sems, total)
    for copy in copies:
        copy.wait()
    features, width = w_g.shape

    def columns(lanes, wait=()):
        gate = dot(x[...], w_g[:, lanes])
        up = dot(x[...], w_u[:, lanes])
        for copy in wait:
            copy.wait()
        grad = dot(g[...], w_d[:, lanes])
        sig = 1.0 / (1.0 + jnp.exp(-gate))
        silu = gate * sig
        hidden[:, lanes] = (silu * up).astype(BF)
        grad_gate[:, lanes] = (grad * up * sig * (1.0 + gate * (1.0 - sig))).astype(BF)
        grad_up[:, lanes] = (grad * silu).astype(BF)

    step = 256
    tail = width % step
    columns(pl.ds(width - tail, tail) if tail else pl.ds(width - step, step), late)

    def chunk(i, _):
        columns(pl.ds(pl.multiple_of(i * step, step), step))
        return 0

    lax.fori_loop(0, (width - 1) // step, chunk, 0)

    def back_rows(i, _):
        at = pl.ds(pl.multiple_of(i * step, step), step)
        total = dot(grad_gate[...], w_g[at, :], 1, 1) + dot(grad_up[...], w_u[at, :], 1, 1)
        grad_x[:, at] = total.astype(BF)
        ffn[:, at] = dot(hidden[...], w_d[at, :], 1, 1).astype(BF)
        return 0

    lax.fori_loop(0, features // step, back_rows, 0)


def mlp(meta, sizes, x, g, w_gate, w_up, w_down):
    rows, features = x.shape
    width = w_down.shape[1]
    counts = (len(w_gate), len(w_up))
    pieces = [*w_gate, *w_up, w_down]
    return call(
        functools.partial(mlp_kernel, sizes, counts),
        "mlp",
        [((rows, width), BF)] * 3 + [((rows, features), BF)] * 2,
        [meta, x, g, *pieces],
        [SMEM] + [VMEM] * 2 + [ANY] * len(pieces),
        [
            *([pltpu.VMEM((features, width), BF)] * 3),
            pltpu.SemaphoreType.DMA((sum(counts) + 2 * sizes[0] * sizes[1],)),
        ],
        12 * rows * features * width,
    )


def outer_kernel(meta, left, right, *refs):
    product = dot(left[...].T, right[...])
    if len(refs) == 2:
        product = product + refs[0][...].astype(F32)
    refs[-1][...] = product.astype(BF)


def outer(meta, sizes, left, right, half=None, natural=False, added=None):
    features = left.shape[1]
    if features // (2 * sizes[0] * sizes[1]) % HEAD_DIM:
        sizes_held = features if half is None else features // 2
        part = left if half is None else left[:, half * sizes_held : (half + 1) * sizes_held]
        product = dot(part, right, 0, 0)
        if natural:
            shape = (2, sizes[0], sizes[1], -1, right.shape[1])
            product = product.reshape(shape)
            for axis, name in enumerate(("core", "far", "zh")):
                product = by_distance(product, axis, lax.axis_index(name))
            product = product.reshape(features, -1)
        return (product if added is None else product + added.astype(F32)).astype(BF)
    slots = 2 * sizes[0] * sizes[1]
    rows, block, width = left.shape[0], features // slots, right.shape[1]
    count, start = (slots, 0) if half is None else (slots // 2, half * slots // 2)
    held = pl.BlockSpec((block, width), lambda i, m: (i, 0))
    return pl.pallas_call(
        outer_kernel,
        out_shape=jax.ShapeDtypeStruct((count * block, width), BF),
        grid_spec=pltpu.PrefetchScalarGridSpec(
            num_scalar_prefetch=1,
            grid=(count,),
            in_specs=[
                pl.BlockSpec((rows, block), lambda i, m: (0, start + i)),
                pl.BlockSpec((rows, width), lambda i, m: (0, 0)),
            ]
            + ([] if added is None else [held]),
            out_specs=pl.BlockSpec((block, width), lambda i, m: (natural_slot(m, sizes, i), 0))
            if natural
            else held,
        ),
        compiler_params=pltpu.CompilerParams(vmem_limit_bytes=48 << 20),
        cost_estimate=pl.CostEstimate(
            flops=2 * rows * count * block * width,
            bytes_accessed=2 * count * block * (rows + width),
            transcendentals=0,
        ),
        name="outer",
    )(meta, left, right, *([] if added is None else [added]))


def qkv_grad_kernel(count, grad_q, grad_kv, x, scale, *refs):
    pieces = refs[:count]
    out, terms, w, sems = refs[count:]
    for copy in load_pieces(pieces, w, sems, 0):
        copy.wait()
    q_width = grad_q.shape[1]
    step = 256

    def rows_of(i, _):
        at = pl.ds(pl.multiple_of(i * step, step), step)
        grad = dot(grad_q[...], w[at, :q_width], 1, 1) + dot(
            grad_kv[...], w[at, q_width : q_width + 2 * HEAD_DIM], 1, 1
        )
        out[:, at] = grad.astype(BF)
        terms[:, at] = (grad * x[:, at].astype(F32) * scale[...]).astype(BF)
        return 0

    lax.fori_loop(0, w.shape[0] // step, rows_of, 0)


def qkv_grad(grad_q, grad_kv, tokens_all, scale_all, pieces):
    rows, features = tokens_all.shape
    width = pieces[0].shape[1]
    return call(
        functools.partial(qkv_grad_kernel, len(pieces)),
        "qkv_grad",
        [((rows, features), BF)] * 2,
        [grad_q, grad_kv, tokens_all, scale_all, *pieces],
        [VMEM] * 4 + [ANY] * len(pieces),
        [pltpu.VMEM((features, width), BF), pltpu.SemaphoreType.DMA((len(pieces),))],
        2 * rows * features * width,
    )


def after(value, *done):
    return lax.optimization_barrier((value, done))[0]


def together(*values):
    return lax.optimization_barrier(values)


def swap(block, axes, distance):
    size = lax.axis_size(axes)
    return lax.ppermute(block, axes, [(i, i ^ distance) for i in range(size)])


def by_distance(array, axis, index):
    size = array.shape[axis]
    bit = 1
    while bit < size:
        shape = array.shape[:axis] + (size // (2 * bit), 2, bit) + array.shape[axis + 1 :]
        pairs = array.reshape(shape)
        flipped = jnp.flip(pairs, axis + 1)
        array = jnp.where((index & bit) != 0, flipped, pairs).reshape(array.shape)
        bit *= 2
    return array


def halves(array):
    half = array.shape[1] // 2
    return array[:, :half], array[:, half:]


def to_team(pieces):
    return lax.all_to_all(pieces, TEAM, split_axis=0, concat_axis=0, tiled=True)


def sum_team(partial):
    team = lax.axis_size(TEAM)
    return to_team(partial.reshape(team, partial.shape[0] // team, partial.shape[1]))


def total_of(parts):
    total = parts[0].astype(F32)
    for i in range(1, len(parts)):
        total = total + parts[i].astype(F32)
    return total


def plane_direct(block):
    size = lax.axis_size("far") * lax.axis_size("zh")
    return [block] + [swap(block, ("far", "zh"), d) for d in range(1, size)]


def plane_first(block):
    near = [swap(block, "zh", d) for d in range(1, lax.axis_size("zh"))]
    far = [[swap(block, "far", d)] for d in range(1, lax.axis_size("far"))]
    return block, near, far


def plane_second(first, *done):
    block, near, far = first
    if done:
        near = after(near, *done)
    far = [f + [swap(b, "far", d + 1) for b in near] for d, f in enumerate(far)]
    return sum(far, [block] + near)


def both_cores(plane):
    if len(plane) > 4:
        plane = [jnp.concatenate(plane, axis=0)]
    return list(plane) + [swap(b, "core", 1) for b in plane]


def sum_axis(part, axis, *done):
    size = lax.axis_size(axis)
    rows = part.shape[0] // size
    got = [swap(part[d * rows : (d + 1) * rows], axis, d) for d in range(1, size)]
    if done:
        got = after(got, *done)
    return total_of([part[:rows]] + got).astype(BF)


SLOT = ("core", "far", "zh")


def spread(block):
    return lax.all_gather(block, SLOT, axis=0, tiled=True)


def gather_back(partial):
    return lax.psum_scatter(partial, SLOT, scatter_dimension=0, tiled=True)


def to_owner(part):
    team = lax.axis_size(TEAM)
    return to_team(part.reshape(team, part.shape[0] // team, part.shape[1]))


def wide(pieces):
    return pieces.transpose(1, 0, 2).reshape(pieces.shape[1], -1).astype(F32)


def turn(values, cosine, sine):
    half = HEAD_DIM // 2
    other = jnp.concatenate([values[:, half:], values[:, :half]], axis=1)
    return values * cosine + other * sine


def to_slots(array):
    sizes = [lax.axis_size(a) for a in AXES]
    rows, width = array.shape
    grid = array.reshape(rows, *sizes[:4], width // (sizes[0] * sizes[1] * sizes[2] * sizes[3]))
    for axis in (0, 2, 3):
        grid = by_distance(grid, axis + 1, lax.axis_index(AXES[axis]))
    return grid.transpose(0, 3, 1, 4, 2, 5).reshape(rows, width)


def from_slots(array):
    far, x, core, zh, zl = [lax.axis_size(a) for a in AXES]
    rows, width = array.shape
    grid = array.reshape(rows, core, far, zh, x, width // (core * far * zh * x))
    grid = grid.transpose(0, 2, 4, 1, 3, 5)
    for axis in (0, 2, 3):
        grid = by_distance(grid, axis + 1, lax.axis_index(AXES[axis]))
    return grid.reshape(rows, width)


def per_device(
    tokens,
    segment_ids,
    layer_skip,
    attn_gain,
    w_query,
    w_key,
    w_value,
    w_output,
    mlp_gain,
    w_gate,
    w_up,
    w_down,
    cotangent,
):
    far_n, x_n, core_n, zh_n, zl_n = [lax.axis_size(a) for a in AXES]
    far, x, core, zh, zl = [lax.axis_index(a) for a in AXES]
    team = x_n * zl_n
    rows = tokens.shape[0]
    tile = team * rows
    run = zl_n * rows
    docs = layer_skip.shape[0]
    part = HEADS * HEAD_DIM // team
    ff = w_gate.shape[1] // team
    width = attn_gain.shape[0]
    features = tokens.shape[1]

    ids = rows // width
    doc_index = lax.iota(jnp.int32, docs)
    skipped = jnp.sum(
        jnp.where(segment_ids[:, None] == doc_index[None, :], layer_skip[None, :], 0), axis=1
    )
    keep = (1 - skipped).astype(F32)[:, None]
    small = jnp.concatenate(
        [segment_ids.astype(BF).reshape(width, ids), attn_gain[:, None], mlp_gain[:, None]], axis=1
    )
    small = jnp.pad(small, ((0, 0), (0, HEAD_DIM - ids - 2)))
    small = jnp.concatenate([small] * team, axis=1)
    first_rows = to_team(pack(team, [w_query, w_key, w_value, small, w_gate]))
    first_rows = first_rows.reshape(-1, first_rows.shape[2])
    qkv_width = part + 3 * HEAD_DIM
    qkv_plane = plane_first(first_rows[:, :qkv_width])
    gate_rows = first_rows[:, qkv_width:]

    last_rows = pack(team, [w_output.T, w_up, w_down.T])
    tokens_own, tokens_sent = slots_and_copies(tokens, keep, False, team)
    cot_own, cot_sent = slots_and_copies(cotangent, keep, True, team)
    tokens_all = to_team(after(tokens_sent, first_rows)).reshape(tile, features)

    local = lax.iota(jnp.int32, tile)
    place = (local // run) * (core_n * zh_n * run) + local % run
    position = ((far * x_n * core_n + core) * zh_n + zh) * run + place
    rates = jnp.power(THETA, -lax.iota(jnp.int32, HEAD_DIM // 2).astype(F32) / (HEAD_DIM // 2))
    angles = position.astype(F32)[:, None] * rates[None, :]
    cosine = jnp.cos(angles)
    sine = jnp.sin(angles)
    cosine = jnp.concatenate([cosine, cosine], axis=1)
    sine = jnp.concatenate([-sine, sine], axis=1)

    qkv_near, last_rows, cot_sent = together(qkv_plane[1], last_rows, cot_sent)
    qkv_plane = (qkv_plane[0], qkv_near, qkv_plane[2])
    gate_plane = plane_first(gate_rows)
    w_qkv = both_cores(plane_second(qkv_plane))
    last_rows = to_team(after(last_rows, tokens_all)).reshape(-1, last_rows.shape[2])
    tokens_all, gate_plane, w_qkv, cosine, sine, last_rows = together(
        tokens_all, gate_plane, w_qkv, cosine, sine, last_rows
    )
    gate_plane = plane_second(gate_plane)
    w_out = spread(last_rows[:, :part])
    grad_ffn = to_team(after(cot_sent, last_rows))

    normed_one, scale_all, q, kv, small_all = project(tokens_all, cosine, sine, w_qkv, ids)
    kv_plane = plane_first(kv)
    gain_one = small_all[ids : ids + 1]
    gain_two = small_all[ids + 1 : ids + 2]
    doc_starts = jnp.sum(
        (small_all[None, :ids] < doc_index.astype(F32)[:, None, None]).astype(F32), axis=(1, 2)
    ).astype(jnp.int32)
    query_seg = jnp.sum((position[:, None] >= doc_starts[None, 1:]).astype(jnp.int32), axis=1)
    query_start = jnp.sum(
        jnp.where(query_seg[:, None] == doc_index[None, :], doc_starts[None, :], 0), axis=1
    )
    low = (far * x_n * core_n + core) * zh_n + zh
    first_start = jnp.max(jnp.where(doc_starts <= low * run, doc_starts, 0))
    meta = jnp.concatenate([jnp.stack([far, core, zh, low, first_start // run]), doc_starts])
    sizes = (far_n, zh_n)
    tables = (
        cosine,
        sine,
        position[None, :],
        query_start[None, :],
        position[:, None],
        lax.iota(jnp.int32, run)[:, None],
    )
    kv_plane, meta, tables = together(kv_plane, meta, tables)
    kv_plane = plane_second(kv_plane)
    kv_plane, gate_plane, last_rows, grad_ffn = together(
        kv_plane, gate_plane, last_rows, grad_ffn
    )
    w_d = spread(last_rows[:, part + ff :])
    kv = both_cores(kv_plane)
    up_plane = plane_first(last_rows[:, part : part + ff])
    attn, query, log_total = attention_forward(meta, docs, sizes, q, tables, kv)
    attn, up_plane = together(attn, up_plane)
    grad_ffn = grad_ffn.reshape(tile, features)

    proj = call(
        functools.partial(proj_kernel, sizes),
        "proj",
        [((tile, features), BF)],
        [meta, attn, w_out],
        [SMEM, VMEM, ANY],
        [pltpu.VMEM(w_out.shape, BF), pltpu.SemaphoreType.DMA((2 * far_n * zh_n,))],
    )[0]
    gate_plane = after(gate_plane, attn)
    proj = sum_team(proj)
    up_plane = plane_second(up_plane)
    w_g = both_cores(gate_plane)
    proj, up_plane, w_g = together(proj, up_plane, w_g)
    middle, normed_sent = call(
        middle_kernel,
        "middle",
        [((rows, features), F32), ((team, rows, features), BF)],
        [proj, tokens_own, keep, gain_two],
    )
    normed_two = to_team(normed_sent)
    w_u = both_cores(up_plane)
    normed_two, w_u = together(normed_two, w_u)
    normed_two = normed_two.reshape(tile, features)

    hidden, grad_gate_act, grad_up_act, grad_two, ffn = mlp(
        meta, sizes, normed_two, grad_ffn, w_g, w_u, w_d
    )
    grad_two_parts = sum_team(grad_two)
    grad_down = outer(meta, sizes, grad_ffn, hidden, natural=True)
    other_up = swap(outer(meta, sizes, normed_two, grad_up_act, half=1), "core", 1)
    grad_gate = outer(meta, sizes, normed_two, grad_gate_act, natural=True)
    up_core = outer(meta, sizes, normed_two, grad_up_act, half=0, added=other_up)
    grad_two_parts, up_core, grad_gate = together(grad_two_parts, up_core, grad_gate)
    grad_down = gather_back(grad_down)
    grad_gate = gather_back(grad_gate)
    grad_middle, grad_proj_sent, terms_two = call(
        middle_grad_kernel,
        "middle_grad",
        [((rows, features), F32), ((team, rows, features), BF), ((rows, features), BF)],
        [grad_two_parts, middle, cot_own, keep, gain_two],
    )
    grad_proj = to_team(grad_proj_sent)
    grad_proj = grad_proj.reshape(tile, features)
    ffn = sum_team(after(ffn, grad_proj))
    grad_query, grad_kv = attention_backward(
        meta, docs, sizes, query, attn, grad_proj, w_out, log_total, tables, kv
    )
    up_far = sum_axis(up_core, "far", grad_kv)
    grad_query, grad_kv, ffn, up_far = together(grad_query, grad_kv, ffn, up_far)
    half = grad_kv.shape[0] // 2
    other_kv = swap(grad_kv[half:], "core", 1)
    grad_kv = grad_kv[:half].astype(F32) + other_kv.astype(F32)
    grad_kv_parts = [grad_kv[:tile]] + [
        swap(grad_kv[d * tile : (d + 1) * tile].astype(BF), ("far", "zh"), d)
        for d in range(1, far_n * zh_n)
    ]
    output = to_natural(
        call(output_kernel, "output", [((rows, features), BF)], [ffn, middle, keep])[0]
    )
    other_q = jnp.concatenate(
        [
            outer(meta, sizes, normed_one, grad_query, half=1),
            outer(meta, sizes, grad_proj, attn, half=1),
        ],
        axis=1,
    )
    other_q = swap(other_q, "core", 1)
    own_q = jnp.concatenate(
        [
            outer(meta, sizes, normed_one, grad_query, half=0),
            outer(meta, sizes, grad_proj, attn, half=0),
        ],
        axis=1,
    )
    q_core = (own_q.astype(F32) + other_q.astype(F32)).astype(BF)
    grad_kv_parts, q_core = together(grad_kv_parts, q_core)
    q_far = sum_axis(q_core, "far")
    up_zh = sum_axis(up_far, "zh")
    grad_kv_sum = total_of(grad_kv_parts)
    grad_key = turn(grad_kv_sum[:, :HEAD_DIM].astype(BF).astype(F32), cosine, -sine).astype(BF)
    grad_kv_tok = jnp.concatenate([grad_key, grad_kv_sum[:, HEAD_DIM:].astype(BF)], axis=1)
    grad_one, terms_one = qkv_grad(grad_query, grad_kv_tok, tokens_all, scale_all, w_qkv)
    grad_one = sum_team(grad_one)

    lanes = lax.broadcasted_iota(jnp.int32, (tile + rows, HEAD_DIM), 1)
    which = lax.broadcasted_iota(jnp.int32, (tile + rows, HEAD_DIM), 0) // tile
    pick = (lanes == which).astype(BF)
    terms = jnp.concatenate([terms_one, terms_two], axis=0)
    other_small, own_small = [
        jnp.concatenate(
            [
                outer(meta, sizes, normed_one, grad_kv_tok, half=i),
                outer(meta, sizes, terms, pick, half=i),
            ],
            axis=1,
        )
        for i in (1, 0)
    ]
    other_small = swap(other_small, "core", 1)
    small_core = (own_small.astype(F32) + other_small.astype(F32)).astype(BF)
    grad_one, small_core, q_far, up_zh = together(grad_one, small_core, q_far, up_zh)
    q_zh = sum_axis(q_far, "zh")
    rows_held = small_core.shape[0] // (far_n * zh_n)
    small_sum = total_of(
        [small_core[:rows_held]]
        + [
            swap(small_core[d * rows_held : (d + 1) * rows_held], ("far", "zh"), d)
            for d in range(1, far_n * zh_n)
        ]
    ).astype(BF)
    grad_up, grad_down, grad_gate = [to_owner(a) for a in (up_zh, grad_down, grad_gate)]
    grad_w = to_owner(jnp.concatenate([q_zh, small_sum], axis=1))
    grad_out = grad_w[:, :, part : 2 * part]
    grad_w = jnp.concatenate([grad_w[:, :, :part], grad_w[:, :, 2 * part :]], axis=2)
    gains = total_of(grad_w[:, :, part + 2 * HEAD_DIM :])
    grad_tokens = to_natural(
        call(
            token_grad_kernel,
            "token_grad",
            [((rows, features), F32)],
            [grad_one, tokens_own, grad_middle, gain_one],
        )[0]
    )
    return (
        output,
        grad_tokens,
        gains[:, 0],
        wide(grad_w[:, :, :part]),
        wide(grad_w[:, :, part : part + HEAD_DIM]),
        wide(grad_w[:, :, part + HEAD_DIM : part + 2 * HEAD_DIM]),
        wide(grad_out).T,
        gains[:, 1],
        wide(grad_gate),
        wide(grad_up),
        wide(grad_down).T,
    )


def solution(mesh):
    blk, uly = mesh.shape["blk"], mesh.shape["uly"]
    grid = Mesh(mesh.devices.reshape(blk // 4, 2, 2, uly // 2, 2), AXES)
    rows = P(AXES, None)
    cols = P(None, AXES)
    flat = P(AXES)
    return jax.shard_map(
        per_device,
        mesh=grid,
        in_specs=(
            rows, flat, P(), flat, rows, rows, rows, cols, flat, rows, rows, cols, rows,
        ),
        out_specs=(rows, rows, flat, rows, rows, rows, cols, flat, rows, rows, cols),
        check_vma=False,
    )
```

time: 4950 us -> 677 us (0.14)
  waiting for transfers between devices: 4210 us -> 273 us
  matrix products: 205 us -> 0 us
  Pallas kernels: 0 us -> 157 us
  blocking collectives: 182 us -> 50.8 us
  starting transfers between devices: 185 us -> 92.6 us
    reduce_scatter x7 -> x2, waiting for transfers between devices: 3800 us -> 0.01 us  [gather_back(): return lax.psum_scatter(partial, SLOT, scatter_dimension=0, tiled=True)]
    all_gather x6 -> x2, waiting for transfers between devices: 350 us -> 0.01 us  [spread(): return lax.all_gather(block, SLOT, axis=0, tiled=True)]
    dot_general x25 -> x0, matrix products: 198 us -> none  [the longest x7 79.8 us: outer_sum(): lax.dot_general(left, right, (((0,), (0,)), ((), ())), preferred_element_...]
    ppermute x44 -> x42, waiting for transfers between devices: 4.22 us -> 187 us  [swap(): return lax.ppermute(block, axes, [(i, i ^ distance) for i in range(size)])]
    pallas_call x0 -> x28, Pallas kernels: none -> 157 us  [the longest x14 86.9 us: call(): pl.pallas_call(kernel, out_shape=tuple((jax.ShapeDtypeStruct(s, d) for s,...]
    ppermute x44 -> x42, starting transfers between devices: 165 us -> 36.4 us  [swap(): return lax.ppermute(block, axes, [(i, i ^ distance) for i in range(size)])]
    unnamed x2 -> x0, blocking collectives: 81.8 us -> none
    all_gather x1 -> x0, blocking collectives: 79.7 us -> none  [per_device(): segments = lax.all_gather(segment_ids, ('blk', 'uly'), axis=0, tiled=True)]
  transfers between devices with their start and end apart: 62 -> 59, of which waited for: 15 -> 25; matrix products, arithmetic and copies ran while one was open for 4% -> 8% of each run, Pallas kernels for 0% -> 17%
where the time goes in v1:
time: 677 us; the launch traced here: 668 us
  waiting for transfers between devices  273 us (40%)
  Pallas kernels  157 us (23%)
  starting transfers between devices  92.6 us (14%)
  blocking collectives  50.8 us (8%)
  local copies, waits for them, and re-layouts  47 us (7%)
  other arithmetic  29.6 us (4%)
  between operations  17.7 us (3%)
    ppermute x42, waiting for transfers between devices, swap(): return lax.ppermute(block, axes, [(i, i ^ distance) for i in range(size)])  187 us
    pallas_call x14, Pallas kernels, call(): pl.pallas_call(kernel, out_shape=tuple((jax.ShapeDtypeStruct(s, d) for s,...  86.9 us
    all_to_all x13, waiting for transfers between devices, to_team(): return lax.all_to_all(pieces, TEAM, split_axis=0, concat_axis=0, tiled=True)  85.1 us
    all_to_all x13, starting transfers between devices, to_team(): return lax.all_to_all(pieces, TEAM, split_axis=0, concat_axis=0, tiled=True)  56 us
    all_to_all x1, blocking collectives, to_team(): return lax.all_to_all(pieces, TEAM, split_axis=0, concat_axis=0, tiled=True)  50.8 us
    pallas_call x12, Pallas kernels, outer(): pl.pallas_call(outer_kernel, out_shape=jax.ShapeDtypeStruct((count * bloc...  40.6 us
    ppermute x42, starting transfers between devices, swap(): return lax.ppermute(block, axes, [(i, i ^ distance) for i in range(size)])  36.4 us
    unnamed x115, local copies, waits for them, and re-layouts  21 us
  transfers between devices with their start and end apart: 59, of which 25 were waited for; matrix products, arithmetic and copies ran while one was open for 8% of the time, Pallas kernels for 17%

profile of v1, /device:TPU:0, one launch (start us, length us, event | category | flops | bytes accessed | tf_op | source)
XLA Modules:
  0.0 667.5 jit_solution(3208668413119484536)
XLA Ops:
  12.7 5.2 all-to-all-start
  22.5 10.4 %all-to-all-done = bf16[4,64,2304]{2,1,0:T(8,128)(2,1)S(1)} async-done(((bf16[4,64,2304]{2,1,0:T(8,128)(2,1)}), bf16[4,64,2304]{2,1,0:T(8,128)(2,1)S(1)}, u32[]{:S(2)}, u32[]{:S(2)}) %all-to-all-start) | async-done | bytes 1179680 | tf_op jit(solution)/shard_map/all_to_all | solution.py:702
  32.9 4.4 all-to-all-start.1
  46.0 23.4 %collective-permute-done.2.refs_1_ = bf16[256,896]{1,0:T(8,128)(2,1)S(1)} collective-permute-done((bf16[256,896]{1,0:T(8,128)(2,1)S(1)}, bf16[256,896]{1,0:T(8,128)(2,1)S(1)}, u32[]{:S(2)}, u32[]{:S(2)}) %collective-permute-start.2) | collective-permute-done | bytes 458784 | tf_op jit(solution)/shard_map/ppermute | solution.py:681
  71.6 5.5 all-to-all-start.2
  81.7 9.0 %collective-permute-done.3.refs_2_ = bf16[256,896]{1,0:T(8,128)(2,1)} collective-permute-done((bf16[256,896]{1,0:T(8,128)(2,1)S(1)}, bf16[256,896]{1,0:T(8,128)(2,1)}, u32[]{:S(2)}, u32[]{:S(2)}) %collective-permute-start.3) | collective-permute-done | bytes 458784 | tf_op jit(solution)/shard_map/ppermute | solution.py:681
  91.2 9.3 %collective-permute-done.4.refs_3_ = bf16[256,896]{1,0:T(8,128)(2,1)} collective-permute-done((bf16[256,896]{1,0:T(8,128)(2,1)}, bf16[256,896]{1,0:T(8,128)(2,1)}, u32[]{:S(2)}, u32[]{:S(2)}) %collective-permute-start.4) | collective-permute-done | bytes 458784 | tf_op jit(solution)/shard_map/ppermute | solution.py:681
  103.2 11.7 %collective-permute-done.refs_1_ = bf16[256,1408]{1,0:T(8,128)(2,1)S(1)} collective-permute-done((bf16[256,1408]{1,0:T(8,128)(2,1)}, bf16[256,1408]{1,0:T(8,128)(2,1)S(1)}, u32[]{:S(2)}, u32[]{:S(2)}) %collective-permute-start) | collective-permute-done | bytes 720928 | tf_op jit(solution)/shard_map/ppermute | solution.py:681
  117.7 3.6 all-to-all-start.3
  126.0 7.5 %project.1 = (bf16[512,2048]{1,0:T(8,128)(2,1)}, f32[512,1]{1,0:T(8,128)}, f32[512,512]{1,0:T(8,128)}, bf16[512,256]{1,0:T(8,128)(2,1)}, f32[8,2048]{1,0:T(8,128)}) custom-call(bf16[512,2048]{1,0:T(8,128)(2,1)} %bitcast.4.x, f32[512,128]{1,0:T(8,128)} %pad_maximum_fusion.3.cosine, f32[512,128]{1,0:T(8,128)} %pad_maximum_fusion.4.sine, ...), custom_call_target="tpu_custom_call" | custom-call | flops 1879048192 | bytes 6291456 | tf_op jit(solution)/shard_map/project/pallas_call | solution.py:331
  140.7 16.7 %collective-permute-done.9.refs_1_ = bf16[512,256]{1,0:T(8,128)(2,1)} collective-permute-done((bf16[512,256]{1,0:T(8,128)(2,1)}, bf16[512,256]{1,0:T(8,128)(2,1)}, u32[]{:S(2)}, u32[]{:S(2)}) %collective-permute-start.9) | collective-permute-done | bytes 262176 | tf_op jit(solution)/shard_map/ppermute | solution.py:681
  159.5 5.3 collective-permute-done.11.refs_3_
  168.9 3.5 collective-permute-start.17
  176.9 12.6 %attention_forward.1 = (bf16[512,512]{1,0:T(8,128)(2,1)}, bf16[512,512]{1,0:T(8,128)(2,1)}, f32[4,512]{1,0:T(4,128)}) custom-call(s32[10]{0:T(128)} %concatenate.43.meta, f32[512,512]{1,0:T(8,128)} %get-tuple-element.146.q, f32[512,128]{1,0:T(8,128)} %pad_maximum_fusion.3.cosine, f32[512,128]{1,0:T(8,128)} %pad_maximum_fusion.4.sine, s32[1,512]{1,0:T(1,128)} %fusion.28.qpos, ...), custom_call_target="tpu_custom_call" | custom-call | flops 2147483648 | bytes 4194304 | tf_op jit(solution)/shard_map/attention_forward/pallas_call | solution.py:274
  189.6 30.4 %collective-permute-done.17.refs_9_ = bf16[256,1408]{1,0:T(8,128)(2,1)S(1)} collective-permute-done((bf16[256,1408]{1,0:T(8,128)(2,1)S(1)}, bf16[256,1408]{1,0:T(8,128)(2,1)S(1)}, u32[]{:S(2)}, u32[]{:S(2)}) %collective-permute-start.17) | collective-permute-done | bytes 720928 | tf_op jit(solution)/shard_map/ppermute | solution.py:681
  221.7 5.2 proj.1
  227.0 3.8 all-to-all-start.4
  234.7 18.4 %collective-permute-done.19.refs_11_ = bf16[256,1408]{1,0:T(8,128)(2,1)S(1)} collective-permute-done((bf16[256,1408]{1,0:T(8,128)(2,1)}, bf16[256,1408]{1,0:T(8,128)(2,1)S(1)}, u32[]{:S(2)}, u32[]{:S(2)}) %collective-permute-start.19) | collective-permute-done | bytes 720928 | tf_op jit(solution)/shard_map/ppermute | solution.py:681
  255.4 14.8 %all-to-all-done.4.parts = bf16[4,128,2048]{2,1,0:T(8,128)(2,1)S(1)} async-done(((bf16[4,128,2048]{2,1,0:T(8,128)(2,1)}), bf16[4,128,2048]{2,1,0:T(8,128)(2,1)S(1)}, u32[]{:S(2)}, u32[]{:S(2)}) %all-to-all-start.4) | async-done | bytes 2097184 | tf_op jit(solution)/shard_map/all_to_all | solution.py:702
  271.6 3.8 middle.1
  275.4 3.7 all-to-all-start.5
  286.4 17.5 %all-to-all-done.5 = bf16[4,128,2048]{2,1,0:T(8,128)(2,1)S(1)} async-done(((bf16[4,128,2048]{2,1,0:T(8,128)(2,1)}), bf16[4,128,2048]{2,1,0:T(8,128)(2,1)S(1)}, u32[]{:S(2)}, u32[]{:S(2)}) %all-to-all-start.5) | async-done | bytes 2097184 | tf_op jit(solution)/shard_map/all_to_all | solution.py:702
  305.2 32.5 %mlp.1 = (bf16[512,1408]{1,0:T(8,128)(2,1)}, bf16[512,1408]{1,0:T(8,128)(2,1)}, bf16[512,1408]{1,0:T(8,128)(2,1)}, bf16[512,2048]{1,0:T(8,128)(2,1)}, bf16[512,2048]{1,0:T(8,128)(2,1)}) custom-call(s32[10]{0:T(128)} %concatenate.43.meta, bf16[512,2048]{1,0:T(8,128)(2,1)} %bitcast.64, bf16[512,2048]{1,0:T(8,128)(2,1)} %bitcast.71, ...), custom_call_target="tpu_custom_call" | custom-call | flops 17716740096 | bytes 21495848 | tf_op jit(solution)/shard_map/mlp/pallas_call | solution.py:331
  339.1 7.4 %outer.23 = bf16[2048,1408]{1,0:T(8,128)(2,1)} custom-call(s32[10]{0:T(128)S(1)} %copy-done.17, bf16[512,2048]{1,0:T(8,128)(2,1)S(1)} %bitcast.72, bf16[512,1408]{1,0:T(8,128)(2,1)S(1)} %copy-done.20), custom_call_target="tpu_custom_call" | custom-call | flops 2952790016 | bytes 7864320 | tf_op jit(solution)/shard_map/outer/pallas_call | solution.py:612
  346.5 5.0 all-to-all-start.6
  351.5 4.2 outer.12
  355.8 7.3 %outer.14 = bf16[2048,1408]{1,0:T(8,128)(2,1)} custom-call(s32[10]{0:T(128)S(1)} %copy-done.17, bf16[512,2048]{1,0:T(8,128)(2,1)S(1)} %bitcast.66, bf16[512,1408]{1,0:T(8,128)(2,1)S(1)} %copy-done.19), custom_call_target="tpu_custom_call" | custom-call | flops 2952790016 | bytes 7864320 | tf_op jit(solution)/shard_map/outer/pallas_call | solution.py:612
  363.1 5.9 outer.13
  369.0 8.2 %all-to-all-done.6.parts = bf16[4,128,2048]{2,1,0:T(8,128)(2,1)} async-done(((bf16[4,128,2048]{2,1,0:T(8,128)(2,1)}), bf16[4,128,2048]{2,1,0:T(8,128)(2,1)}, u32[]{:S(2)}, u32[]{:S(2)}) %all-to-all-start.6) | async-done | bytes 2097184 | tf_op jit(solution)/shard_map/all_to_all | solution.py:702
  377.1 5.0 middle_grad.1
  382.1 50.8 %all_to_all.70 = bf16[4,128,2048]{2,1,0:T(8,128)(2,1)} all-to-all(bf16[4,128,2048]{2,1,0:T(8,128)(2,1)} %get-tuple-element.212), channel_id=1, replica_groups=mesh['far'=2,'x'=2,'core'=2,'zh'=2,'zl'=2] {'x','zl'}, dimensions={0} | all-to-all | bytes 4194304 | tf_op jit(solution)/shard_map/all_to_all | solution.py:702
  432.9 4.7 all-to-all-start.8
  440.0 16.9 %attention_backward.1 = (bf16[512,512]{1,0:T(8,128)(2,1)}, bf16[4096,256]{1,0:T(8,128)(2,1)}) custom-call(s32[10]{0:T(128)} %concatenate.43.meta, bf16[512,512]{1,0:T(8,128)(2,1)} %get-tuple-element.166.q, bf16[512,512]{1,0:T(8,128)(2,1)} %get-tuple-element.169.attn.o.right, bf16[512,2048]{1,0:T(8,128)(2,1)} %bitcast.68, ...), custom_call_target="tpu_custom_call" | custom-call | flops 5368709120 | bytes 6291456 | tf_op jit(solution)/shard_map/attention_backward/pallas_call | solution.py:305
  456.9 6.0 collective-permute-done.29
  477.5 3.9 all-to-all-start.13
  485.1 8.3 %collective-permute-start.32 = (bf16[512,256]{1,0:T(8,128)(2,1)S(1)}, bf16[512,256]{1,0:T(8,128)(2,1)S(1)}, u32[]{:S(2)}, u32[]{:S(2)}) collective-permute-start(bf16[512,256]{1,0:T(8,128)(2,1)S(1)} %get-tuple-element.248), channel_id=1, source_target_pairs={{0,16},{2,18},{16,0},{18,2},{1,17},{3,19},{17,1},{19,3},{4,20},{6,... | collective-permute-start | bytes 786440 | tf_op jit(solution)/shard_map/ppermute | solution.py:681
  495.6 3.8 add_convert_fusion
  499.4 12.6 %collective-permute-done.31 = bf16[512,256]{1,0:T(8,128)(2,1)S(1)} collective-permute-done((bf16[512,256]{1,0:T(8,128)(2,1)S(1)}, bf16[512,256]{1,0:T(8,128)(2,1)S(1)}, u32[]{:S(2)}, u32[]{:S(2)}) %collective-permute-start.31) | collective-permute-done | bytes 262176 | tf_op jit(solution)/shard_map/ppermute | solution.py:681
  512.0 9.8 %collective-permute-done.33 = bf16[512,256]{1,0:T(8,128)(2,1)S(1)} collective-permute-done((bf16[512,256]{1,0:T(8,128)(2,1)S(1)}, bf16[512,256]{1,0:T(8,128)(2,1)S(1)}, u32[]{:S(2)}, u32[]{:S(2)}) %collective-permute-start.33) | collective-permute-done | bytes 262176 | tf_op jit(solution)/shard_map/ppermute | solution.py:681
  523.0 9.7 %qkv_grad.1 = (bf16[512,2048]{1,0:T(8,128)(2,1)}, bf16[512,2048]{1,0:T(8,128)(2,1)}) custom-call(bf16[512,512]{1,0:T(8,128)(2,1)} %get-tuple-element.221.right.grad_q, bf16[512,256]{1,0:T(8,128)(2,1)} %pad_maximum_fusion.5.grad_kv.right, bf16[512,2048]{1,0:T(8,128)(2,1)} %bitcast.4.x, f32[512,1]{1,0:T(8,128)} %get-tuple-element.228.scale, ...), custom_call_target="tpu_custom_call" | custom-call | flops 1879048192 | bytes 6555648 | tf_op jit(solution)/shard_map/qkv_grad/pallas_call | solution.py:331
  532.7 4.5 all-to-all-start.9
  547.8 32.7 %all-to-all-done.9.parts = bf16[4,128,2048]{2,1,0:T(8,128)(2,1)} async-done(((bf16[4,128,2048]{2,1,0:T(8,128)(2,1)}), bf16[4,128,2048]{2,1,0:T(8,128)(2,1)}, u32[]{:S(2)}, u32[]{:S(2)}) %all-to-all-start.9) | async-done | bytes 2097184 | tf_op jit(solution)/shard_map/all_to_all | solution.py:702
  580.5 4.2 all-to-all-start.11
  596.6 4.2 all-to-all-start.12
  600.8 3.9 collective-permute-start.41
  611.2 26.1 %collective-permute-done.41 = bf16[256,384]{1,0:T(8,128)(2,1)S(1)} collective-permute-done((bf16[256,384]{1,0:T(8,128)(2,1)S(1)}, bf16[256,384]{1,0:T(8,128)(2,1)S(1)}, u32[]{:S(2)}, u32[]{:S(2)}) %collective-permute-start.41) | collective-permute-done | bytes 196640 | tf_op jit(solution)/shard_map/ppermute | solution.py:681
  641.9 3.5 all-to-all-start.10
  649.1 3.9 token_grad.1.array
  (293 shorter events, 139.3 us)
Async XLA Ops:
  12.7 20.3 %all-to-all-start = ((bf16[4,64,2304]{2,1,0:T(8,128)(2,1)}), bf16[4,64,2304]{2,1,0:T(8,128)(2,1)S(1)}, u32[]{:S(2)}, u32[]{:S(2)}) async-start(bf16[4,64,2304]{2,1,0:T(8,128)(2,1)} %pack.2), calls=%async_computation | async-start | bytes 2359296 | tf_op jit(solution)/shard_map/all_to_all | solution.py:702
  32.9 38.7 %all-to-all-start.1 = ((bf16[4,128,2048]{2,1,0:T(8,128)(2,1)}), bf16[4,128,2048]{2,1,0:T(8,128)(2,1)}, u32[]{:S(2)}, u32[]{:S(2)}) async-start(bf16[4,128,2048]{2,1,0:T(8,128)(2,1)} %get-tuple-element.127), calls=%async_computation.1 | async-start | bytes 4194304 | tf_op jit(solution)/shard_map/all_to_all | solution.py:702
  37.5 31.9 %collective-permute-start.2 = (bf16[256,896]{1,0:T(8,128)(2,1)S(1)}, bf16[256,896]{1,0:T(8,128)(2,1)S(1)}, u32[]{:S(2)}, u32[]{:S(2)}) collective-permute-start(bf16[256,896]{1,0:T(8,128)(2,1)S(1)} %slice.179.refs_0_), channel_id=1, source_target_pairs={{0,2},{2,0},{1,3},{3,1},{4,6},{6,4},{5,7},{7,5},{8,10},{10,8},{9,1... | collective-permute-start | bytes 1376264 | tf_op jit(solution)/shard_map/ppermute | solution.py:681
  71.6 44.9 %all-to-all-start.2 = ((bf16[4,64,3328]{2,1,0:T(8,128)(2,1)}), bf16[4,64,3328]{2,1,0:T(8,128)(2,1)S(1)}, u32[]{:S(2)}, u32[]{:S(2)}) async-start(bf16[4,64,3328]{2,1,0:T(8,128)(2,1)} %pack.3), calls=%async_computation.2 | async-start | bytes 3407872 | tf_op jit(solution)/shard_map/all_to_all | solution.py:702
  77.1 13.6 %collective-permute-start.3 = (bf16[256,896]{1,0:T(8,128)(2,1)S(1)}, bf16[256,896]{1,0:T(8,128)(2,1)}, u32[]{:S(2)}, u32[]{:S(2)}) collective-permute-start(bf16[256,896]{1,0:T(8,128)(2,1)S(1)} %slice.179.refs_0_), channel_id=1, source_target_pairs={{0,16},{16,0},{1,17},{17,1},{2,18},{18,2},{3,19},{19,3},{4,20},{20... | collective-permute-start | bytes 1376264 | tf_op jit(solution)/shard_map/ppermute | solution.py:681
  78.6 12.0 %collective-permute-start.5 = (bf16[256,896]{1,0:T(8,128)(2,1)S(1)}, bf16[256,896]{1,0:T(8,128)(2,1)}, u32[]{:S(2)}, u32[]{:S(2)}) collective-permute-start(bf16[256,896]{1,0:T(8,128)(2,1)S(1)} %slice.179.refs_0_), channel_id=1, source_target_pairs={{0,4},{4,0},{1,5},{5,1},{2,6},{6,2},{3,7},{7,3},{8,12},{12,8},{9,1... | collective-permute-start | bytes 1376264 | tf_op jit(solution)/shard_map/ppermute | solution.py:681
  78.6 21.9 %collective-permute-start.4 = (bf16[256,896]{1,0:T(8,128)(2,1)}, bf16[256,896]{1,0:T(8,128)(2,1)}, u32[]{:S(2)}, u32[]{:S(2)}) collective-permute-start(bf16[256,896]{1,0:T(8,128)(2,1)} %copy-done.47), channel_id=1, source_target_pairs={{0,16},{16,0},{1,17},{17,1},{2,18},{18,2},{3,19},{19,3},{4,20},{20... | collective-permute-start | bytes 1376264 | tf_op jit(solution)/shard_map/ppermute | solution.py:681
  80.0 34.9 %collective-permute-start = (bf16[256,1408]{1,0:T(8,128)(2,1)}, bf16[256,1408]{1,0:T(8,128)(2,1)S(1)}, u32[]{:S(2)}, u32[]{:S(2)}) collective-permute-start(bf16[256,1408]{1,0:T(8,128)(2,1)} %slice.178.refs_0_), channel_id=1, source_target_pairs={{0,2},{2,0},{1,3},{3,1},{4,6},{6,4},{5,7},{7,5},{8,10},{10,8},{9,1... | collective-permute-start | bytes 2162696 | tf_op jit(solution)/shard_map/ppermute | solution.py:681
  80.1 34.8 %collective-permute-start.1 = (bf16[256,1408]{1,0:T(8,128)(2,1)}, bf16[256,1408]{1,0:T(8,128)(2,1)}, u32[]{:S(2)}, u32[]{:S(2)}) collective-permute-start(bf16[256,1408]{1,0:T(8,128)(2,1)} %slice.178.refs_0_), channel_id=1, source_target_pairs={{0,16},{16,0},{1,17},{17,1},{2,18},{18,2},{3,19},{19,3},{4,20},{20... | collective-permute-start | bytes 2162696 | tf_op jit(solution)/shard_map/ppermute | solution.py:681
  90.6 24.3 %collective-permute-start.6 = (bf16[256,896]{1,0:T(8,128)(2,1)}, bf16[256,896]{1,0:T(8,128)(2,1)S(1)}, u32[]{:S(2)}, u32[]{:S(2)}) collective-permute-start(bf16[256,896]{1,0:T(8,128)(2,1)} %copy-done.47), channel_id=1, source_target_pairs={{0,4},{4,0},{1,5},{5,1},{2,6},{6,2},{3,7},{7,3},{8,12},{12,8},{9,1... | collective-permute-start | bytes 1376264 | tf_op jit(solution)/shard_map/ppermute | solution.py:681
  90.6 24.3 %collective-permute-start.7 = (bf16[256,896]{1,0:T(8,128)(2,1)}, bf16[256,896]{1,0:T(8,128)(2,1)S(1)}, u32[]{:S(2)}, u32[]{:S(2)}) collective-permute-start(bf16[256,896]{1,0:T(8,128)(2,1)} %collective-permute-done.3.refs_2_), channel_id=1, source_target_pairs={{0,4},{4,0},{1,5},{5,1},{2,6},{6,2},{3,7},{7,3},{8,12},{12,8},{9,1... | collective-permute-start | bytes 1376264 | tf_op jit(solution)/shard_map/ppermute | solution.py:681
  100.5 16.0 %collective-permute-start.8 = (bf16[256,896]{1,0:T(8,128)(2,1)}, bf16[256,896]{1,0:T(8,128)(2,1)}, u32[]{:S(2)}, u32[]{:S(2)}) collective-permute-start(bf16[256,896]{1,0:T(8,128)(2,1)} %collective-permute-done.4.refs_3_), channel_id=1, source_target_pairs={{0,4},{4,0},{1,5},{5,1},{2,6},{6,2},{3,7},{7,3},{8,12},{12,8},{9,1... | collective-permute-start | bytes 1376264 | tf_op jit(solution)/shard_map/ppermute | solution.py:681
  117.7 47.7 %all-to-all-start.3 = ((bf16[4,128,2048]{2,1,0:T(8,128)(2,1)}), bf16[4,128,2048]{2,1,0:T(8,128)(2,1)S(1)}, u32[]{:S(2)}, u32[]{:S(2)}) async-start(bf16[4,128,2048]{2,1,0:T(8,128)(2,1)} %get-tuple-element.161), calls=%async_computation.3 | async-start | bytes 4194304 | tf_op jit(solution)/shard_map/all_to_all | solution.py:702
  121.3 100.4 %all-gather.3.cloned.1.call-start = ((), (), s32[]{:S(2)}) async-start(), calls=%async_computation.16 | async-start | bytes 2359296 | tf_op jit(solution)/shard_map/all_gather | solution.py:755
  123.1 180.8 %all-gather.5.cloned.1.call-start = ((), (), s32[]{:S(2)}) async-start(), calls=%async_computation.17 | async-start | bytes 6488064 | tf_op jit(solution)/shard_map/all_gather | solution.py:755
  124.5 40.9 %collective-permute-start.12 = (bf16[256,1408]{1,0:T(8,128)(2,1)S(1)}, bf16[256,1408]{1,0:T(8,128)(2,1)S(1)}, u32[]{:S(2)}, u32[]{:S(2)}) collective-permute-start(bf16[256,1408]{1,0:T(8,128)(2,1)S(1)} %collective-permute-done.refs_1_), channel_id=1, source_target_pairs={{0,16},{16,0},{1,17},{17,1},{2,18},{18,2},{3,19},{19,3},{4,20},{20... | collective-permute-start | bytes 2162696 | tf_op jit(solution)/shard_map/ppermute | solution.py:681
  133.6 23.9 %collective-permute-start.9 = (bf16[512,256]{1,0:T(8,128)(2,1)}, bf16[512,256]{1,0:T(8,128)(2,1)}, u32[]{:S(2)}, u32[]{:S(2)}) collective-permute-start(bf16[512,256]{1,0:T(8,128)(2,1)} %get-tuple-element.162.refs_0_), channel_id=1, source_target_pairs={{0,2},{2,0},{1,3},{3,1},{4,6},{6,4},{5,7},{7,5},{8,10},{10,8},{9,1... | collective-permute-start | bytes 786440 | tf_op jit(solution)/shard_map/ppermute | solution.py:681
  134.4 23.0 %collective-permute-start.10 = (bf16[512,256]{1,0:T(8,128)(2,1)}, bf16[512,256]{1,0:T(8,128)(2,1)}, u32[]{:S(2)}, u32[]{:S(2)}) collective-permute-start(bf16[512,256]{1,0:T(8,128)(2,1)} %get-tuple-element.162.refs_0_), channel_id=1, source_target_pairs={{0,16},{16,0},{1,17},{17,1},{2,18},{18,2},{3,19},{19,3},{4,20},{20... | collective-permute-start | bytes 786440 | tf_op jit(solution)/shard_map/ppermute | solution.py:681
  168.9 51.1 %collective-permute-start.17 = (bf16[256,1408]{1,0:T(8,128)(2,1)S(1)}, bf16[256,1408]{1,0:T(8,128)(2,1)S(1)}, u32[]{:S(2)}, u32[]{:S(2)}) collective-permute-start(bf16[256,1408]{1,0:T(8,128)(2,1)S(1)} %get-tuple-element.198.refs_8_), channel_id=1, source_target_pairs={{0,2},{2,0},{1,3},{3,1},{4,6},{6,4},{5,7},{7,5},{8,10},{10,8},{9,1... | collective-permute-start | bytes 2162696 | tf_op jit(solution)/shard_map/ppermute | solution.py:681
  172.4 47.6 %collective-permute-start.18 = (bf16[256,1408]{1,0:T(8,128)(2,1)S(1)}, bf16[256,1408]{1,0:T(8,128)(2,1)S(1)}, u32[]{:S(2)}, u32[]{:S(2)}) collective-permute-start(bf16[256,1408]{1,0:T(8,128)(2,1)S(1)} %get-tuple-element.198.refs_8_), channel_id=1, source_target_pairs={{0,16},{16,0},{1,17},{17,1},{2,18},{18,2},{3,19},{19,3},{4,20},{20... | collective-permute-start | bytes 2162696 | tf_op jit(solution)/shard_map/ppermute | solution.py:681
  227.0 43.3 %all-to-all-start.4 = ((bf16[4,128,2048]{2,1,0:T(8,128)(2,1)}), bf16[4,128,2048]{2,1,0:T(8,128)(2,1)S(1)}, u32[]{:S(2)}, u32[]{:S(2)}) async-start(bf16[4,128,2048]{2,1,0:T(8,128)(2,1)} %bitcast.73), calls=%async_computation.4 | async-start | bytes 4194304 | tf_op jit(solution)/shard_map/all_to_all | solution.py:702
  230.7 22.4 %collective-permute-start.19 = (bf16[256,1408]{1,0:T(8,128)(2,1)}, bf16[256,1408]{1,0:T(8,128)(2,1)S(1)}, u32[]{:S(2)}, u32[]{:S(2)}) collective-permute-start(bf16[256,1408]{1,0:T(8,128)(2,1)} %copy-done.37), channel_id=1, source_target_pairs={{0,16},{16,0},{1,17},{17,1},{2,18},{18,2},{3,19},{19,3},{4,20},{20... | collective-permute-start | bytes 2162696 | tf_op jit(solution)/shard_map/ppermute | solution.py:681
  232.1 21.0 %collective-permute-start.20 = (bf16[256,1408]{1,0:T(8,128)(2,1)}, bf16[256,1408]{1,0:T(8,128)(2,1)S(1)}, u32[]{:S(2)}, u32[]{:S(2)}) collective-permute-start(bf16[256,1408]{1,0:T(8,128)(2,1)} %slice.178.refs_0_), channel_id=1, source_target_pairs={{0,4},{4,0},{1,5},{5,1},{2,6},{6,2},{3,7},{7,3},{8,12},{12,8},{9,1... | collective-permute-start | bytes 2162696 | tf_op jit(solution)/shard_map/ppermute | solution.py:681
  232.1 21.0 %collective-permute-start.21 = (bf16[256,1408]{1,0:T(8,128)(2,1)S(1)}, bf16[256,1408]{1,0:T(8,128)(2,1)S(1)}, u32[]{:S(2)}, u32[]{:S(2)}) collective-permute-start(bf16[256,1408]{1,0:T(8,128)(2,1)S(1)} %copy-done.35), channel_id=1, source_target_pairs={{0,4},{4,0},{1,5},{5,1},{2,6},{6,2},{3,7},{7,3},{8,12},{12,8},{9,1... | collective-permute-start | bytes 2162696 | tf_op jit(solution)/shard_map/ppermute | solution.py:681
  232.6 20.5 %collective-permute-start.22 = (bf16[256,1408]{1,0:T(8,128)(2,1)}, bf16[256,1408]{1,0:T(8,128)(2,1)S(1)}, u32[]{:S(2)}, u32[]{:S(2)}) collective-permute-start(bf16[256,1408]{1,0:T(8,128)(2,1)} %collective-permute-done.1.refs_2_), channel_id=1, source_target_pairs={{0,4},{4,0},{1,5},{5,1},{2,6},{6,2},{3,7},{7,3},{8,12},{12,8},{9,1... | collective-permute-start | bytes 2162696 | tf_op jit(solution)/shard_map/ppermute | solution.py:681
  232.6 22.8 %collective-permute-start.23 = (bf16[256,1408]{1,0:T(8,128)(2,1)}, bf16[256,1408]{1,0:T(8,128)(2,1)}, u32[]{:S(2)}, u32[]{:S(2)}) collective-permute-start(bf16[256,1408]{1,0:T(8,128)(2,1)} %copy-done.36), channel_id=1, source_target_pairs={{0,4},{4,0},{1,5},{5,1},{2,6},{6,2},{3,7},{7,3},{8,12},{12,8},{9,1... | collective-permute-start | bytes 2162696 | tf_op jit(solution)/shard_map/ppermute | solution.py:681
  275.4 28.4 %all-to-all-start.5 = ((bf16[4,128,2048]{2,1,0:T(8,128)(2,1)}), bf16[4,128,2048]{2,1,0:T(8,128)(2,1)S(1)}, u32[]{:S(2)}, u32[]{:S(2)}) async-start(bf16[4,128,2048]{2,1,0:T(8,128)(2,1)} %get-tuple-element.183), calls=%async_computation.5 | async-start | bytes 4194304 | tf_op jit(solution)/shard_map/all_to_all | solution.py:702
  279.2 198.3 %reduce-scatter.5.cloned.1.call-start = ((), (), s32[]{:S(2)}) async-start(), calls=%async_computation.19 | async-start | bytes 6488064 | tf_op jit(solution)/shard_map/reduce_scatter | solution.py:759
  346.5 30.6 %all-to-all-start.6 = ((bf16[4,128,2048]{2,1,0:T(8,128)(2,1)}), bf16[4,128,2048]{2,1,0:T(8,128)(2,1)}, u32[]{:S(2)}, u32[]{:S(2)}) async-start(bf16[4,128,2048]{2,1,0:T(8,128)(2,1)} %bitcast.80), calls=%async_computation.6 | async-start | bytes 4194304 | tf_op jit(solution)/shard_map/all_to_all | solution.py:702
  432.9 36.0 %all-to-all-start.8 = ((bf16[4,128,2048]{2,1,0:T(8,128)(2,1)}), bf16[4,128,2048]{2,1,0:T(8,128)(2,1)}, u32[]{:S(2)}, u32[]{:S(2)}) async-start(bf16[4,128,2048]{2,1,0:T(8,128)(2,1)} %bitcast.78), calls=%async_computation.8 | async-start | bytes 4194304 | tf_op jit(solution)/shard_map/all_to_all | solution.py:702
  437.6 110.2 %reduce-scatter.3.cloned.1.call-start = ((), (), s32[]{:S(2)}) async-start(), calls=%async_computation.18 | async-start | bytes 6488064 | tf_op jit(solution)/shard_map/reduce_scatter | solution.py:759
  438.9 24.0 %collective-permute-start.29 = (bf16[512,1408]{1,0:T(8,128)(2,1)}, bf16[512,1408]{1,0:T(8,128)(2,1)}, u32[]{:S(2)}, u32[]{:S(2)}) collective-permute-start(bf16[512,1408]{1,0:T(8,128)(2,1)} %slice.146), channel_id=1, source_target_pairs={{0,16},{16,0},{1,17},{17,1},{2,18},{18,2},{3,19},{19,3},{4,20},{20... | collective-permute-start | bytes 4325384 | tf_op jit(solution)/shard_map/ppermute | solution.py:681
  472.7 22.9 %collective-permute-start.34 = (bf16[1024,1024]{1,0:T(8,128)(2,1)}, bf16[1024,1024]{1,0:T(8,128)(2,1)}, u32[]{:S(2)}, u32[]{:S(2)}) collective-permute-start(bf16[1024,1024]{1,0:T(8,128)(2,1)} %pad_maximum_fusion), channel_id=1, source_target_pairs={{0,4},{4,0},{1,5},{5,1},{2,6},{6,2},{3,7},{7,3},{8,12},{12,8},{9,1... | collective-permute-start | bytes 6291464 | tf_op jit(solution)/shard_map/ppermute | solution.py:681
  477.5 55.2 %all-to-all-start.13 = ((bf16[4,64,1408]{2,1,0:T(8,128)(2,1)}), bf16[4,64,1408]{2,1,0:T(8,128)(2,1)S(1)}, u32[]{:S(2)}, u32[]{:S(2)}) async-start(bf16[4,64,1408]{2,1,0:T(8,128)(2,1)} %bitcast.85), calls=%async_computation.15 | async-start | bytes 1441792 | tf_op jit(solution)/shard_map/all_to_all | solution.py:702
  485.0 26.9 %collective-permute-start.31 = (bf16[512,256]{1,0:T(8,128)(2,1)S(1)}, bf16[512,256]{1,0:T(8,128)(2,1)S(1)}, u32[]{:S(2)}, u32[]{:S(2)}) collective-permute-start(bf16[512,256]{1,0:T(8,128)(2,1)S(1)} %get-tuple-element.249), channel_id=1, source_target_pairs={{0,2},{2,0},{16,18},{18,16},{1,3},{3,1},{17,19},{19,17},{4,6},{6,4... | collective-permute-start | bytes 786440 | tf_op jit(solution)/shard_map/ppermute | solution.py:681
  485.1 26.9 %collective-permute-start.32 = (bf16[512,256]{1,0:T(8,128)(2,1)S(1)}, bf16[512,256]{1,0:T(8,128)(2,1)S(1)}, u32[]{:S(2)}, u32[]{:S(2)}) collective-permute-start(bf16[512,256]{1,0:T(8,128)(2,1)S(1)} %get-tuple-element.248), channel_id=1, source_target_pairs={{0,16},{2,18},{16,0},{18,2},{1,17},{3,19},{17,1},{19,3},{4,20},{6,... | collective-permute-start | bytes 786440 | tf_op jit(solution)/shard_map/ppermute | solution.py:681
  493.3 28.4 %collective-permute-start.33 = (bf16[512,256]{1,0:T(8,128)(2,1)S(1)}, bf16[512,256]{1,0:T(8,128)(2,1)S(1)}, u32[]{:S(2)}, u32[]{:S(2)}) collective-permute-start(bf16[512,256]{1,0:T(8,128)(2,1)S(1)} %get-tuple-element.247), channel_id=1, source_target_pairs={{0,18},{2,16},{16,2},{18,0},{1,19},{3,17},{17,3},{19,1},{4,22},{6,... | collective-permute-start | bytes 786440 | tf_op jit(solution)/shard_map/ppermute | solution.py:681
  532.7 47.8 %all-to-all-start.9 = ((bf16[4,128,2048]{2,1,0:T(8,128)(2,1)}), bf16[4,128,2048]{2,1,0:T(8,128)(2,1)}, u32[]{:S(2)}, u32[]{:S(2)}) async-start(bf16[4,128,2048]{2,1,0:T(8,128)(2,1)} %bitcast.79), calls=%async_computation.9 | async-start | bytes 4194304 | tf_op jit(solution)/shard_map/all_to_all | solution.py:702
  539.6 45.1 %collective-permute-start.37 = (bf16[256,1408]{1,0:T(8,128)(2,1)}, bf16[256,1408]{1,0:T(8,128)(2,1)}, u32[]{:S(2)}, u32[]{:S(2)}) collective-permute-start(bf16[256,1408]{1,0:T(8,128)(2,1)} %slice.160), channel_id=1, source_target_pairs={{0,2},{2,0},{1,3},{3,1},{4,6},{6,4},{5,7},{7,5},{8,10},{10,8},{9,1... | collective-permute-start | bytes 2162696 | tf_op jit(solution)/shard_map/ppermute | solution.py:681
  546.5 46.2 %collective-permute-start.35 = (bf16[1024,384]{1,0:T(8,128)(2,1)}, bf16[1024,384]{1,0:T(8,128)(2,1)}, u32[]{:S(2)}, u32[]{:S(2)}) collective-permute-start(bf16[1024,384]{1,0:T(8,128)(2,1)} %pad_maximum_fusion.1), channel_id=1, source_target_pairs={{0,4},{4,0},{1,5},{5,1},{2,6},{6,2},{3,7},{7,3},{8,12},{12,8},{9,1... | collective-permute-start | bytes 2359304 | tf_op jit(solution)/shard_map/ppermute | solution.py:681
  547.5 46.5 %collective-permute-start.36 = (bf16[512,1024]{1,0:T(8,128)(2,1)}, bf16[512,1024]{1,0:T(8,128)(2,1)}, u32[]{:S(2)}, u32[]{:S(2)}) collective-permute-start(bf16[512,1024]{1,0:T(8,128)(2,1)} %slice.158), channel_id=1, source_target_pairs={{0,16},{16,0},{1,17},{17,1},{2,18},{18,2},{3,19},{19,3},{4,20},{20... | collective-permute-start | bytes 3145736 | tf_op jit(solution)/shard_map/ppermute | solution.py:681
  580.5 16.0 %all-to-all-start.11 = ((bf16[4,64,1408]{2,1,0:T(8,128)(2,1)}), bf16[4,64,1408]{2,1,0:T(8,128)(2,1)}, u32[]{:S(2)}, u32[]{:S(2)}) async-start(bf16[4,64,1408]{2,1,0:T(8,128)(2,1)} %bitcast.84), calls=%async_computation.12 | async-start | bytes 1441792 | tf_op jit(solution)/shard_map/all_to_all | solution.py:702
  596.6 43.1 %collective-permute-start.38 = (bf16[256,1024]{1,0:T(8,128)(2,1)}, bf16[256,1024]{1,0:T(8,128)(2,1)}, u32[]{:S(2)}, u32[]{:S(2)}) collective-permute-start(bf16[256,1024]{1,0:T(8,128)(2,1)} %slice.163), channel_id=1, source_target_pairs={{0,2},{2,0},{1,3},{3,1},{4,6},{6,4},{5,7},{7,5},{8,10},{10,8},{9,1... | collective-permute-start | bytes 1572872 | tf_op jit(solution)/shard_map/ppermute | solution.py:681
  596.6 45.3 %all-to-all-start.12 = ((bf16[4,64,1408]{2,1,0:T(8,128)(2,1)}), bf16[4,64,1408]{2,1,0:T(8,128)(2,1)S(1)}, u32[]{:S(2)}, u32[]{:S(2)}) async-start(bf16[4,64,1408]{2,1,0:T(8,128)(2,1)} %bitcast.30), calls=%async_computation.13 | async-start | bytes 1441792 | tf_op jit(solution)/shard_map/all_to_all | solution.py:702
  600.8 36.5 %collective-permute-start.41 = (bf16[256,384]{1,0:T(8,128)(2,1)S(1)}, bf16[256,384]{1,0:T(8,128)(2,1)S(1)}, u32[]{:S(2)}, u32[]{:S(2)}) collective-permute-start(bf16[256,384]{1,0:T(8,128)(2,1)S(1)} %get-tuple-element.251), channel_id=1, source_target_pairs={{0,18},{2,16},{16,2},{18,0},{1,19},{3,17},{17,3},{19,1},{4,22},{6,... | collective-permute-start | bytes 589832 | tf_op jit(solution)/shard_map/ppermute | solution.py:681
  604.7 32.6 %collective-permute-start.40 = (bf16[256,384]{1,0:T(8,128)(2,1)S(1)}, bf16[256,384]{1,0:T(8,128)(2,1)S(1)}, u32[]{:S(2)}, u32[]{:S(2)}) collective-permute-start(bf16[256,384]{1,0:T(8,128)(2,1)S(1)} %get-tuple-element.252), channel_id=1, source_target_pairs={{0,16},{2,18},{16,0},{18,2},{1,17},{3,19},{17,1},{19,3},{4,20},{6,... | collective-permute-start | bytes 589832 | tf_op jit(solution)/shard_map/ppermute | solution.py:681
  605.2 34.4 %collective-permute-start.39 = (bf16[256,384]{1,0:T(8,128)(2,1)S(1)}, bf16[256,384]{1,0:T(8,128)(2,1)S(1)}, u32[]{:S(2)}, u32[]{:S(2)}) collective-permute-start(bf16[256,384]{1,0:T(8,128)(2,1)S(1)} %get-tuple-element.250), channel_id=1, source_target_pairs={{0,2},{2,0},{16,18},{18,16},{1,3},{3,1},{17,19},{19,17},{4,6},{6,4... | collective-permute-start | bytes 589832 | tf_op jit(solution)/shard_map/ppermute | solution.py:681
  641.9 14.8 %all-to-all-start.10 = ((bf16[4,64,1408]{2,1,0:T(8,128)(2,1)}), bf16[4,64,1408]{2,1,0:T(8,128)(2,1)S(1)}, u32[]{:S(2)}, u32[]{:S(2)}) async-start(bf16[4,64,1408]{2,1,0:T(8,128)(2,1)} %bitcast.21), calls=%async_computation.10 | async-start | bytes 1441792 | tf_op jit(solution)/shard_map/all_to_all | solution.py:702
  (68 other events, 601.6 us)
Sparse Core Ops, SparseCore 0:
  124.6 42.9 all-gather.2
  170.1 85.7 all-gather.4
  346.6 84.8 reduce-scatter.4
  442.0 101.8 reduce-scatter.2

commit v2 on v1

--- a/solution.py
+++ b/solution.py
@@ -68,6 +68,10 @@
     return ((core_i ^ core) * far_n + (far_i ^ far)) * zh_n + (zh_i ^ zh)
 
 
+def pair_rows(meta, sizes, i, run):
+    return [pl.ds(run_row(meta, sizes, 2 * i + n, run), run) for n in range(2)]
+
+
 def forward_kernel(
     docs, sizes, run, count, meta, q, cosine, sine, qpos, qstart, kown, klocal, *refs
 ):
@@ -77,37 +81,25 @@
     starts = [meta[5 + d] for d in range(docs)]
     factor = SCALE * LOG2E
     tile = 2 * run
-    out, q_rot, lse, kv, sems, vt, vown, top, total, acc = refs[count:]
+    out, q_rot, lse, kv, sems, top, total, acc = refs[count:]
     copies = load_pieces(refs[:count], kv, sems, 0)
     for copy in copies:
         copy.wait()
-    vown[...] = kv[:tile, HEAD_DIM:].T
-
-    def flip(j, _):
-        vt[j] = kv[pl.ds(run_row(meta, sizes, j, run), run), HEAD_DIM:].T
-        return 0
-
-    lax.fori_loop(first, high, flip, 0)
 
     heads = range(SHARE)
-    keys = kv[:tile, :HEAD_DIM]
-    own = visible(kown[...], qpos[...], qstart[...])
     for h in heads:
         lanes = slice(h * HEAD_DIM, (h + 1) * HEAD_DIM)
-        q_head = turned(q[:, lanes], cosine[...], sine[...]).astype(BF)
-        q_rot[:, lanes] = q_head
-        raw = jnp.where(own, dot(keys, q_head, 1, 1), -FAR)
-        peak = jnp.max(raw, axis=0, keepdims=True)
-        weights = jnp.exp2(raw * factor - peak * factor)
-        top[h : h + 1, :] = peak
-        total[h : h + 1, :] = jnp.sum(weights, axis=0, keepdims=True)
-        acc[h] = dot(vown[...], weights.astype(BF))
-
-    def fold(j, masked):
-        base = j * run
-        keys = kv[pl.ds(run_row(meta, sizes, j, run), run), :HEAD_DIM]
-        values = vt[j]
-        seen = (qstart[...] <= base) & (qpos[...] >= base + run - 1)
+        q_rot[:, lanes] = turned(q[:, lanes], cosine[...], sine[...]).astype(BF)
+    top[...] = jnp.full_like(top, -FAR)
+    total[...] = jnp.zeros_like(total)
+    acc[...] = jnp.zeros_like(acc)
+
+    def fold(i, masked):
+        base = i * tile
+        rows = pair_rows(meta, sizes, i, run)
+        keys = jnp.concatenate([kv[r, :HEAD_DIM] for r in rows], axis=0)
+        values = jnp.concatenate([kv[r, HEAD_DIM:] for r in rows], axis=0).T
+        seen = (qstart[...] <= base) & (qpos[...] >= base + tile - 1)
         if masked:
             allowed = visible(klocal[...] + base, qpos[...], qstart[...])
         for h in heads:
@@ -117,7 +109,7 @@
             if masked:
                 raw = jnp.where(allowed, raw, -FAR)
                 peak = jnp.maximum(before, jnp.max(raw, axis=0, keepdims=True))
-                level = peak * factor
+                level = jnp.where(peak > -0.5 * FAR, peak * factor, FAR)
             else:
                 new = jnp.max(raw, axis=0, keepdims=True)
                 peak = jnp.maximum(before, jnp.where(seen, new, -FAR))
@@ -130,21 +122,20 @@
             )
             acc[h] = acc[h] * fade + dot(values, weights.astype(BF))
 
-    def step(j, _):
-        mixed = is_mixed(starts, j * run, run)
-        other = j != low
-
-        @pl.when(other & mixed)
+    def step(i, _):
+        mixed = is_mixed(starts, i * tile, tile) | (i == low // 2) | (i == high // 2)
+
+        @pl.when(mixed)
         def _():
-            fold(j, True)
-
-        @pl.when(other & jnp.logical_not(mixed))
+            fold(i, True)
+
+        @pl.when(jnp.logical_not(mixed))
         def _():
-            fold(j, False)
+            fold(i, False)
 
         return 0
 
-    lax.fori_loop(first, high, step, 0)
+    lax.fori_loop(first // 2, high // 2 + 1, step, 0)
     for h in heads:
         lanes = slice(h * HEAD_DIM, (h + 1) * HEAD_DIM)
         out[:, lanes] = (acc[h] / total[h : h + 1, :]).T.astype(BF)
@@ -200,57 +191,51 @@
 
     lax.fori_loop(0, SHARE, prepare, 0)
 
-    def key_step(rows, count, kpos, base):
-        k_tile = kv[rows, :HEAD_DIM]
-        v_tile = kv[rows, HEAD_DIM:]
+    def key_step(i, masked):
+        base = i * tile
+        rows = pair_rows(meta, sizes, i, run)
+        k_tile = jnp.concatenate([kv[r, :HEAD_DIM] for r in rows], axis=0)
+        v_tile = jnp.concatenate([kv[r, HEAD_DIM:] for r in rows], axis=0)
         kt = k_tile.T
-
-        def head(h, carry):
-            grad_k, grad_v = carry
+        seen = (qstart[...] <= base) & (qpos[...] >= base + tile - 1)
+        if masked:
+            allowed = visible(klocal[...] + base, qpos[...], qstart[...])
+        grad_k = jnp.zeros((tile, HEAD_DIM), F32)
+        grad_v = jnp.zeros((tile, HEAD_DIM), F32)
+        for h in range(SHARE):
             lanes = slice(h * HEAD_DIM, (h + 1) * HEAD_DIM)
             q_head = q[:, lanes]
             g_head = g[:, lanes]
             raw = dot(k_tile, q_head, 1, 1) * factor
             level = lse[h : h + 1, :]
-            if kpos is not None:
-                probs = jnp.exp2(raw - level)
-                probs = jnp.where(visible(kpos, qpos[...], qstart[...]), probs, 0.0)
+            if masked:
+                probs = jnp.where(allowed, jnp.exp2(raw - level), 0.0)
             else:
-                seen = (qstart[...] <= base) & (qpos[...] >= base + run - 1)
                 probs = jnp.exp2(raw - jnp.where(seen, level, FAR))
             slopes = dot(v_tile, g_head, 1, 1)
             grads = (probs * (slopes - delta[h : h + 1, :])).astype(BF)
             grad_v = grad_v + dot(probs.astype(BF), g_head)
             grad_k = grad_k + dot(grads, q_head)
             dqt[h] = dqt[h] + dot(kt, grads)
-            return grad_k, grad_v
-
-        zero = jnp.zeros((count, HEAD_DIM), F32)
-        grad_k, grad_v = zero, zero
-        for h in range(SHARE):
-            grad_k, grad_v = head(h, (grad_k, grad_v))
-        grad_kv[rows, :HEAD_DIM] = (grad_k * SCALE).astype(BF)
-        grad_kv[rows, HEAD_DIM:] = grad_v.astype(BF)
-
-    key_step(pl.ds(0, tile), tile, kown[...], 0)
-
-    def step(j, _):
-        base = j * run
-        mixed = is_mixed(starts, base, run)
-        other = j != low
-        rows = pl.ds(run_row(meta, sizes, j, run), run)
-
-        @pl.when(other & mixed)
+        for n, at in enumerate(rows):
+            part = slice(n * run, (n + 1) * run)
+            grad_kv[at, :HEAD_DIM] = (grad_k[part] * SCALE).astype(BF)
+            grad_kv[at, HEAD_DIM:] = grad_v[part].astype(BF)
+
+    def step(i, _):
+        mixed = is_mixed(starts, i * tile, tile) | (i == low // 2) | (i == high // 2)
+
+        @pl.when(mixed)
         def _():
-            key_step(rows, run, klocal[...] + base, base)
-
-        @pl.when(other & jnp.logical_not(mixed))
+            key_step(i, True)
+
+        @pl.when(jnp.logical_not(mixed))
         def _():
-            key_step(rows, run, None, base)
+            key_step(i, False)
 
         return 0
 
-    lax.fori_loop(first, high, step, 0)
+    lax.fori_loop(first // 2, high // 2 + 1, step, 0)
 
     def finish(h, _):
         lanes = pl.ds(pl.multiple_of(h * HEAD_DIM, HEAD_DIM), HEAD_DIM)
@@ -283,8 +268,6 @@
         scratch_shapes=[
             pltpu.VMEM((span, 2 * HEAD_DIM), BF),
             pltpu.SemaphoreType.DMA((len(kv),)),
-            pltpu.VMEM((span // run, HEAD_DIM, run), BF),
-            pltpu.VMEM((HEAD_DIM, tile), BF),
             pltpu.VMEM((SHARE, tile), F32),
             pltpu.VMEM((SHARE, tile), F32),
             pltpu.VMEM((SHARE, HEAD_DIM, tile), F32),
@@ -522,14 +505,12 @@
     out[...] = (middle[...] + keep[...] * ffn).astype(BF)
 
 
-def mlp_kernel(sizes, counts, meta, x, g, *refs):
-    total = sum(counts)
-    gate_pieces, up_pieces = refs[: counts[0]], refs[counts[0] : total]
-    down = refs[total]
-    hidden, grad_gate, grad_up, grad_x, ffn, w_g, w_u, w_d, sems = refs[total + 1 :]
-    copies = load_pieces(gate_pieces, w_g, sems, 0)
-    copies += load_pieces(up_pieces, w_u, sems, counts[0])
-    late = load_natural(meta, sizes, down, w_d, sems, total)
+def mlp_kernel(sizes, count, meta, x, g, gate_rows, *refs):
+    pieces = refs[: 2 * count]
+    hidden, grad_gate, grad_up, grad_x, ffn, w_g, w_u, w_d, sems = refs[2 * count :]
+    copies = load_natural(meta, sizes, gate_rows, w_g, sems, 2 * count)
+    copies += load_pieces(pieces[:count], w_u, sems, 0)
+    late = load_pieces(pieces[count:], w_d, sems, count)
     for copy in copies:
         copy.wait()
     features, width = w_g.shape
@@ -568,19 +549,17 @@
 
 def mlp(meta, sizes, x, g, w_gate, w_up, w_down):
     rows, features = x.shape
-    width = w_down.shape[1]
-    counts = (len(w_gate), len(w_up))
-    pieces = [*w_gate, *w_up, w_down]
+    width = w_gate.shape[1]
+    count = len(w_up)
+    pieces = [w_gate, *w_up, *w_down]
+    copies = 2 * count + 2 * sizes[0] * sizes[1]
     return call(
-        functools.partial(mlp_kernel, sizes, counts),
+        functools.partial(mlp_kernel, sizes, count),
         "mlp",
         [((rows, width), BF)] * 3 + [((rows, features), BF)] * 2,
         [meta, x, g, *pieces],
         [SMEM] + [VMEM] * 2 + [ANY] * len(pieces),
-        [
-            *([pltpu.VMEM((features, width), BF)] * 3),
-            pltpu.SemaphoreType.DMA((sum(counts) + 2 * sizes[0] * sizes[1],)),
-        ],
+        [*([pltpu.VMEM((features, width), BF)] * 3), pltpu.SemaphoreType.DMA((copies,))],
         12 * rows * features * width,
     )
 
@@ -599,16 +578,19 @@
         part = left if half is None else left[:, half * sizes_held : (half + 1) * sizes_held]
         product = dot(part, right, 0, 0)
         if natural:
-            shape = (2, sizes[0], sizes[1], -1, right.shape[1])
+            shape = (sizes[0], sizes[1], -1, right.shape[1])
             product = product.reshape(shape)
-            for axis, name in enumerate(("core", "far", "zh")):
+            for axis, name in enumerate(("far", "zh")):
                 product = by_distance(product, axis, lax.axis_index(name))
-            product = product.reshape(features, -1)
+            product = product.reshape(sizes_held, -1)
         return (product if added is None else product + added.astype(F32)).astype(BF)
     slots = 2 * sizes[0] * sizes[1]
     rows, block, width = left.shape[0], features // slots, right.shape[1]
     count, start = (slots, 0) if half is None else (slots // 2, half * slots // 2)
     held = pl.BlockSpec((block, width), lambda i, m: (i, 0))
+    natural_rows = pl.BlockSpec(
+        (block, width), lambda i, m: (lax.rem(natural_slot(m, sizes, i), count), 0)
+    )
     return pl.pallas_call(
         outer_kernel,
         out_shape=jax.ShapeDtypeStruct((count * block, width), BF),
@@ -619,10 +601,8 @@
                 pl.BlockSpec((rows, block), lambda i, m: (0, start + i)),
                 pl.BlockSpec((rows, width), lambda i, m: (0, 0)),
             ]
-            + ([] if added is None else [held]),
-            out_specs=pl.BlockSpec((block, width), lambda i, m: (natural_slot(m, sizes, i), 0))
-            if natural
-            else held,
+            + ([] if added is None else [natural_rows if natural else held]),
+            out_specs=natural_rows if natural else held,
         ),
         compiler_params=pltpu.CompilerParams(vmem_limit_bytes=48 << 20),
         cost_estimate=pl.CostEstimate(
@@ -756,7 +736,7 @@
 
 
 def gather_back(partial):
-    return lax.psum_scatter(partial, SLOT, scatter_dimension=0, tiled=True)
+    return lax.psum_scatter(partial, ("far", "zh"), scatter_dimension=0, tiled=True)
 
 
 def to_owner(part):
@@ -831,13 +811,14 @@
     )
     small = jnp.pad(small, ((0, 0), (0, HEAD_DIM - ids - 2)))
     small = jnp.concatenate([small] * team, axis=1)
-    first_rows = to_team(pack(team, [w_query, w_key, w_value, small, w_gate]))
+    first_rows = to_team(pack(team, [w_query, w_key, w_value, small, w_output.T, w_gate]))
     first_rows = first_rows.reshape(-1, first_rows.shape[2])
     qkv_width = part + 3 * HEAD_DIM
     qkv_plane = plane_first(first_rows[:, :qkv_width])
-    gate_rows = first_rows[:, qkv_width:]
-
-    last_rows = pack(team, [w_output.T, w_up, w_down.T])
+    out_rows = first_rows[:, qkv_width : qkv_width + part]
+    gate_rows = first_rows[:, qkv_width + part :]
+
+    last_rows = pack(team, [w_up, w_down.T])
     tokens_own, tokens_sent = slots_and_copies(tokens, keep, False, team)
     cot_own, cot_sent = slots_and_copies(cotangent, keep, True, team)
     tokens_all = to_team(after(tokens_sent, first_rows)).reshape(tile, features)
@@ -852,20 +833,17 @@
     cosine = jnp.concatenate([cosine, cosine], axis=1)
     sine = jnp.concatenate([-sine, sine], axis=1)
 
-    qkv_near, last_rows, cot_sent = together(qkv_plane[1], last_rows, cot_sent)
-    qkv_plane = (qkv_plane[0], qkv_near, qkv_plane[2])
-    gate_plane = plane_first(gate_rows)
+    qkv_plane, last_rows, cot_sent, tokens_all = together(
+        qkv_plane, last_rows, cot_sent, tokens_all
+    )
+    w_out = spread(after(out_rows, qkv_plane))
     w_qkv = both_cores(plane_second(qkv_plane))
+    tokens_all, w_qkv, cosine, sine = together(tokens_all, w_qkv, cosine, sine)
     last_rows = to_team(after(last_rows, tokens_all)).reshape(-1, last_rows.shape[2])
-    tokens_all, gate_plane, w_qkv, cosine, sine, last_rows = together(
-        tokens_all, gate_plane, w_qkv, cosine, sine, last_rows
-    )
-    gate_plane = plane_second(gate_plane)
-    w_out = spread(last_rows[:, :part])
-    grad_ffn = to_team(after(cot_sent, last_rows))
 
     normed_one, scale_all, q, kv, small_all = project(tokens_all, cosine, sine, w_qkv, ids)
     kv_plane = plane_first(kv)
+    w_g = spread(after(gate_rows, kv))
     gain_one = small_all[ids : ids + 1]
     gain_two = small_all[ids + 1 : ids + 2]
     doc_starts = jnp.sum(
@@ -885,18 +863,17 @@
         position[None, :],
         query_start[None, :],
         position[:, None],
-        lax.iota(jnp.int32, run)[:, None],
-    )
+        lax.iota(jnp.int32, tile)[:, None],
+    )
+    up_rows, down_rows = last_rows[:, :ff], last_rows[:, ff:]
     kv_plane, meta, tables = together(kv_plane, meta, tables)
     kv_plane = plane_second(kv_plane)
-    kv_plane, gate_plane, last_rows, grad_ffn = together(
-        kv_plane, gate_plane, last_rows, grad_ffn
-    )
-    w_d = spread(last_rows[:, part + ff :])
+    kv_plane, w_out, up_rows, down_rows = together(kv_plane, w_out, up_rows, down_rows)
+    grad_ffn = to_team(after(cot_sent, up_rows))
     kv = both_cores(kv_plane)
-    up_plane = plane_first(last_rows[:, part : part + ff])
+    up_plane = plane_first(up_rows)
     attn, query, log_total = attention_forward(meta, docs, sizes, q, tables, kv)
-    attn, up_plane = together(attn, up_plane)
+    attn, grad_ffn, up_plane, w_g = together(attn, grad_ffn, up_plane, w_g)
     grad_ffn = grad_ffn.reshape(tile, features)
 
     proj = call(
@@ -907,11 +884,10 @@
         [SMEM, VMEM, ANY],
         [pltpu.VMEM(w_out.shape, BF), pltpu.SemaphoreType.DMA((2 * far_n * zh_n,))],
     )[0]
-    gate_plane = after(gate_plane, attn)
+    down_plane = plane_first(after(down_rows, attn))
     proj = sum_team(proj)
     up_plane = plane_second(up_plane)
-    w_g = both_cores(gate_plane)
-    proj, up_plane, w_g = together(proj, up_plane, w_g)
+    proj, up_plane, down_plane = together(proj, up_plane, down_plane)
     middle, normed_sent = call(
         middle_kernel,
         "middle",
@@ -920,20 +896,21 @@
     )
     normed_two = to_team(normed_sent)
     w_u = both_cores(up_plane)
-    normed_two, w_u = together(normed_two, w_u)
+    w_d = both_cores(plane_second(down_plane))
+    normed_two, w_u, w_d = together(normed_two, w_u, w_d)
     normed_two = normed_two.reshape(tile, features)
 
     hidden, grad_gate_act, grad_up_act, grad_two, ffn = mlp(
         meta, sizes, normed_two, grad_ffn, w_g, w_u, w_d
     )
     grad_two_parts = sum_team(grad_two)
-    grad_down = outer(meta, sizes, grad_ffn, hidden, natural=True)
-    other_up = swap(outer(meta, sizes, normed_two, grad_up_act, half=1), "core", 1)
-    grad_gate = outer(meta, sizes, normed_two, grad_gate_act, natural=True)
-    up_core = outer(meta, sizes, normed_two, grad_up_act, half=0, added=other_up)
-    grad_two_parts, up_core, grad_gate = together(grad_two_parts, up_core, grad_gate)
-    grad_down = gather_back(grad_down)
-    grad_gate = gather_back(grad_gate)
+    other_down = swap(outer(meta, sizes, grad_ffn, hidden, 1, True), "core", 1)
+    other_gate = swap(outer(meta, sizes, normed_two, grad_gate_act, 1), "core", 1)
+    other_up = swap(outer(meta, sizes, normed_two, grad_up_act, 1), "core", 1)
+    grad_down = gather_back(outer(meta, sizes, grad_ffn, hidden, 0, True, other_down))
+    gate_core = outer(meta, sizes, normed_two, grad_gate_act, 0, False, other_gate)
+    up_core = outer(meta, sizes, normed_two, grad_up_act, 0, False, other_up)
+    grad_two_parts, gate_core = together(grad_two_parts, gate_core)
     grad_middle, grad_proj_sent, terms_two = call(
         middle_grad_kernel,
         "middle_grad",
@@ -941,15 +918,22 @@
         [grad_two_parts, middle, cot_own, keep, gain_two],
     )
     grad_proj = to_team(grad_proj_sent)
+    gate_far = sum_axis(gate_core, "far", grad_proj_sent)
+    grad_proj, up_core, gate_far = together(grad_proj, up_core, gate_far)
     grad_proj = grad_proj.reshape(tile, features)
     ffn = sum_team(after(ffn, grad_proj))
     grad_query, grad_kv = attention_backward(
         meta, docs, sizes, query, attn, grad_proj, w_out, log_total, tables, kv
     )
+    gate_zh = sum_axis(gate_far, "zh", grad_kv)
     up_far = sum_axis(up_core, "far", grad_kv)
-    grad_query, grad_kv, ffn, up_far = together(grad_query, grad_kv, ffn, up_far)
+    grad_query, grad_kv, ffn, gate_zh, up_far, grad_down = together(
+        grad_query, grad_kv, ffn, gate_zh, up_far, grad_down
+    )
     half = grad_kv.shape[0] // 2
     other_kv = swap(grad_kv[half:], "core", 1)
+    grad_query = after(grad_query, other_kv)
+    attn_late = after(attn, other_kv)
     grad_kv = grad_kv[:half].astype(F32) + other_kv.astype(F32)
     grad_kv_parts = [grad_kv[:tile]] + [
         swap(grad_kv[d * tile : (d + 1) * tile].astype(BF), ("far", "zh"), d)
@@ -961,7 +945,7 @@
     other_q = jnp.concatenate(
         [
             outer(meta, sizes, normed_one, grad_query, half=1),
-            outer(meta, sizes, grad_proj, attn, half=1),
+            outer(meta, sizes, grad_proj, attn_late, half=1),
         ],
         axis=1,
     )
@@ -969,14 +953,14 @@
     own_q = jnp.concatenate(
         [
             outer(meta, sizes, normed_one, grad_query, half=0),
-            outer(meta, sizes, grad_proj, attn, half=0),
+            outer(meta, sizes, grad_proj, attn_late, half=0),
         ],
         axis=1,
     )
     q_core = (own_q.astype(F32) + other_q.astype(F32)).astype(BF)
     grad_kv_parts, q_core = together(grad_kv_parts, q_core)
     q_far = sum_axis(q_core, "far")
-    up_zh = sum_axis(up_far, "zh")
+    up_zh = sum_axis(after(up_far, grad_kv_parts), "zh")
     grad_kv_sum = total_of(grad_kv_parts)
     grad_key = turn(grad_kv_sum[:, :HEAD_DIM].astype(BF).astype(F32), cosine, -sine).astype(BF)
     grad_kv_tok = jnp.concatenate([grad_key, grad_kv_sum[:, HEAD_DIM:].astype(BF)], axis=1)
@@ -1009,11 +993,10 @@
             for d in range(1, far_n * zh_n)
         ]
     ).astype(BF)
-    grad_up, grad_down, grad_gate = [to_owner(a) for a in (up_zh, grad_down, grad_gate)]
-    grad_w = to_owner(jnp.concatenate([q_zh, small_sum], axis=1))
-    grad_out = grad_w[:, :, part : 2 * part]
-    grad_w = jnp.concatenate([grad_w[:, :, :part], grad_w[:, :, 2 * part :]], axis=2)
-    gains = total_of(grad_w[:, :, part + 2 * HEAD_DIM :])
+    merged = to_owner(jnp.concatenate([grad_down, gate_zh, up_zh], axis=1))
+    grad_down, grad_gate, grad_up = (
+        merged[:, :, :ff], merged[:, :, ff : 2 * ff], merged[:, :, 2 * ff :]
+    )
     grad_tokens = to_natural(
         call(
             token_grad_kernel,
@@ -1022,6 +1005,13 @@
             [grad_one, tokens_own, grad_middle, gain_one],
         )[0]
     )
+    finished = [wide(grad_gate), wide(grad_up), wide(grad_down).T]
+    grad_w = jnp.concatenate([q_zh, small_sum], axis=1)
+    grad_w, finished, output, grad_tokens = together(grad_w, finished, output, grad_tokens)
+    grad_w = to_owner(grad_w)
+    grad_out = grad_w[:, :, part : 2 * part]
+    grad_w = jnp.concatenate([grad_w[:, :, :part], grad_w[:, :, 2 * part :]], axis=2)
+    gains = total_of(grad_w[:, :, part + 2 * HEAD_DIM :])
     return (
         output,
         grad_tokens,
@@ -1031,9 +1021,7 @@
         wide(grad_w[:, :, part + HEAD_DIM : part + 2 * HEAD_DIM]),
         wide(grad_out).T,
         gains[:, 1],
-        wide(grad_gate),
-        wide(grad_up),
-        wide(grad_down).T,
+        *finished,
     )
 
 

time: 677 us -> 668 us (0.987)
  blocking collectives: 50.8 us -> 15.3 us
  waiting for transfers between devices: 273 us -> 308 us
  local copies, waits for them, and re-layouts: 47 us -> 37.7 us
  Pallas kernels: 157 us -> 165 us
  other arithmetic: 29.6 us -> 22.2 us
    ppermute x42 -> x46, waiting for transfers between devices: 187 us -> 275 us  [swap(): return lax.ppermute(block, axes, [(i, i ^ distance) for i in range(size)])]
    all_to_all x13 -> x11, waiting for transfers between devices: 85.1 us -> 27.9 us  [to_team(): return lax.all_to_all(pieces, TEAM, split_axis=0, concat_axis=0, tiled=True)]
    all_to_all x1, blocking collectives: 50.8 us -> 15.3 us  [to_team(): return lax.all_to_all(pieces, TEAM, split_axis=0, concat_axis=0, tiled=True)]
    pallas_call x12 -> x14, Pallas kernels: 40.6 us -> 49.4 us  [outer(): pl.pallas_call(outer_kernel, out_shape=jax.ShapeDtypeStruct((count * bloc...]
    unnamed x115 -> x107, local copies, waits for them, and re-layouts: 21 us -> 16.1 us
    all_to_all x13 -> x11, starting transfers between devices: 56 us -> 51.8 us  [to_team(): return lax.all_to_all(pieces, TEAM, split_axis=0, concat_axis=0, tiled=True)]
    ppermute x42 -> x46, starting transfers between devices: 36.4 us -> 40.2 us  [swap(): return lax.ppermute(block, axes, [(i, i ^ distance) for i in range(size)])]
  transfers between devices with their start and end apart: 59 -> 60, of which waited for: 25 -> 30; matrix products, arithmetic and copies ran while one was open for 8% -> 5% of each run, Pallas kernels for 17% -> 16%
where the time goes in v2:
time: 668 us; the launch traced here: 658 us
  waiting for transfers between devices  308 us (46%)
  Pallas kernels  165 us (25%)
  starting transfers between devices  92.3 us (14%)
  local copies, waits for them, and re-layouts  37.7 us (6%)
  other arithmetic  22.2 us (3%)
  between operations  17.7 us (3%)
  blocking collectives  15.3 us (2%)
    ppermute x46, waiting for transfers between devices, swap(): return lax.ppermute(block, axes, [(i, i ^ distance) for i in range(size)])  275 us
    pallas_call x14, Pallas kernels, call(): pl.pallas_call(kernel, out_shape=tuple((jax.ShapeDtypeStruct(s, d) for s,...  86.2 us
    all_to_all x11, starting transfers between devices, to_team(): return lax.all_to_all(pieces, TEAM, split_axis=0, concat_axis=0, tiled=True)  51.8 us
    pallas_call x14, Pallas kernels, outer(): pl.pallas_call(outer_kernel, out_shape=jax.ShapeDtypeStruct((count * bloc...  49.4 us
    ppermute x46, starting transfers between devices, swap(): return lax.ppermute(block, axes, [(i, i ^ distance) for i in range(size)])  40.2 us
    all_to_all x11, waiting for transfers between devices, to_team(): return lax.all_to_all(pieces, TEAM, split_axis=0, concat_axis=0, tiled=True)  27.9 us
    pallas_call x1, Pallas kernels, attention_backward(): pl.pallas_call(functools.partial(backward_kernel, docs, sizes, run, len(k...  18.1 us
    unnamed x107, local copies, waits for them, and re-layouts  16.1 us
  transfers between devices with their start and end apart: 60, of which 30 were waited for; matrix products, arithmetic and copies ran while one was open for 5% of the time, Pallas kernels for 16%

profile of v2, /device:TPU:0, one launch (start us, length us, event | category | flops | bytes accessed | tf_op | source)
XLA Modules:
  0.0 658.3 jit_solution(14651826134683255794)
XLA Ops:
  12.8 5.4 all-to-all-start
  22.8 13.3 %all-to-all-done = bf16[4,64,2816]{2,1,0:T(8,128)(2,1)S(1)} async-done(((bf16[4,64,2816]{2,1,0:T(8,128)(2,1)}), bf16[4,64,2816]{2,1,0:T(8,128)(2,1)S(1)}, u32[]{:S(2)}, u32[]{:S(2)}) %all-to-all-start) | async-done | bytes 1441824 | tf_op jit(solution)/shard_map/all_to_all | solution.py:682
  36.0 3.6 all-to-all-start.1
  51.0 20.7 %collective-permute-done.refs_1_ = bf16[256,896]{1,0:T(8,128)(2,1)} collective-permute-done((bf16[256,896]{1,0:T(8,128)(2,1)}, bf16[256,896]{1,0:T(8,128)(2,1)}, u32[]{:S(2)}, u32[]{:S(2)}) %collective-permute-start) | collective-permute-done | bytes 458784 | tf_op jit(solution)/shard_map/ppermute | solution.py:661
  76.2 10.6 %collective-permute-done.2.refs_3_ = bf16[256,896]{1,0:T(8,128)(2,1)} collective-permute-done((bf16[256,896]{1,0:T(8,128)(2,1)}, bf16[256,896]{1,0:T(8,128)(2,1)}, u32[]{:S(2)}, u32[]{:S(2)}) %collective-permute-start.2) | collective-permute-done | bytes 458784 | tf_op jit(solution)/shard_map/ppermute | solution.py:661
  90.4 7.5 %project.1 = (bf16[512,2048]{1,0:T(8,128)(2,1)}, f32[512,1]{1,0:T(8,128)}, f32[512,512]{1,0:T(8,128)}, bf16[512,256]{1,0:T(8,128)(2,1)}, f32[8,2048]{1,0:T(8,128)}) custom-call(bf16[512,2048]{1,0:T(8,128)(2,1)} %bitcast.77, f32[512,128]{1,0:T(8,128)} %pad_maximum_fusion.4.cosine, f32[512,128]{1,0:T(8,128)} %pad_maximum_fusion.5.sine, ...), custom_call_target="tpu_custom_call" | custom-call | flops 1879048192 | bytes 6291456 | tf_op jit(solution)/shard_map/project/pallas_call | solution.py:314
  98.0 5.9 all-to-all-start.2
  112.7 17.7 %collective-permute-done.7.refs_1_ = bf16[512,256]{1,0:T(8,128)(2,1)S(1)} collective-permute-done((bf16[512,256]{1,0:T(8,128)(2,1)S(1)}, bf16[512,256]{1,0:T(8,128)(2,1)S(1)}, u32[]{:S(2)}, u32[]{:S(2)}) %collective-permute-start.7) | collective-permute-done | bytes 262176 | tf_op jit(solution)/shard_map/ppermute | solution.py:661
  132.7 6.3 collective-permute-done.9.refs_3_
  139.6 3.6 all-to-all-start.3
  143.3 3.5 collective-permute-start.14
  152.0 11.7 %attention_forward.1 = (bf16[512,512]{1,0:T(8,128)(2,1)}, bf16[512,512]{1,0:T(8,128)(2,1)}, f32[4,512]{1,0:T(4,128)}) custom-call(s32[10]{0:T(128)} %concatenate.46.meta, f32[512,512]{1,0:T(8,128)} %get-tuple-element.162.q, f32[512,128]{1,0:T(8,128)} %pad_maximum_fusion.4.cosine, f32[512,128]{1,0:T(8,128)} %pad_maximum_fusion.5.sine, s32[1,512]{1,0:T(1,128)} %fusion.28.qpos, ...), custom_call_target="tpu_custom_call" | custom-call | flops 2147483648 | bytes 4194304 | tf_op jit(solution)/shard_map/attention_forward/pallas_call | solution.py:259
  163.7 42.3 %collective-permute-done.14.refs_1_ = bf16[256,1408]{1,0:T(8,128)(2,1)S(1)} collective-permute-done((bf16[256,1408]{1,0:T(8,128)(2,1)S(1)}, bf16[256,1408]{1,0:T(8,128)(2,1)S(1)}, u32[]{:S(2)}, u32[]{:S(2)}) %collective-permute-start.14) | collective-permute-done | bytes 720928 | tf_op jit(solution)/shard_map/ppermute | solution.py:661
  206.9 5.0 all-gather.5.cloned.1.call-done.gate_rows
  211.8 5.3 proj.1
  217.1 3.6 all-to-all-start.4
  227.4 32.1 %collective-permute-done.17.refs_9_ = bf16[256,1408]{1,0:T(8,128)(2,1)S(1)} collective-permute-done((bf16[256,1408]{1,0:T(8,128)(2,1)S(1)}, bf16[256,1408]{1,0:T(8,128)(2,1)S(1)}, u32[]{:S(2)}, u32[]{:S(2)}) %collective-permute-start.17) | collective-permute-done | bytes 720928 | tf_op jit(solution)/shard_map/ppermute | solution.py:661
  263.1 3.9 middle.1
  267.0 6.8 %all-to-all-start.5 = ((bf16[4,128,2048]{2,1,0:T(8,128)(2,1)}), bf16[4,128,2048]{2,1,0:T(8,128)(2,1)S(1)}, u32[]{:S(2)}, u32[]{:S(2)}) async-start(bf16[4,128,2048]{2,1,0:T(8,128)(2,1)} %get-tuple-element.194), calls=%async_computation.5 | async-start | bytes 4194304 | tf_op jit(solution)/shard_map/all_to_all | solution.py:682
  276.1 14.9 %collective-permute-done.23.refs_11_ = bf16[256,1408]{1,0:T(8,128)(2,1)S(1)} collective-permute-done((bf16[256,1408]{1,0:T(8,128)(2,1)}, bf16[256,1408]{1,0:T(8,128)(2,1)S(1)}, u32[]{:S(2)}, u32[]{:S(2)}) %collective-permute-start.23) | collective-permute-done | bytes 720928 | tf_op jit(solution)/shard_map/ppermute | solution.py:661
  299.4 32.4 %mlp.1 = (bf16[512,1408]{1,0:T(8,128)(2,1)}, bf16[512,1408]{1,0:T(8,128)(2,1)}, bf16[512,1408]{1,0:T(8,128)(2,1)}, bf16[512,2048]{1,0:T(8,128)(2,1)}, bf16[512,2048]{1,0:T(8,128)(2,1)}) custom-call(s32[10]{0:T(128)} %concatenate.46.meta, bf16[512,2048]{1,0:T(8,128)(2,1)} %bitcast.62, bf16[512,2048]{1,0:T(8,128)(2,1)} %bitcast.67, ...), custom_call_target="tpu_custom_call" | custom-call | flops 17716740096 | bytes 21495848 | tf_op jit(solution)/shard_map/mlp/pallas_call | solution.py:314
  331.8 4.7 all-to-all-start.6
  336.6 4.3 outer.14
  341.0 4.3 outer.18
  345.8 4.3 outer.16
  351.7 5.9 outer.15
  357.6 4.4 all-to-all-done.6.parts
  362.0 4.9 middle_grad.1
  366.9 4.5 all-to-all-start.7
  374.6 5.9 outer.19
  383.3 6.0 outer.17
  389.4 44.5 %collective-permute-done.30 = bf16[512,1408]{1,0:T(8,128)(2,1)S(1)} collective-permute-done((bf16[512,1408]{1,0:T(8,128)(2,1)S(1)}, bf16[512,1408]{1,0:T(8,128)(2,1)S(1)}, u32[]{:S(2)}, u32[]{:S(2)}) %collective-permute-start.30) | collective-permute-done | bytes 1441824 | tf_op jit(solution)/shard_map/ppermute | solution.py:661
  435.3 4.7 all-to-all-start.8
  443.3 18.1 %attention_backward.1 = (bf16[512,512]{1,0:T(8,128)(2,1)}, bf16[4096,256]{1,0:T(8,128)(2,1)}) custom-call(s32[10]{0:T(128)} %concatenate.46.meta, bf16[512,512]{1,0:T(8,128)(2,1)} %get-tuple-element.179.q, bf16[512,512]{1,0:T(8,128)(2,1)} %get-tuple-element.245.attn.o.right, bf16[512,2048]{1,0:T(8,128)(2,1)} %bitcast.18.g_proj.left, ...), custom_call_target="tpu_custom_call" | custom-call | flops 5368709120 | bytes 6291456 | tf_op jit(solution)/shard_map/attention_backward/pallas_call | solution.py:288
  461.4 11.9 %collective-permute-done.31 = bf16[256,1408]{1,0:T(8,128)(2,1)} collective-permute-done((bf16[256,1408]{1,0:T(8,128)(2,1)}, bf16[256,1408]{1,0:T(8,128)(2,1)}, u32[]{:S(2)}, u32[]{:S(2)}) %collective-permute-start.31) | collective-permute-done | bytes 720928 | tf_op jit(solution)/shard_map/ppermute | solution.py:661
  476.8 5.3 all-to-all-done.8.parts
  486.2 3.5 outer.23
  500.2 3.5 outer.21
  505.7 8.5 %collective-permute-done.35 = bf16[512,256]{1,0:T(8,128)(2,1)S(1)} collective-permute-done((bf16[512,256]{1,0:T(8,128)(2,1)S(1)}, bf16[512,256]{1,0:T(8,128)(2,1)S(1)}, u32[]{:S(2)}, u32[]{:S(2)}) %collective-permute-start.35) | collective-permute-done | bytes 262176 | tf_op jit(solution)/shard_map/ppermute | solution.py:661
  514.2 6.2 collective-permute-done.37
  521.7 9.2 %qkv_grad.1 = (bf16[512,2048]{1,0:T(8,128)(2,1)}, bf16[512,2048]{1,0:T(8,128)(2,1)}) custom-call(bf16[512,512]{1,0:T(8,128)(2,1)} %get-tuple-element.243.right.grad_q, bf16[512,256]{1,0:T(8,128)(2,1)} %pad_maximum_fusion.6.grad_kv.right, bf16[512,2048]{1,0:T(8,128)(2,1)} %bitcast.78, f32[512,1]{1,0:T(8,128)} %get-tuple-element.250.scale, ...), custom_call_target="tpu_custom_call" | custom-call | flops 1879048192 | bytes 6555648 | tf_op jit(solution)/shard_map/qkv_grad/pallas_call | solution.py:314
  530.9 4.6 all-to-all-start.9
  546.8 27.3 %collective-permute-done.41 = bf16[256,1408]{1,0:T(8,128)(2,1)S(1)} collective-permute-done((bf16[256,1408]{1,0:T(8,128)(2,1)S(1)}, bf16[256,1408]{1,0:T(8,128)(2,1)S(1)}, u32[]{:S(2)}, u32[]{:S(2)}) %collective-permute-start.41) | collective-permute-done | bytes 720928 | tf_op jit(solution)/shard_map/ppermute | solution.py:661
  578.2 4.3 all-to-all-start.10
  591.4 3.4 output.1.array
  596.8 3.9 token_grad.1.array
  603.0 19.5 %collective-permute-done.43 = bf16[256,384]{1,0:T(8,128)(2,1)S(1)} collective-permute-done((bf16[256,384]{1,0:T(8,128)(2,1)S(1)}, bf16[256,384]{1,0:T(8,128)(2,1)S(1)}, u32[]{:S(2)}, u32[]{:S(2)}) %collective-permute-start.43) | collective-permute-done | bytes 196640 | tf_op jit(solution)/shard_map/ppermute | solution.py:661
  632.1 15.3 %all_to_all.60 = bf16[4,64,1408]{2,1,0:T(8,128)(2,1)S(1)} all-to-all(bf16[4,64,1408]{2,1,0:T(8,128)(2,1)S(1)} %bitcast.76), channel_id=1, replica_groups=mesh['far'=2,'x'=2,'core'=2,'zh'=2,'zl'=2] {'x','zl'}, dimensions={0} | all-to-all | bytes 1441792 | tf_op jit(solution)/shard_map/all_to_all | solution.py:682
  (291 shorter events, 141.6 us)
Async XLA Ops:
  12.8 23.2 %all-to-all-start = ((bf16[4,64,2816]{2,1,0:T(8,128)(2,1)}), bf16[4,64,2816]{2,1,0:T(8,128)(2,1)S(1)}, u32[]{:S(2)}, u32[]{:S(2)}) async-start(bf16[4,64,2816]{2,1,0:T(8,128)(2,1)} %pack.2), calls=%async_computation | async-start | bytes 2883584 | tf_op jit(solution)/shard_map/all_to_all | solution.py:682
  36.0 37.8 %all-to-all-start.1 = ((bf16[4,128,2048]{2,1,0:T(8,128)(2,1)}), bf16[4,128,2048]{2,1,0:T(8,128)(2,1)S(1)}, u32[]{:S(2)}, u32[]{:S(2)}) async-start(bf16[4,128,2048]{2,1,0:T(8,128)(2,1)} %get-tuple-element.143), calls=%async_computation.1 | async-start | bytes 4194304 | tf_op jit(solution)/shard_map/all_to_all | solution.py:682
  39.7 99.3 %all-gather.3.cloned.1.call-start = ((), (), s32[]{:S(2)}) async-start(), calls=%async_computation.13 | async-start | bytes 2359296 | tf_op jit(solution)/shard_map/all_gather | solution.py:735
  40.5 31.2 %collective-permute-start = (bf16[256,896]{1,0:T(8,128)(2,1)}, bf16[256,896]{1,0:T(8,128)(2,1)}, u32[]{:S(2)}, u32[]{:S(2)}) collective-permute-start(bf16[256,896]{1,0:T(8,128)(2,1)} %slice.206.refs_0_), channel_id=1, source_target_pairs={{0,2},{2,0},{1,3},{3,1},{4,6},{6,4},{5,7},{7,5},{8,10},{10,8},{9,1... | collective-permute-start | bytes 1376264 | tf_op jit(solution)/shard_map/ppermute | solution.py:661
  43.1 28.6 %collective-permute-start.1 = (bf16[256,896]{1,0:T(8,128)(2,1)}, bf16[256,896]{1,0:T(8,128)(2,1)}, u32[]{:S(2)}, u32[]{:S(2)}) collective-permute-start(bf16[256,896]{1,0:T(8,128)(2,1)} %slice.206.refs_0_), channel_id=1, source_target_pairs={{0,16},{16,0},{1,17},{17,1},{2,18},{18,2},{3,19},{19,3},{4,20},{20... | collective-permute-start | bytes 1376264 | tf_op jit(solution)/shard_map/ppermute | solution.py:661
  73.9 138.0 %all-gather.5.cloned.1.call-start = ((), (), s32[]{:S(2)}) async-start(), calls=%async_computation.14 | async-start | bytes 6488064 | tf_op jit(solution)/shard_map/all_gather | solution.py:735
  73.9 12.9 %collective-permute-start.2 = (bf16[256,896]{1,0:T(8,128)(2,1)}, bf16[256,896]{1,0:T(8,128)(2,1)}, u32[]{:S(2)}, u32[]{:S(2)}) collective-permute-start(bf16[256,896]{1,0:T(8,128)(2,1)} %collective-permute-done.refs_1_), channel_id=1, source_target_pairs={{0,16},{16,0},{1,17},{17,1},{2,18},{18,2},{3,19},{19,3},{4,20},{20... | collective-permute-start | bytes 1376264 | tf_op jit(solution)/shard_map/ppermute | solution.py:661
  75.5 14.9 %collective-permute-start.4 = (bf16[256,896]{1,0:T(8,128)(2,1)}, bf16[256,896]{1,0:T(8,128)(2,1)}, u32[]{:S(2)}, u32[]{:S(2)}) collective-permute-start(bf16[256,896]{1,0:T(8,128)(2,1)} %collective-permute-done.refs_1_), channel_id=1, source_target_pairs={{0,4},{4,0},{1,5},{5,1},{2,6},{6,2},{3,7},{7,3},{8,12},{12,8},{9,1... | collective-permute-start | bytes 1376264 | tf_op jit(solution)/shard_map/ppermute | solution.py:661
  75.6 14.8 %collective-permute-start.3 = (bf16[256,896]{1,0:T(8,128)(2,1)}, bf16[256,896]{1,0:T(8,128)(2,1)}, u32[]{:S(2)}, u32[]{:S(2)}) collective-permute-start(bf16[256,896]{1,0:T(8,128)(2,1)} %slice.206.refs_0_), channel_id=1, source_target_pairs={{0,4},{4,0},{1,5},{5,1},{2,6},{6,2},{3,7},{7,3},{8,12},{12,8},{9,1... | collective-permute-start | bytes 1376264 | tf_op jit(solution)/shard_map/ppermute | solution.py:661
  76.1 14.3 %collective-permute-start.5 = (bf16[256,896]{1,0:T(8,128)(2,1)}, bf16[256,896]{1,0:T(8,128)(2,1)}, u32[]{:S(2)}, u32[]{:S(2)}) collective-permute-start(bf16[256,896]{1,0:T(8,128)(2,1)} %collective-permute-done.1.refs_2_), channel_id=1, source_target_pairs={{0,4},{4,0},{1,5},{5,1},{2,6},{6,2},{3,7},{7,3},{8,12},{12,8},{9,1... | collective-permute-start | bytes 1376264 | tf_op jit(solution)/shard_map/ppermute | solution.py:661
  98.0 34.5 %all-to-all-start.2 = ((bf16[4,64,2816]{2,1,0:T(8,128)(2,1)}), bf16[4,64,2816]{2,1,0:T(8,128)(2,1)S(1)}, u32[]{:S(2)}, u32[]{:S(2)}) async-start(bf16[4,64,2816]{2,1,0:T(8,128)(2,1)} %pack.3), calls=%async_computation.2 | async-start | bytes 2883584 | tf_op jit(solution)/shard_map/all_to_all | solution.py:682
  105.3 25.1 %collective-permute-start.7 = (bf16[512,256]{1,0:T(8,128)(2,1)S(1)}, bf16[512,256]{1,0:T(8,128)(2,1)S(1)}, u32[]{:S(2)}, u32[]{:S(2)}) collective-permute-start(bf16[512,256]{1,0:T(8,128)(2,1)S(1)} %copy-done.43), channel_id=1, source_target_pairs={{0,2},{2,0},{1,3},{3,1},{4,6},{6,4},{5,7},{7,5},{8,10},{10,8},{9,1... | collective-permute-start | bytes 786440 | tf_op jit(solution)/shard_map/ppermute | solution.py:661
  105.3 25.1 %collective-permute-start.8 = (bf16[512,256]{1,0:T(8,128)(2,1)S(1)}, bf16[512,256]{1,0:T(8,128)(2,1)S(1)}, u32[]{:S(2)}, u32[]{:S(2)}) collective-permute-start(bf16[512,256]{1,0:T(8,128)(2,1)S(1)} %copy-done.43), channel_id=1, source_target_pairs={{0,16},{16,0},{1,17},{17,1},{2,18},{18,2},{3,19},{19,3},{4,20},{20... | collective-permute-start | bytes 786440 | tf_op jit(solution)/shard_map/ppermute | solution.py:661
  139.6 67.2 %all-to-all-start.3 = ((bf16[4,128,2048]{2,1,0:T(8,128)(2,1)}), bf16[4,128,2048]{2,1,0:T(8,128)(2,1)S(1)}, u32[]{:S(2)}, u32[]{:S(2)}) async-start(bf16[4,128,2048]{2,1,0:T(8,128)(2,1)} %get-tuple-element.183), calls=%async_computation.3 | async-start | bytes 4194304 | tf_op jit(solution)/shard_map/all_to_all | solution.py:682
  143.3 62.7 %collective-permute-start.14 = (bf16[256,1408]{1,0:T(8,128)(2,1)S(1)}, bf16[256,1408]{1,0:T(8,128)(2,1)S(1)}, u32[]{:S(2)}, u32[]{:S(2)}) collective-permute-start(bf16[256,1408]{1,0:T(8,128)(2,1)S(1)} %get-tuple-element.205.refs_0_), channel_id=1, source_target_pairs={{0,2},{2,0},{1,3},{3,1},{4,6},{6,4},{5,7},{7,5},{8,10},{10,8},{9,1... | collective-permute-start | bytes 2162696 | tf_op jit(solution)/shard_map/ppermute | solution.py:661
  146.9 60.0 %collective-permute-start.15 = (bf16[256,1408]{1,0:T(8,128)(2,1)S(1)}, bf16[256,1408]{1,0:T(8,128)(2,1)}, u32[]{:S(2)}, u32[]{:S(2)}) collective-permute-start(bf16[256,1408]{1,0:T(8,128)(2,1)S(1)} %get-tuple-element.205.refs_0_), channel_id=1, source_target_pairs={{0,16},{16,0},{1,17},{17,1},{2,18},{18,2},{3,19},{19,3},{4,20},{20... | collective-permute-start | bytes 2162696 | tf_op jit(solution)/shard_map/ppermute | solution.py:661
  217.1 44.6 %all-to-all-start.4 = ((bf16[4,128,2048]{2,1,0:T(8,128)(2,1)}), bf16[4,128,2048]{2,1,0:T(8,128)(2,1)S(1)}, u32[]{:S(2)}, u32[]{:S(2)}) async-start(bf16[4,128,2048]{2,1,0:T(8,128)(2,1)} %bitcast.71), calls=%async_computation.4 | async-start | bytes 4194304 | tf_op jit(solution)/shard_map/all_to_all | solution.py:682
  220.7 38.8 %collective-permute-start.17 = (bf16[256,1408]{1,0:T(8,128)(2,1)S(1)}, bf16[256,1408]{1,0:T(8,128)(2,1)S(1)}, u32[]{:S(2)}, u32[]{:S(2)}) collective-permute-start(bf16[256,1408]{1,0:T(8,128)(2,1)S(1)} %get-tuple-element.213.refs_8_), channel_id=1, source_target_pairs={{0,2},{2,0},{1,3},{3,1},{4,6},{6,4},{5,7},{7,5},{8,10},{10,8},{9,1... | collective-permute-start | bytes 2162696 | tf_op jit(solution)/shard_map/ppermute | solution.py:661
  223.9 35.7 %collective-permute-start.18 = (bf16[256,1408]{1,0:T(8,128)(2,1)S(1)}, bf16[256,1408]{1,0:T(8,128)(2,1)S(1)}, u32[]{:S(2)}, u32[]{:S(2)}) collective-permute-start(bf16[256,1408]{1,0:T(8,128)(2,1)S(1)} %get-tuple-element.213.refs_8_), channel_id=1, source_target_pairs={{0,16},{16,0},{1,17},{17,1},{2,18},{18,2},{3,19},{19,3},{4,20},{20... | collective-permute-start | bytes 2162696 | tf_op jit(solution)/shard_map/ppermute | solution.py:661
  225.1 36.2 %collective-permute-start.16 = (bf16[256,1408]{1,0:T(8,128)(2,1)}, bf16[256,1408]{1,0:T(8,128)(2,1)}, u32[]{:S(2)}, u32[]{:S(2)}) collective-permute-start(bf16[256,1408]{1,0:T(8,128)(2,1)} %copy-done.32), channel_id=1, source_target_pairs={{0,16},{16,0},{1,17},{17,1},{2,18},{18,2},{3,19},{19,3},{4,20},{20... | collective-permute-start | bytes 2162696 | tf_op jit(solution)/shard_map/ppermute | solution.py:661
  267.0 31.0 %all-to-all-start.5 = ((bf16[4,128,2048]{2,1,0:T(8,128)(2,1)}), bf16[4,128,2048]{2,1,0:T(8,128)(2,1)S(1)}, u32[]{:S(2)}, u32[]{:S(2)}) async-start(bf16[4,128,2048]{2,1,0:T(8,128)(2,1)} %get-tuple-element.194), calls=%async_computation.5 | async-start | bytes 4194304 | tf_op jit(solution)/shard_map/all_to_all | solution.py:682
  273.8 17.1 %collective-permute-start.23 = (bf16[256,1408]{1,0:T(8,128)(2,1)}, bf16[256,1408]{1,0:T(8,128)(2,1)S(1)}, u32[]{:S(2)}, u32[]{:S(2)}) collective-permute-start(bf16[256,1408]{1,0:T(8,128)(2,1)} %copy-done.33), channel_id=1, source_target_pairs={{0,16},{16,0},{1,17},{17,1},{2,18},{18,2},{3,19},{19,3},{4,20},{20... | collective-permute-start | bytes 2162696 | tf_op jit(solution)/shard_map/ppermute | solution.py:661
  275.1 15.9 %collective-permute-start.19 = (bf16[256,1408]{1,0:T(8,128)(2,1)S(1)}, bf16[256,1408]{1,0:T(8,128)(2,1)S(1)}, u32[]{:S(2)}, u32[]{:S(2)}) collective-permute-start(bf16[256,1408]{1,0:T(8,128)(2,1)S(1)} %get-tuple-element.205.refs_0_), channel_id=1, source_target_pairs={{0,4},{4,0},{1,5},{5,1},{2,6},{6,2},{3,7},{7,3},{8,12},{12,8},{9,1... | collective-permute-start | bytes 2162696 | tf_op jit(solution)/shard_map/ppermute | solution.py:661
  275.1 16.5 %collective-permute-start.20 = (bf16[256,1408]{1,0:T(8,128)(2,1)}, bf16[256,1408]{1,0:T(8,128)(2,1)S(1)}, u32[]{:S(2)}, u32[]{:S(2)}) collective-permute-start(bf16[256,1408]{1,0:T(8,128)(2,1)} %copy-done.32), channel_id=1, source_target_pairs={{0,4},{4,0},{1,5},{5,1},{2,6},{6,2},{3,7},{7,3},{8,12},{12,8},{9,1... | collective-permute-start | bytes 2162696 | tf_op jit(solution)/shard_map/ppermute | solution.py:661
  275.6 16.1 %collective-permute-start.21 = (bf16[256,1408]{1,0:T(8,128)(2,1)}, bf16[256,1408]{1,0:T(8,128)(2,1)S(1)}, u32[]{:S(2)}, u32[]{:S(2)}) collective-permute-start(bf16[256,1408]{1,0:T(8,128)(2,1)} %collective-permute-done.15.refs_2_), channel_id=1, source_target_pairs={{0,4},{4,0},{1,5},{5,1},{2,6},{6,2},{3,7},{7,3},{8,12},{12,8},{9,1... | collective-permute-start | bytes 2162696 | tf_op jit(solution)/shard_map/ppermute | solution.py:661
  275.6 20.5 %collective-permute-start.25 = (bf16[256,1408]{1,0:T(8,128)(2,1)}, bf16[256,1408]{1,0:T(8,128)(2,1)S(1)}, u32[]{:S(2)}, u32[]{:S(2)}) collective-permute-start(bf16[256,1408]{1,0:T(8,128)(2,1)} %copy-done.33), channel_id=1, source_target_pairs={{0,4},{4,0},{1,5},{5,1},{2,6},{6,2},{3,7},{7,3},{8,12},{12,8},{9,1... | collective-permute-start | bytes 2162696 | tf_op jit(solution)/shard_map/ppermute | solution.py:661
  331.8 30.1 %all-to-all-start.6 = ((bf16[4,128,2048]{2,1,0:T(8,128)(2,1)}), bf16[4,128,2048]{2,1,0:T(8,128)(2,1)}, u32[]{:S(2)}, u32[]{:S(2)}) async-start(bf16[4,128,2048]{2,1,0:T(8,128)(2,1)} %bitcast.81), calls=%async_computation.6 | async-start | bytes 4194304 | tf_op jit(solution)/shard_map/all_to_all | solution.py:682
  345.3 26.4 %collective-permute-start.33 = (bf16[1024,1408]{1,0:T(8,128)(2,1)}, bf16[1024,1408]{1,0:T(8,128)(2,1)}, u32[]{:S(2)}, u32[]{:S(2)}) collective-permute-start(bf16[1024,1408]{1,0:T(8,128)(2,1)} %outer.18), channel_id=1, source_target_pairs={{0,4},{4,0},{1,5},{5,1},{2,6},{6,2},{3,7},{7,3},{8,12},{12,8},{9,1... | collective-permute-start | bytes 8650760 | tf_op jit(solution)/shard_map/ppermute | solution.py:661
  350.1 33.2 %collective-permute-start.29 = (bf16[1024,1408]{1,0:T(8,128)(2,1)}, bf16[1024,1408]{1,0:T(8,128)(2,1)}, u32[]{:S(2)}, u32[]{:S(2)}) collective-permute-start(bf16[1024,1408]{1,0:T(8,128)(2,1)} %outer.16), channel_id=1, source_target_pairs={{0,4},{4,0},{1,5},{5,1},{2,6},{6,2},{3,7},{7,3},{8,12},{12,8},{9,1... | collective-permute-start | bytes 8650760 | tf_op jit(solution)/shard_map/ppermute | solution.py:661
  366.9 68.4 %all-to-all-start.7 = ((bf16[4,128,2048]{2,1,0:T(8,128)(2,1)}), bf16[4,128,2048]{2,1,0:T(8,128)(2,1)}, u32[]{:S(2)}, u32[]{:S(2)}) async-start(bf16[4,128,2048]{2,1,0:T(8,128)(2,1)} %get-tuple-element.226), calls=%async_computation.7 | async-start | bytes 4194304 | tf_op jit(solution)/shard_map/all_to_all | solution.py:682
  371.4 105.5 %reduce-scatter.2.cloned.1.call-start = ((), (), s32[]{:S(2)}) async-start(), calls=%async_computation.15 | async-start | bytes 3604480 | tf_op jit(solution)/shard_map/reduce_scatter | solution.py:739
  382.0 51.9 %collective-permute-start.30 = (bf16[512,1408]{1,0:T(8,128)(2,1)S(1)}, bf16[512,1408]{1,0:T(8,128)(2,1)S(1)}, u32[]{:S(2)}, u32[]{:S(2)}) collective-permute-start(bf16[512,1408]{1,0:T(8,128)(2,1)S(1)} %slice.167), channel_id=1, source_target_pairs={{0,16},{16,0},{1,17},{17,1},{2,18},{18,2},{3,19},{19,3},{4,20},{20... | collective-permute-start | bytes 4325384 | tf_op jit(solution)/shard_map/ppermute | solution.py:661
  435.3 46.8 %all-to-all-start.8 = ((bf16[4,128,2048]{2,1,0:T(8,128)(2,1)}), bf16[4,128,2048]{2,1,0:T(8,128)(2,1)}, u32[]{:S(2)}, u32[]{:S(2)}) async-start(bf16[4,128,2048]{2,1,0:T(8,128)(2,1)} %bitcast.79), calls=%async_computation.8 | async-start | bytes 4194304 | tf_op jit(solution)/shard_map/all_to_all | solution.py:682
  440.2 35.2 %collective-permute-start.32 = (bf16[512,1408]{1,0:T(8,128)(2,1)S(1)}, bf16[512,1408]{1,0:T(8,128)(2,1)S(1)}, u32[]{:S(2)}, u32[]{:S(2)}) collective-permute-start(bf16[512,1408]{1,0:T(8,128)(2,1)S(1)} %slice.171), channel_id=1, source_target_pairs={{0,16},{16,0},{1,17},{17,1},{2,18},{18,2},{3,19},{19,3},{4,20},{20... | collective-permute-start | bytes 4325384 | tf_op jit(solution)/shard_map/ppermute | solution.py:661
  443.3 29.9 %collective-permute-start.31 = (bf16[256,1408]{1,0:T(8,128)(2,1)}, bf16[256,1408]{1,0:T(8,128)(2,1)}, u32[]{:S(2)}, u32[]{:S(2)}) collective-permute-start(bf16[256,1408]{1,0:T(8,128)(2,1)} %slice.169), channel_id=1, source_target_pairs={{0,2},{2,0},{1,3},{3,1},{4,6},{6,4},{5,7},{7,5},{8,10},{10,8},{9,1... | collective-permute-start | bytes 2162696 | tf_op jit(solution)/shard_map/ppermute | solution.py:661
  492.0 11.6 %collective-permute-start.38 = (bf16[1024,1024]{1,0:T(8,128)(2,1)S(1)}, bf16[1024,1024]{1,0:T(8,128)(2,1)S(1)}, u32[]{:S(2)}, u32[]{:S(2)}) collective-permute-start(bf16[1024,1024]{1,0:T(8,128)(2,1)S(1)} %pad_maximum_fusion.1), channel_id=1, source_target_pairs={{0,4},{4,0},{1,5},{5,1},{2,6},{6,2},{3,7},{7,3},{8,12},{12,8},{9,1... | collective-permute-start | bytes 6291464 | tf_op jit(solution)/shard_map/ppermute | solution.py:661
  493.6 20.6 %collective-permute-start.35 = (bf16[512,256]{1,0:T(8,128)(2,1)S(1)}, bf16[512,256]{1,0:T(8,128)(2,1)S(1)}, u32[]{:S(2)}, u32[]{:S(2)}) collective-permute-start(bf16[512,256]{1,0:T(8,128)(2,1)S(1)} %get-tuple-element.282), channel_id=1, source_target_pairs={{0,2},{2,0},{16,18},{18,16},{1,3},{3,1},{17,19},{19,17},{4,6},{6,4... | collective-permute-start | bytes 786440 | tf_op jit(solution)/shard_map/ppermute | solution.py:661
  493.7 20.5 %collective-permute-start.36 = (bf16[512,256]{1,0:T(8,128)(2,1)S(1)}, bf16[512,256]{1,0:T(8,128)(2,1)S(1)}, u32[]{:S(2)}, u32[]{:S(2)}) collective-permute-start(bf16[512,256]{1,0:T(8,128)(2,1)S(1)} %get-tuple-element.281), channel_id=1, source_target_pairs={{0,16},{2,18},{16,0},{18,2},{1,17},{3,19},{17,1},{19,3},{4,20},{6,... | collective-permute-start | bytes 786440 | tf_op jit(solution)/shard_map/ppermute | solution.py:661
  495.7 24.8 %collective-permute-start.37 = (bf16[512,256]{1,0:T(8,128)(2,1)S(1)}, bf16[512,256]{1,0:T(8,128)(2,1)S(1)}, u32[]{:S(2)}, u32[]{:S(2)}) collective-permute-start(bf16[512,256]{1,0:T(8,128)(2,1)S(1)} %get-tuple-element.280), channel_id=1, source_target_pairs={{0,18},{2,16},{16,2},{18,0},{1,19},{3,17},{17,3},{19,1},{4,22},{6,... | collective-permute-start | bytes 786440 | tf_op jit(solution)/shard_map/ppermute | solution.py:661
  530.9 45.5 %all-to-all-start.9 = ((bf16[4,128,2048]{2,1,0:T(8,128)(2,1)}), bf16[4,128,2048]{2,1,0:T(8,128)(2,1)}, u32[]{:S(2)}, u32[]{:S(2)}) async-start(bf16[4,128,2048]{2,1,0:T(8,128)(2,1)} %bitcast.80), calls=%async_computation.10 | async-start | bytes 4194304 | tf_op jit(solution)/shard_map/all_to_all | solution.py:682
  535.9 38.1 %collective-permute-start.41 = (bf16[256,1408]{1,0:T(8,128)(2,1)S(1)}, bf16[256,1408]{1,0:T(8,128)(2,1)S(1)}, u32[]{:S(2)}, u32[]{:S(2)}) collective-permute-start(bf16[256,1408]{1,0:T(8,128)(2,1)S(1)} %slice.185), channel_id=1, source_target_pairs={{0,2},{2,0},{1,3},{3,1},{4,6},{6,4},{5,7},{7,5},{8,10},{10,8},{9,1... | collective-permute-start | bytes 2162696 | tf_op jit(solution)/shard_map/ppermute | solution.py:661
  542.0 32.3 %collective-permute-start.39 = (bf16[1024,384]{1,0:T(8,128)(2,1)S(1)}, bf16[1024,384]{1,0:T(8,128)(2,1)S(1)}, u32[]{:S(2)}, u32[]{:S(2)}) collective-permute-start(bf16[1024,384]{1,0:T(8,128)(2,1)S(1)} %pad_maximum_fusion.2), channel_id=1, source_target_pairs={{0,4},{4,0},{1,5},{5,1},{2,6},{6,2},{3,7},{7,3},{8,12},{12,8},{9,1... | collective-permute-start | bytes 2359304 | tf_op jit(solution)/shard_map/ppermute | solution.py:661
  542.1 33.3 %collective-permute-start.40 = (bf16[512,1024]{1,0:T(8,128)(2,1)S(1)}, bf16[512,1024]{1,0:T(8,128)(2,1)S(1)}, u32[]{:S(2)}, u32[]{:S(2)}) collective-permute-start(bf16[512,1024]{1,0:T(8,128)(2,1)S(1)} %slice.183), channel_id=1, source_target_pairs={{0,16},{16,0},{1,17},{17,1},{2,18},{18,2},{3,19},{19,3},{4,20},{20... | collective-permute-start | bytes 3145736 | tf_op jit(solution)/shard_map/ppermute | solution.py:661
  578.2 49.9 %all-to-all-start.10 = ((bf16[4,64,4224]{2,1,0:T(8,128)(2,1)}), bf16[4,64,4224]{2,1,0:T(8,128)(2,1)S(1)}, u32[]{:S(2)}, u32[]{:S(2)}) async-start(bf16[4,64,4224]{2,1,0:T(8,128)(2,1)} %bitcast.70), calls=%async_computation.11 | async-start | bytes 4325376 | tf_op jit(solution)/shard_map/all_to_all | solution.py:682
  582.5 43.6 %collective-permute-start.42 = (bf16[256,1024]{1,0:T(8,128)(2,1)S(1)}, bf16[256,1024]{1,0:T(8,128)(2,1)S(1)}, u32[]{:S(2)}, u32[]{:S(2)}) collective-permute-start(bf16[256,1024]{1,0:T(8,128)(2,1)S(1)} %slice.187), channel_id=1, source_target_pairs={{0,2},{2,0},{1,3},{3,1},{4,6},{6,4},{5,7},{7,5},{8,10},{10,8},{9,1... | collective-permute-start | bytes 1572872 | tf_op jit(solution)/shard_map/ppermute | solution.py:661
  586.5 36.1 %collective-permute-start.43 = (bf16[256,384]{1,0:T(8,128)(2,1)S(1)}, bf16[256,384]{1,0:T(8,128)(2,1)S(1)}, u32[]{:S(2)}, u32[]{:S(2)}) collective-permute-start(bf16[256,384]{1,0:T(8,128)(2,1)S(1)} %get-tuple-element.283), channel_id=1, source_target_pairs={{0,2},{2,0},{16,18},{18,16},{1,3},{3,1},{17,19},{19,17},{4,6},{6,4... | collective-permute-start | bytes 589832 | tf_op jit(solution)/shard_map/ppermute | solution.py:661
  586.8 35.7 %collective-permute-start.44 = (bf16[256,384]{1,0:T(8,128)(2,1)S(1)}, bf16[256,384]{1,0:T(8,128)(2,1)S(1)}, u32[]{:S(2)}, u32[]{:S(2)}) collective-permute-start(bf16[256,384]{1,0:T(8,128)(2,1)S(1)} %get-tuple-element.285), channel_id=1, source_target_pairs={{0,16},{2,18},{16,0},{18,2},{1,17},{3,19},{17,1},{19,3},{4,20},{6,... | collective-permute-start | bytes 589832 | tf_op jit(solution)/shard_map/ppermute | solution.py:661
  587.6 37.4 %collective-permute-start.45 = (bf16[256,384]{1,0:T(8,128)(2,1)S(1)}, bf16[256,384]{1,0:T(8,128)(2,1)S(1)}, u32[]{:S(2)}, u32[]{:S(2)}) collective-permute-start(bf16[256,384]{1,0:T(8,128)(2,1)S(1)} %get-tuple-element.284), channel_id=1, source_target_pairs={{0,18},{2,16},{16,2},{18,0},{1,19},{3,17},{17,3},{19,1},{4,22},{6,... | collective-permute-start | bytes 589832 | tf_op jit(solution)/shard_map/ppermute | solution.py:661
  (65 other events, 623.4 us)
Sparse Core Ops, SparseCore 0:
  74.0 38.3 all-gather.2
  114.8 96.9 all-gather.4
  380.7 67.1 reduce-scatter.1

commit v3 on v2

--- a/solution.py
+++ b/solution.py
@@ -505,12 +505,29 @@
     out[...] = (middle[...] + keep[...] * ffn).astype(BF)
 
 
+def load_halves(sizes, pieces, target, sems, base):
+    slots = 2 * sizes[0] * sizes[1]
+    rows = target.shape[0] // (2 * slots)
+    copies = []
+    for piece in pieces:
+        for at in range(0, piece.shape[0], rows):
+            n = len(copies)
+            place = (n % slots * 2 + n // slots) * rows
+            copy = pltpu.make_async_copy(
+                piece.at[pl.ds(at, rows), :], target.at[pl.ds(place, rows), :], sems.at[base + n]
+            )
+            copy.start()
+            copies.append(copy)
+    return copies
+
+
 def mlp_kernel(sizes, count, meta, x, g, gate_rows, *refs):
     pieces = refs[: 2 * count]
     hidden, grad_gate, grad_up, grad_x, ffn, w_g, w_u, w_d, sems = refs[2 * count :]
-    copies = load_natural(meta, sizes, gate_rows, w_g, sems, 2 * count)
-    copies += load_pieces(pieces[:count], w_u, sems, 0)
-    late = load_pieces(pieces[count:], w_d, sems, count)
+    slots = 2 * sizes[0] * sizes[1]
+    copies = load_natural(meta, sizes, gate_rows, w_g, sems, 0)
+    copies += load_halves(sizes, pieces[:count], w_u, sems, slots)
+    late = load_halves(sizes, pieces[count:], w_d, sems, 3 * slots)
     for copy in copies:
         copy.wait()
     features, width = w_g.shape
@@ -552,7 +569,7 @@
     width = w_gate.shape[1]
     count = len(w_up)
     pieces = [w_gate, *w_up, *w_down]
-    copies = 2 * count + 2 * sizes[0] * sizes[1]
+    copies = 5 * 2 * sizes[0] * sizes[1]
     return call(
         functools.partial(mlp_kernel, sizes, count),
         "mlp",
@@ -713,8 +730,8 @@
     return sum(far, [block] + near)
 
 
-def both_cores(plane):
-    if len(plane) > 4:
+def both_cores(plane, joined=False):
+    if joined or len(plane) > 4:
         plane = [jnp.concatenate(plane, axis=0)]
     return list(plane) + [swap(b, "core", 1) for b in plane]
 
@@ -871,9 +888,11 @@
     kv_plane, w_out, up_rows, down_rows = together(kv_plane, w_out, up_rows, down_rows)
     grad_ffn = to_team(after(cot_sent, up_rows))
     kv = both_cores(kv_plane)
-    up_plane = plane_first(up_rows)
+    low_rows = up_rows.shape[0] // 2
+    up_a = plane_first(up_rows[:low_rows])
     attn, query, log_total = attention_forward(meta, docs, sizes, q, tables, kv)
-    attn, grad_ffn, up_plane, w_g = together(attn, grad_ffn, up_plane, w_g)
+    attn, grad_ffn, up_a = together(attn, grad_ffn, up_a)
+    up_b = plane_first(after(up_rows[low_rows:], attn))
     grad_ffn = grad_ffn.reshape(tile, features)
 
     proj = call(
@@ -884,10 +903,11 @@
         [SMEM, VMEM, ANY],
         [pltpu.VMEM(w_out.shape, BF), pltpu.SemaphoreType.DMA((2 * far_n * zh_n,))],
     )[0]
-    down_plane = plane_first(after(down_rows, attn))
+    down_a = plane_first(after(down_rows[:low_rows], attn))
     proj = sum_team(proj)
-    up_plane = plane_second(up_plane)
-    proj, up_plane, down_plane = together(proj, up_plane, down_plane)
+    up_a = plane_second(up_a)
+    proj, up_a, up_b, down_a, w_g = together(proj, up_a, up_b, down_a, w_g)
+    down_b = plane_first(after(down_rows[low_rows:], proj))
     middle, normed_sent = call(
         middle_kernel,
         "middle",
@@ -895,8 +915,9 @@
         [proj, tokens_own, keep, gain_two],
     )
     normed_two = to_team(normed_sent)
-    w_u = both_cores(up_plane)
-    w_d = both_cores(plane_second(down_plane))
+    w_u = both_cores(up_a, True) + both_cores(plane_second(up_b), True)
+    down_a = both_cores(plane_second(down_a), True)
+    w_d = down_a + both_cores(plane_second(down_b), True)
     normed_two, w_u, w_d = together(normed_two, w_u, w_d)
     normed_two = normed_two.reshape(tile, features)
 

time: 668 us -> 651 us (0.975)
  waiting for transfers between devices: 308 us -> 269 us
  local copies, waits for them, and re-layouts: 37.7 us -> 51.2 us
  starting transfers between devices: 92.3 us -> 102 us
    ppermute x46 -> x48, waiting for transfers between devices: 275 us -> 240 us  [swap(): return lax.ppermute(block, axes, [(i, i ^ distance) for i in range(size)])]
    unnamed x107 -> x135, local copies, waits for them, and re-layouts: 16.1 us -> 25.1 us
    ppermute x46 -> x48, starting transfers between devices: 40.2 us -> 46.3 us  [swap(): return lax.ppermute(block, axes, [(i, i ^ distance) for i in range(size)])]
  transfers between devices with their start and end apart: 60 -> 62, of which waited for: 30 -> 26; matrix products, arithmetic and copies ran while one was open for 5% -> 7% of each run, Pallas kernels for 16% -> 18%
where the time goes in v3:
time: 651 us; the launch traced here: 640 us
  waiting for transfers between devices  269 us (41%)
  Pallas kernels  166 us (25%)
  starting transfers between devices  102 us (16%)
  local copies, waits for them, and re-layouts  51.2 us (8%)
  other arithmetic  22.3 us (3%)
  between operations  17.7 us (3%)
  blocking collectives  12.8 us (2%)
    ppermute x48, waiting for transfers between devices, swap(): return lax.ppermute(block, axes, [(i, i ^ distance) for i in range(size)])  240 us
    pallas_call x14, Pallas kernels, call(): pl.pallas_call(kernel, out_shape=tuple((jax.ShapeDtypeStruct(s, d) for s,...  86.8 us
    all_to_all x11, starting transfers between devices, to_team(): return lax.all_to_all(pieces, TEAM, split_axis=0, concat_axis=0, tiled=True)  55.7 us
    pallas_call x14, Pallas kernels, outer(): pl.pallas_call(outer_kernel, out_shape=jax.ShapeDtypeStruct((count * bloc...  49.4 us
    ppermute x48, starting transfers between devices, swap(): return lax.ppermute(block, axes, [(i, i ^ distance) for i in range(size)])  46.3 us
    all_to_all x11, waiting for transfers between devices, to_team(): return lax.all_to_all(pieces, TEAM, split_axis=0, concat_axis=0, tiled=True)  28.1 us
    unnamed x135, local copies, waits for them, and re-layouts  25.1 us
    pallas_call x1, Pallas kernels, attention_backward(): pl.pallas_call(functools.partial(backward_kernel, docs, sizes, run, len(k...  18 us
  transfers between devices with their start and end apart: 62, of which 26 were waited for; matrix products, arithmetic and copies ran while one was open for 7% of the time, Pallas kernels for 18%

profile of v3, /device:TPU:0, one launch (start us, length us, event | category | flops | bytes accessed | tf_op | source)
XLA Modules:
  0.0 640.4 jit_solution(3402750300788405665)
XLA Ops:
  12.8 5.4 all-to-all-start
  22.8 13.3 %all-to-all-done = bf16[4,64,2816]{2,1,0:T(8,128)(2,1)S(1)} async-done(((bf16[4,64,2816]{2,1,0:T(8,128)(2,1)}), bf16[4,64,2816]{2,1,0:T(8,128)(2,1)S(1)}, u32[]{:S(2)}, u32[]{:S(2)}) %all-to-all-start) | async-done | bytes 1441824 | tf_op jit(solution)/shard_map/all_to_all | solution.py:699
  36.0 3.6 all-to-all-start.1
  51.1 20.6 %collective-permute-done.refs_1_ = bf16[256,896]{1,0:T(8,128)(2,1)} collective-permute-done((bf16[256,896]{1,0:T(8,128)(2,1)}, bf16[256,896]{1,0:T(8,128)(2,1)}, u32[]{:S(2)}, u32[]{:S(2)}) %collective-permute-start) | collective-permute-done | bytes 458784 | tf_op jit(solution)/shard_map/ppermute | solution.py:678
  76.2 10.6 %collective-permute-done.2.refs_3_ = bf16[256,896]{1,0:T(8,128)(2,1)} collective-permute-done((bf16[256,896]{1,0:T(8,128)(2,1)}, bf16[256,896]{1,0:T(8,128)(2,1)}, u32[]{:S(2)}, u32[]{:S(2)}) %collective-permute-start.2) | collective-permute-done | bytes 458784 | tf_op jit(solution)/shard_map/ppermute | solution.py:678
  90.4 7.5 %project.1 = (bf16[512,2048]{1,0:T(8,128)(2,1)}, f32[512,1]{1,0:T(8,128)}, f32[512,512]{1,0:T(8,128)}, bf16[512,256]{1,0:T(8,128)(2,1)}, f32[8,2048]{1,0:T(8,128)}) custom-call(bf16[512,2048]{1,0:T(8,128)(2,1)} %bitcast.77, f32[512,128]{1,0:T(8,128)} %pad_maximum_fusion.4.cosine, f32[512,128]{1,0:T(8,128)} %pad_maximum_fusion.5.sine, ...), custom_call_target="tpu_custom_call" | custom-call | flops 1879048192 | bytes 6291456 | tf_op jit(solution)/shard_map/project/pallas_call | solution.py:314
  98.0 5.9 all-to-all-start.2
  112.7 17.7 %collective-permute-done.7.refs_1_ = bf16[512,256]{1,0:T(8,128)(2,1)S(1)} collective-permute-done((bf16[512,256]{1,0:T(8,128)(2,1)S(1)}, bf16[512,256]{1,0:T(8,128)(2,1)S(1)}, u32[]{:S(2)}, u32[]{:S(2)}) %collective-permute-start.7) | collective-permute-done | bytes 262176 | tf_op jit(solution)/shard_map/ppermute | solution.py:678
  132.6 6.3 collective-permute-done.9.refs_3_
  139.7 3.6 all-to-all-start.3
  145.2 3.5 collective-permute-start.14
  150.8 11.7 %attention_forward.1 = (bf16[512,512]{1,0:T(8,128)(2,1)}, bf16[512,512]{1,0:T(8,128)(2,1)}, f32[4,512]{1,0:T(4,128)}) custom-call(s32[10]{0:T(128)} %concatenate.58.meta, f32[512,512]{1,0:T(8,128)} %get-tuple-element.159.q, f32[512,128]{1,0:T(8,128)} %pad_maximum_fusion.4.cosine, f32[512,128]{1,0:T(8,128)} %pad_maximum_fusion.5.sine, s32[1,512]{1,0:T(1,128)} %fusion.28.qpos, ...), custom_call_target="tpu_custom_call" | custom-call | flops 2147483648 | bytes 4194304 | tf_op jit(solution)/shard_map/attention_forward/pallas_call | solution.py:259
  162.5 25.8 %collective-permute-done.14 = bf16[128,1408]{1,0:T(8,128)(2,1)S(1)} collective-permute-done((bf16[128,1408]{1,0:T(8,128)(2,1)S(1)}, bf16[128,1408]{1,0:T(8,128)(2,1)S(1)}, u32[]{:S(2)}, u32[]{:S(2)}) %collective-permute-start.14) | collective-permute-done | bytes 360480 | tf_op jit(solution)/shard_map/ppermute | solution.py:678
  189.1 5.7 proj.1
  194.8 8.0 %all-to-all-start.4 = ((bf16[4,128,2048]{2,1,0:T(8,128)(2,1)}), bf16[4,128,2048]{2,1,0:T(8,128)(2,1)S(1)}, u32[]{:S(2)}, u32[]{:S(2)}) async-start(bf16[4,128,2048]{2,1,0:T(8,128)(2,1)} %bitcast.71), calls=%async_computation.4 | async-start | bytes 4194304 | tf_op jit(solution)/shard_map/all_to_all | solution.py:699
  210.5 23.9 %collective-permute-done.19 = bf16[128,1408]{1,0:T(8,128)(2,1)S(1)} collective-permute-done((bf16[128,1408]{1,0:T(8,128)(2,1)S(1)}, bf16[128,1408]{1,0:T(8,128)(2,1)S(1)}, u32[]{:S(2)}, u32[]{:S(2)}) %collective-permute-start.19) | collective-permute-done | bytes 360480 | tf_op jit(solution)/shard_map/ppermute | solution.py:678
  234.4 4.6 collective-permute-done.17
  250.5 3.9 middle.1
  254.4 3.7 all-to-all-start.5
  270.0 7.9 %collective-permute-done.28 = bf16[128,1408]{1,0:T(8,128)(2,1)S(1)} collective-permute-done((bf16[128,1408]{1,0:T(8,128)(2,1)}, bf16[128,1408]{1,0:T(8,128)(2,1)S(1)}, u32[]{:S(2)}, u32[]{:S(2)}) %collective-permute-start.28) | collective-permute-done | bytes 360480 | tf_op jit(solution)/shard_map/ppermute | solution.py:678
  283.1 32.6 %mlp.1 = (bf16[512,1408]{1,0:T(8,128)(2,1)}, bf16[512,1408]{1,0:T(8,128)(2,1)}, bf16[512,1408]{1,0:T(8,128)(2,1)}, bf16[512,2048]{1,0:T(8,128)(2,1)}, bf16[512,2048]{1,0:T(8,128)(2,1)}) custom-call(s32[10]{0:T(128)} %concatenate.58.meta, bf16[512,2048]{1,0:T(8,128)(2,1)} %bitcast.62, bf16[512,2048]{1,0:T(8,128)(2,1)} %bitcast.67, ...), custom_call_target="tpu_custom_call" | custom-call | flops 17716740096 | bytes 21495848 | tf_op jit(solution)/shard_map/mlp/pallas_call | solution.py:314
  315.7 5.1 all-to-all-start.6
  320.9 4.3 outer.14
  325.4 4.3 outer.18
  330.1 4.4 outer.16
  336.1 5.9 outer.15
  342.0 4.4 all-to-all-done.6.parts
  346.4 4.9 middle_grad.1
  351.3 4.4 all-to-all-start.7
  358.7 5.9 outer.19
  367.2 6.0 outer.17
  373.1 42.0 %collective-permute-done.32 = bf16[512,1408]{1,0:T(8,128)(2,1)S(1)} collective-permute-done((bf16[512,1408]{1,0:T(8,128)(2,1)S(1)}, bf16[512,1408]{1,0:T(8,128)(2,1)S(1)}, u32[]{:S(2)}, u32[]{:S(2)}) %collective-permute-start.32) | collective-permute-done | bytes 1441824 | tf_op jit(solution)/shard_map/ppermute | solution.py:678
  416.6 4.7 all-to-all-start.8
  427.2 18.0 %attention_backward.1 = (bf16[512,512]{1,0:T(8,128)(2,1)}, bf16[4096,256]{1,0:T(8,128)(2,1)}) custom-call(s32[10]{0:T(128)} %concatenate.58.meta, bf16[512,512]{1,0:T(8,128)(2,1)} %get-tuple-element.176.q, bf16[512,512]{1,0:T(8,128)(2,1)} %get-tuple-element.239.attn.o.right, bf16[512,2048]{1,0:T(8,128)(2,1)} %bitcast.18.g_proj.left, ...), custom_call_target="tpu_custom_call" | custom-call | flops 5368709120 | bytes 6291456 | tf_op jit(solution)/shard_map/attention_backward/pallas_call | solution.py:288
  445.2 12.6 %collective-permute-done.33 = bf16[256,1408]{1,0:T(8,128)(2,1)} collective-permute-done((bf16[256,1408]{1,0:T(8,128)(2,1)}, bf16[256,1408]{1,0:T(8,128)(2,1)}, u32[]{:S(2)}, u32[]{:S(2)}) %collective-permute-start.33) | collective-permute-done | bytes 720928 | tf_op jit(solution)/shard_map/ppermute | solution.py:678
  461.4 5.2 all-to-all-done.8.parts
  470.6 3.5 outer.23
  484.6 3.5 outer.21
  490.2 9.2 %collective-permute-done.37 = bf16[512,256]{1,0:T(8,128)(2,1)S(1)} collective-permute-done((bf16[512,256]{1,0:T(8,128)(2,1)S(1)}, bf16[512,256]{1,0:T(8,128)(2,1)S(1)}, u32[]{:S(2)}, u32[]{:S(2)}) %collective-permute-start.37) | collective-permute-done | bytes 262176 | tf_op jit(solution)/shard_map/ppermute | solution.py:678
  499.4 5.2 collective-permute-done.39
  505.8 9.2 %qkv_grad.1 = (bf16[512,2048]{1,0:T(8,128)(2,1)}, bf16[512,2048]{1,0:T(8,128)(2,1)}) custom-call(bf16[512,512]{1,0:T(8,128)(2,1)} %get-tuple-element.237.right.grad_q, bf16[512,256]{1,0:T(8,128)(2,1)} %pad_maximum_fusion.6.grad_kv.right, bf16[512,2048]{1,0:T(8,128)(2,1)} %bitcast.78, f32[512,1]{1,0:T(8,128)} %get-tuple-element.244.scale, ...), custom_call_target="tpu_custom_call" | custom-call | flops 1879048192 | bytes 6555648 | tf_op jit(solution)/shard_map/qkv_grad/pallas_call | solution.py:314
  515.0 4.8 all-to-all-start.9
  532.0 25.7 %collective-permute-done.43 = bf16[256,1408]{1,0:T(8,128)(2,1)S(1)} collective-permute-done((bf16[256,1408]{1,0:T(8,128)(2,1)S(1)}, bf16[256,1408]{1,0:T(8,128)(2,1)S(1)}, u32[]{:S(2)}, u32[]{:S(2)}) %collective-permute-start.43) | collective-permute-done | bytes 720928 | tf_op jit(solution)/shard_map/ppermute | solution.py:678
  561.8 6.3 all-to-all-start.10
  575.0 3.4 output.1.array
  580.4 3.9 token_grad.1.array
  586.6 21.5 %collective-permute-done.45 = bf16[256,384]{1,0:T(8,128)(2,1)S(1)} collective-permute-done((bf16[256,384]{1,0:T(8,128)(2,1)S(1)}, bf16[256,384]{1,0:T(8,128)(2,1)S(1)}, u32[]{:S(2)}, u32[]{:S(2)}) %collective-permute-start.45) | collective-permute-done | bytes 196640 | tf_op jit(solution)/shard_map/ppermute | solution.py:678
  617.0 12.8 %all_to_all.60 = bf16[4,64,1408]{2,1,0:T(8,128)(2,1)S(1)} all-to-all(bf16[4,64,1408]{2,1,0:T(8,128)(2,1)S(1)} %bitcast.76), channel_id=1, replica_groups=mesh['far'=2,'x'=2,'core'=2,'zh'=2,'zl'=2] {'x','zl'}, dimensions={0} | all-to-all | bytes 1441792 | tf_op jit(solution)/shard_map/all_to_all | solution.py:699
  (329 shorter events, 156.0 us)
Async XLA Ops:
  12.8 23.2 %all-to-all-start = ((bf16[4,64,2816]{2,1,0:T(8,128)(2,1)}), bf16[4,64,2816]{2,1,0:T(8,128)(2,1)S(1)}, u32[]{:S(2)}, u32[]{:S(2)}) async-start(bf16[4,64,2816]{2,1,0:T(8,128)(2,1)} %pack.2), calls=%async_computation | async-start | bytes 2883584 | tf_op jit(solution)/shard_map/all_to_all | solution.py:699
  36.0 37.8 %all-to-all-start.1 = ((bf16[4,128,2048]{2,1,0:T(8,128)(2,1)}), bf16[4,128,2048]{2,1,0:T(8,128)(2,1)S(1)}, u32[]{:S(2)}, u32[]{:S(2)}) async-start(bf16[4,128,2048]{2,1,0:T(8,128)(2,1)} %get-tuple-element.140), calls=%async_computation.1 | async-start | bytes 4194304 | tf_op jit(solution)/shard_map/all_to_all | solution.py:699
  39.7 99.3 %all-gather.3.cloned.1.call-start = ((), (), s32[]{:S(2)}) async-start(), calls=%async_computation.13 | async-start | bytes 2359296 | tf_op jit(solution)/shard_map/all_gather | solution.py:752
  40.5 31.2 %collective-permute-start = (bf16[256,896]{1,0:T(8,128)(2,1)}, bf16[256,896]{1,0:T(8,128)(2,1)}, u32[]{:S(2)}, u32[]{:S(2)}) collective-permute-start(bf16[256,896]{1,0:T(8,128)(2,1)} %slice.222.refs_0_), channel_id=1, source_target_pairs={{0,2},{2,0},{1,3},{3,1},{4,6},{6,4},{5,7},{7,5},{8,10},{10,8},{9,1... | collective-permute-start | bytes 1376264 | tf_op jit(solution)/shard_map/ppermute | solution.py:678
  43.2 28.6 %collective-permute-start.1 = (bf16[256,896]{1,0:T(8,128)(2,1)}, bf16[256,896]{1,0:T(8,128)(2,1)}, u32[]{:S(2)}, u32[]{:S(2)}) collective-permute-start(bf16[256,896]{1,0:T(8,128)(2,1)} %slice.222.refs_0_), channel_id=1, source_target_pairs={{0,16},{16,0},{1,17},{17,1},{2,18},{18,2},{3,19},{19,3},{4,20},{20... | collective-permute-start | bytes 1376264 | tf_op jit(solution)/shard_map/ppermute | solution.py:678
  73.9 167.2 %all-gather.5.cloned.1.call-start = ((), (), s32[]{:S(2)}) async-start(), calls=%async_computation.14 | async-start | bytes 6488064 | tf_op jit(solution)/shard_map/all_gather | solution.py:752
  75.5 14.8 %collective-permute-start.4 = (bf16[256,896]{1,0:T(8,128)(2,1)}, bf16[256,896]{1,0:T(8,128)(2,1)}, u32[]{:S(2)}, u32[]{:S(2)}) collective-permute-start(bf16[256,896]{1,0:T(8,128)(2,1)} %collective-permute-done.refs_1_), channel_id=1, source_target_pairs={{0,4},{4,0},{1,5},{5,1},{2,6},{6,2},{3,7},{7,3},{8,12},{12,8},{9,1... | collective-permute-start | bytes 1376264 | tf_op jit(solution)/shard_map/ppermute | solution.py:678
  75.6 14.8 %collective-permute-start.3 = (bf16[256,896]{1,0:T(8,128)(2,1)}, bf16[256,896]{1,0:T(8,128)(2,1)}, u32[]{:S(2)}, u32[]{:S(2)}) collective-permute-start(bf16[256,896]{1,0:T(8,128)(2,1)} %slice.222.refs_0_), channel_id=1, source_target_pairs={{0,4},{4,0},{1,5},{5,1},{2,6},{6,2},{3,7},{7,3},{8,12},{12,8},{9,1... | collective-permute-start | bytes 1376264 | tf_op jit(solution)/shard_map/ppermute | solution.py:678
  76.1 14.3 %collective-permute-start.5 = (bf16[256,896]{1,0:T(8,128)(2,1)}, bf16[256,896]{1,0:T(8,128)(2,1)}, u32[]{:S(2)}, u32[]{:S(2)}) collective-permute-start(bf16[256,896]{1,0:T(8,128)(2,1)} %collective-permute-done.1.refs_2_), channel_id=1, source_target_pairs={{0,4},{4,0},{1,5},{5,1},{2,6},{6,2},{3,7},{7,3},{8,12},{12,8},{9,1... | collective-permute-start | bytes 1376264 | tf_op jit(solution)/shard_map/ppermute | solution.py:678
  98.0 34.5 %all-to-all-start.2 = ((bf16[4,64,2816]{2,1,0:T(8,128)(2,1)}), bf16[4,64,2816]{2,1,0:T(8,128)(2,1)S(1)}, u32[]{:S(2)}, u32[]{:S(2)}) async-start(bf16[4,64,2816]{2,1,0:T(8,128)(2,1)} %pack.3), calls=%async_computation.2 | async-start | bytes 2883584 | tf_op jit(solution)/shard_map/all_to_all | solution.py:699
  105.3 25.1 %collective-permute-start.7 = (bf16[512,256]{1,0:T(8,128)(2,1)S(1)}, bf16[512,256]{1,0:T(8,128)(2,1)S(1)}, u32[]{:S(2)}, u32[]{:S(2)}) collective-permute-start(bf16[512,256]{1,0:T(8,128)(2,1)S(1)} %copy-done.51), channel_id=1, source_target_pairs={{0,2},{2,0},{1,3},{3,1},{4,6},{6,4},{5,7},{7,5},{8,10},{10,8},{9,1... | collective-permute-start | bytes 786440 | tf_op jit(solution)/shard_map/ppermute | solution.py:678
  105.3 25.1 %collective-permute-start.8 = (bf16[512,256]{1,0:T(8,128)(2,1)S(1)}, bf16[512,256]{1,0:T(8,128)(2,1)S(1)}, u32[]{:S(2)}, u32[]{:S(2)}) collective-permute-start(bf16[512,256]{1,0:T(8,128)(2,1)S(1)} %copy-done.51), channel_id=1, source_target_pairs={{0,16},{16,0},{1,17},{17,1},{2,18},{18,2},{3,19},{19,3},{4,20},{20... | collective-permute-start | bytes 786440 | tf_op jit(solution)/shard_map/ppermute | solution.py:678
  139.7 49.4 %all-to-all-start.3 = ((bf16[4,128,2048]{2,1,0:T(8,128)(2,1)}), bf16[4,128,2048]{2,1,0:T(8,128)(2,1)S(1)}, u32[]{:S(2)}, u32[]{:S(2)}) async-start(bf16[4,128,2048]{2,1,0:T(8,128)(2,1)} %get-tuple-element.180), calls=%async_computation.3 | async-start | bytes 4194304 | tf_op jit(solution)/shard_map/all_to_all | solution.py:699
  145.2 43.1 %collective-permute-start.14 = (bf16[128,1408]{1,0:T(8,128)(2,1)S(1)}, bf16[128,1408]{1,0:T(8,128)(2,1)S(1)}, u32[]{:S(2)}, u32[]{:S(2)}) collective-permute-start(bf16[128,1408]{1,0:T(8,128)(2,1)S(1)} %get-tuple-element.193), channel_id=1, source_target_pairs={{0,2},{2,0},{1,3},{3,1},{4,6},{6,4},{5,7},{7,5},{8,10},{10,8},{9,1... | collective-permute-start | bytes 1081352 | tf_op jit(solution)/shard_map/ppermute | solution.py:678
  148.7 40.4 %collective-permute-start.15 = (bf16[128,1408]{1,0:T(8,128)(2,1)S(1)}, bf16[128,1408]{1,0:T(8,128)(2,1)}, u32[]{:S(2)}, u32[]{:S(2)}) collective-permute-start(bf16[128,1408]{1,0:T(8,128)(2,1)S(1)} %get-tuple-element.193), channel_id=1, source_target_pairs={{0,16},{16,0},{1,17},{17,1},{2,18},{18,2},{3,19},{19,3},{4,20},{20... | collective-permute-start | bytes 1081352 | tf_op jit(solution)/shard_map/ppermute | solution.py:678
  194.8 46.3 %all-to-all-start.4 = ((bf16[4,128,2048]{2,1,0:T(8,128)(2,1)}), bf16[4,128,2048]{2,1,0:T(8,128)(2,1)S(1)}, u32[]{:S(2)}, u32[]{:S(2)}) async-start(bf16[4,128,2048]{2,1,0:T(8,128)(2,1)} %bitcast.71), calls=%async_computation.4 | async-start | bytes 4194304 | tf_op jit(solution)/shard_map/all_to_all | solution.py:699
  202.8 31.5 %collective-permute-start.19 = (bf16[128,1408]{1,0:T(8,128)(2,1)S(1)}, bf16[128,1408]{1,0:T(8,128)(2,1)S(1)}, u32[]{:S(2)}, u32[]{:S(2)}) collective-permute-start(bf16[128,1408]{1,0:T(8,128)(2,1)S(1)} %get-tuple-element.200), channel_id=1, source_target_pairs={{0,2},{2,0},{1,3},{3,1},{4,6},{6,4},{5,7},{7,5},{8,10},{10,8},{9,1... | collective-permute-start | bytes 1081352 | tf_op jit(solution)/shard_map/ppermute | solution.py:678
  202.9 31.5 %collective-permute-start.20 = (bf16[128,1408]{1,0:T(8,128)(2,1)S(1)}, bf16[128,1408]{1,0:T(8,128)(2,1)S(1)}, u32[]{:S(2)}, u32[]{:S(2)}) collective-permute-start(bf16[128,1408]{1,0:T(8,128)(2,1)S(1)} %get-tuple-element.200), channel_id=1, source_target_pairs={{0,16},{16,0},{1,17},{17,1},{2,18},{18,2},{3,19},{19,3},{4,20},{20... | collective-permute-start | bytes 1081352 | tf_op jit(solution)/shard_map/ppermute | solution.py:678
  204.1 34.9 %collective-permute-start.17 = (bf16[128,1408]{1,0:T(8,128)(2,1)S(1)}, bf16[128,1408]{1,0:T(8,128)(2,1)S(1)}, u32[]{:S(2)}, u32[]{:S(2)}) collective-permute-start(bf16[128,1408]{1,0:T(8,128)(2,1)S(1)} %copy-done.28), channel_id=1, source_target_pairs={{0,2},{2,0},{1,3},{3,1},{4,6},{6,4},{5,7},{7,5},{8,10},{10,8},{9,1... | collective-permute-start | bytes 1081352 | tf_op jit(solution)/shard_map/ppermute | solution.py:678
  206.9 32.0 %collective-permute-start.18 = (bf16[128,1408]{1,0:T(8,128)(2,1)S(1)}, bf16[128,1408]{1,0:T(8,128)(2,1)S(1)}, u32[]{:S(2)}, u32[]{:S(2)}) collective-permute-start(bf16[128,1408]{1,0:T(8,128)(2,1)S(1)} %copy-done.28), channel_id=1, source_target_pairs={{0,16},{16,0},{1,17},{17,1},{2,18},{18,2},{3,19},{19,3},{4,20},{20... | collective-permute-start | bytes 1081352 | tf_op jit(solution)/shard_map/ppermute | solution.py:678
  207.9 31.8 %collective-permute-start.16 = (bf16[128,1408]{1,0:T(8,128)(2,1)}, bf16[128,1408]{1,0:T(8,128)(2,1)}, u32[]{:S(2)}, u32[]{:S(2)}) collective-permute-start(bf16[128,1408]{1,0:T(8,128)(2,1)} %copy-done.34), channel_id=1, source_target_pairs={{0,16},{16,0},{1,17},{17,1},{2,18},{18,2},{3,19},{19,3},{4,20},{20... | collective-permute-start | bytes 1081352 | tf_op jit(solution)/shard_map/ppermute | solution.py:678
  241.9 25.0 %collective-permute-start.26 = (bf16[128,1408]{1,0:T(8,128)(2,1)S(1)}, bf16[128,1408]{1,0:T(8,128)(2,1)}, u32[]{:S(2)}, u32[]{:S(2)}) collective-permute-start(bf16[128,1408]{1,0:T(8,128)(2,1)S(1)} %get-tuple-element.203), channel_id=1, source_target_pairs={{0,2},{2,0},{1,3},{3,1},{4,6},{6,4},{5,7},{7,5},{8,10},{10,8},{9,1... | collective-permute-start | bytes 1081352 | tf_op jit(solution)/shard_map/ppermute | solution.py:678
  244.0 25.0 %collective-permute-start.27 = (bf16[128,1408]{1,0:T(8,128)(2,1)S(1)}, bf16[128,1408]{1,0:T(8,128)(2,1)}, u32[]{:S(2)}, u32[]{:S(2)}) collective-permute-start(bf16[128,1408]{1,0:T(8,128)(2,1)S(1)} %get-tuple-element.203), channel_id=1, source_target_pairs={{0,16},{16,0},{1,17},{17,1},{2,18},{18,2},{3,19},{19,3},{4,20},{20... | collective-permute-start | bytes 1081352 | tf_op jit(solution)/shard_map/ppermute | solution.py:678
  245.9 17.3 %collective-permute-start.24 = (bf16[128,1408]{1,0:T(8,128)(2,1)}, bf16[128,1408]{1,0:T(8,128)(2,1)}, u32[]{:S(2)}, u32[]{:S(2)}) collective-permute-start(bf16[128,1408]{1,0:T(8,128)(2,1)} %copy-done.36), channel_id=1, source_target_pairs={{0,16},{16,0},{1,17},{17,1},{2,18},{18,2},{3,19},{19,3},{4,20},{20... | collective-permute-start | bytes 1081352 | tf_op jit(solution)/shard_map/ppermute | solution.py:678
  248.2 18.6 %collective-permute-start.22 = (bf16[128,1408]{1,0:T(8,128)(2,1)S(1)}, bf16[128,1408]{1,0:T(8,128)(2,1)S(1)}, u32[]{:S(2)}, u32[]{:S(2)}) collective-permute-start(bf16[128,1408]{1,0:T(8,128)(2,1)S(1)} %collective-permute-done.17), channel_id=1, source_target_pairs={{0,16},{16,0},{1,17},{17,1},{2,18},{18,2},{3,19},{19,3},{4,20},{20... | collective-permute-start | bytes 1081352 | tf_op jit(solution)/shard_map/ppermute | solution.py:678
  254.4 27.2 %all-to-all-start.5 = ((bf16[4,128,2048]{2,1,0:T(8,128)(2,1)}), bf16[4,128,2048]{2,1,0:T(8,128)(2,1)S(1)}, u32[]{:S(2)}, u32[]{:S(2)}) async-start(bf16[4,128,2048]{2,1,0:T(8,128)(2,1)} %get-tuple-element.192), calls=%async_computation.5 | async-start | bytes 4194304 | tf_op jit(solution)/shard_map/all_to_all | solution.py:699
  262.4 15.7 %collective-permute-start.21 = (bf16[512,1408]{1,0:T(8,128)(2,1)}, bf16[512,1408]{1,0:T(8,128)(2,1)S(1)}, u32[]{:S(2)}, u32[]{:S(2)}) collective-permute-start(bf16[512,1408]{1,0:T(8,128)(2,1)} %constant_dynamic-update-slice_fusion.refs_0_), channel_id=1, source_target_pairs={{0,4},{4,0},{1,5},{5,1},{2,6},{6,2},{3,7},{7,3},{8,12},{12,8},{9,1... | collective-permute-start | bytes 4325384 | tf_op jit(solution)/shard_map/ppermute | solution.py:678
  315.7 30.6 %all-to-all-start.6 = ((bf16[4,128,2048]{2,1,0:T(8,128)(2,1)}), bf16[4,128,2048]{2,1,0:T(8,128)(2,1)}, u32[]{:S(2)}, u32[]{:S(2)}) async-start(bf16[4,128,2048]{2,1,0:T(8,128)(2,1)} %bitcast.81), calls=%async_computation.6 | async-start | bytes 4194304 | tf_op jit(solution)/shard_map/all_to_all | solution.py:699
  329.7 26.1 %collective-permute-start.35 = (bf16[1024,1408]{1,0:T(8,128)(2,1)}, bf16[1024,1408]{1,0:T(8,128)(2,1)}, u32[]{:S(2)}, u32[]{:S(2)}) collective-permute-start(bf16[1024,1408]{1,0:T(8,128)(2,1)} %outer.18), channel_id=1, source_target_pairs={{0,4},{4,0},{1,5},{5,1},{2,6},{6,2},{3,7},{7,3},{8,12},{12,8},{9,1... | collective-permute-start | bytes 8650760 | tf_op jit(solution)/shard_map/ppermute | solution.py:678
  334.4 32.8 %collective-permute-start.31 = (bf16[1024,1408]{1,0:T(8,128)(2,1)}, bf16[1024,1408]{1,0:T(8,128)(2,1)}, u32[]{:S(2)}, u32[]{:S(2)}) collective-permute-start(bf16[1024,1408]{1,0:T(8,128)(2,1)} %outer.16), channel_id=1, source_target_pairs={{0,4},{4,0},{1,5},{5,1},{2,6},{6,2},{3,7},{7,3},{8,12},{12,8},{9,1... | collective-permute-start | bytes 8650760 | tf_op jit(solution)/shard_map/ppermute | solution.py:678
  351.3 65.3 %all-to-all-start.7 = ((bf16[4,128,2048]{2,1,0:T(8,128)(2,1)}), bf16[4,128,2048]{2,1,0:T(8,128)(2,1)}, u32[]{:S(2)}, u32[]{:S(2)}) async-start(bf16[4,128,2048]{2,1,0:T(8,128)(2,1)} %get-tuple-element.220), calls=%async_computation.7 | async-start | bytes 4194304 | tf_op jit(solution)/shard_map/all_to_all | solution.py:699
  355.7 105.6 %reduce-scatter.2.cloned.1.call-start = ((), (), s32[]{:S(2)}) async-start(), calls=%async_computation.15 | async-start | bytes 3604480 | tf_op jit(solution)/shard_map/reduce_scatter | solution.py:756
  366.2 48.9 %collective-permute-start.32 = (bf16[512,1408]{1,0:T(8,128)(2,1)S(1)}, bf16[512,1408]{1,0:T(8,128)(2,1)S(1)}, u32[]{:S(2)}, u32[]{:S(2)}) collective-permute-start(bf16[512,1408]{1,0:T(8,128)(2,1)S(1)} %slice.183), channel_id=1, source_target_pairs={{0,16},{16,0},{1,17},{17,1},{2,18},{18,2},{3,19},{19,3},{4,20},{20... | collective-permute-start | bytes 4325384 | tf_op jit(solution)/shard_map/ppermute | solution.py:678
  416.6 50.0 %all-to-all-start.8 = ((bf16[4,128,2048]{2,1,0:T(8,128)(2,1)}), bf16[4,128,2048]{2,1,0:T(8,128)(2,1)}, u32[]{:S(2)}, u32[]{:S(2)}) async-start(bf16[4,128,2048]{2,1,0:T(8,128)(2,1)} %bitcast.79), calls=%async_computation.8 | async-start | bytes 4194304 | tf_op jit(solution)/shard_map/all_to_all | solution.py:699
  421.4 38.5 %collective-permute-start.34 = (bf16[512,1408]{1,0:T(8,128)(2,1)S(1)}, bf16[512,1408]{1,0:T(8,128)(2,1)S(1)}, u32[]{:S(2)}, u32[]{:S(2)}) collective-permute-start(bf16[512,1408]{1,0:T(8,128)(2,1)S(1)} %slice.187), channel_id=1, source_target_pairs={{0,16},{16,0},{1,17},{17,1},{2,18},{18,2},{3,19},{19,3},{4,20},{20... | collective-permute-start | bytes 4325384 | tf_op jit(solution)/shard_map/ppermute | solution.py:678
  424.6 33.2 %collective-permute-start.33 = (bf16[256,1408]{1,0:T(8,128)(2,1)}, bf16[256,1408]{1,0:T(8,128)(2,1)}, u32[]{:S(2)}, u32[]{:S(2)}) collective-permute-start(bf16[256,1408]{1,0:T(8,128)(2,1)} %slice.185), channel_id=1, source_target_pairs={{0,2},{2,0},{1,3},{3,1},{4,6},{6,4},{5,7},{7,5},{8,10},{10,8},{9,1... | collective-permute-start | bytes 2162696 | tf_op jit(solution)/shard_map/ppermute | solution.py:678
  478.1 21.4 %collective-permute-start.37 = (bf16[512,256]{1,0:T(8,128)(2,1)S(1)}, bf16[512,256]{1,0:T(8,128)(2,1)S(1)}, u32[]{:S(2)}, u32[]{:S(2)}) collective-permute-start(bf16[512,256]{1,0:T(8,128)(2,1)S(1)} %get-tuple-element.276), channel_id=1, source_target_pairs={{0,2},{2,0},{16,18},{18,16},{1,3},{3,1},{17,19},{19,17},{4,6},{6,4... | collective-permute-start | bytes 786440 | tf_op jit(solution)/shard_map/ppermute | solution.py:678
  479.3 20.1 %collective-permute-start.38 = (bf16[512,256]{1,0:T(8,128)(2,1)S(1)}, bf16[512,256]{1,0:T(8,128)(2,1)S(1)}, u32[]{:S(2)}, u32[]{:S(2)}) collective-permute-start(bf16[512,256]{1,0:T(8,128)(2,1)S(1)} %get-tuple-element.275), channel_id=1, source_target_pairs={{0,16},{2,18},{16,0},{18,2},{1,17},{3,19},{17,1},{19,3},{4,20},{6,... | collective-permute-start | bytes 786440 | tf_op jit(solution)/shard_map/ppermute | solution.py:678
  480.4 24.3 %collective-permute-start.39 = (bf16[512,256]{1,0:T(8,128)(2,1)S(1)}, bf16[512,256]{1,0:T(8,128)(2,1)S(1)}, u32[]{:S(2)}, u32[]{:S(2)}) collective-permute-start(bf16[512,256]{1,0:T(8,128)(2,1)S(1)} %get-tuple-element.274), channel_id=1, source_target_pairs={{0,18},{2,16},{16,2},{18,0},{1,19},{3,17},{17,3},{19,1},{4,22},{6,... | collective-permute-start | bytes 786440 | tf_op jit(solution)/shard_map/ppermute | solution.py:678
  515.0 44.9 %all-to-all-start.9 = ((bf16[4,128,2048]{2,1,0:T(8,128)(2,1)}), bf16[4,128,2048]{2,1,0:T(8,128)(2,1)}, u32[]{:S(2)}, u32[]{:S(2)}) async-start(bf16[4,128,2048]{2,1,0:T(8,128)(2,1)} %bitcast.80), calls=%async_computation.10 | async-start | bytes 4194304 | tf_op jit(solution)/shard_map/all_to_all | solution.py:699
  520.2 37.4 %collective-permute-start.43 = (bf16[256,1408]{1,0:T(8,128)(2,1)S(1)}, bf16[256,1408]{1,0:T(8,128)(2,1)S(1)}, u32[]{:S(2)}, u32[]{:S(2)}) collective-permute-start(bf16[256,1408]{1,0:T(8,128)(2,1)S(1)} %slice.201), channel_id=1, source_target_pairs={{0,2},{2,0},{1,3},{3,1},{4,6},{6,4},{5,7},{7,5},{8,10},{10,8},{9,1... | collective-permute-start | bytes 2162696 | tf_op jit(solution)/shard_map/ppermute | solution.py:678
  527.0 30.9 %collective-permute-start.41 = (bf16[1024,384]{1,0:T(8,128)(2,1)S(1)}, bf16[1024,384]{1,0:T(8,128)(2,1)S(1)}, u32[]{:S(2)}, u32[]{:S(2)}) collective-permute-start(bf16[1024,384]{1,0:T(8,128)(2,1)S(1)} %pad_maximum_fusion.2), channel_id=1, source_target_pairs={{0,4},{4,0},{1,5},{5,1},{2,6},{6,2},{3,7},{7,3},{8,12},{12,8},{9,1... | collective-permute-start | bytes 2359304 | tf_op jit(solution)/shard_map/ppermute | solution.py:678
  527.1 31.8 %collective-permute-start.42 = (bf16[512,1024]{1,0:T(8,128)(2,1)S(1)}, bf16[512,1024]{1,0:T(8,128)(2,1)S(1)}, u32[]{:S(2)}, u32[]{:S(2)}) collective-permute-start(bf16[512,1024]{1,0:T(8,128)(2,1)S(1)} %slice.199), channel_id=1, source_target_pairs={{0,16},{16,0},{1,17},{17,1},{2,18},{18,2},{3,19},{19,3},{4,20},{20... | collective-permute-start | bytes 3145736 | tf_op jit(solution)/shard_map/ppermute | solution.py:678
  561.8 51.2 %all-to-all-start.10 = ((bf16[4,64,4224]{2,1,0:T(8,128)(2,1)}), bf16[4,64,4224]{2,1,0:T(8,128)(2,1)S(1)}, u32[]{:S(2)}, u32[]{:S(2)}) async-start(bf16[4,64,4224]{2,1,0:T(8,128)(2,1)} %bitcast.70), calls=%async_computation.11 | async-start | bytes 4325376 | tf_op jit(solution)/shard_map/all_to_all | solution.py:699
  568.2 43.7 %collective-permute-start.44 = (bf16[256,1024]{1,0:T(8,128)(2,1)S(1)}, bf16[256,1024]{1,0:T(8,128)(2,1)S(1)}, u32[]{:S(2)}, u32[]{:S(2)}) collective-permute-start(bf16[256,1024]{1,0:T(8,128)(2,1)S(1)} %slice.203), channel_id=1, source_target_pairs={{0,2},{2,0},{1,3},{3,1},{4,6},{6,4},{5,7},{7,5},{8,10},{10,8},{9,1... | collective-permute-start | bytes 1572872 | tf_op jit(solution)/shard_map/ppermute | solution.py:678
  570.1 38.1 %collective-permute-start.45 = (bf16[256,384]{1,0:T(8,128)(2,1)S(1)}, bf16[256,384]{1,0:T(8,128)(2,1)S(1)}, u32[]{:S(2)}, u32[]{:S(2)}) collective-permute-start(bf16[256,384]{1,0:T(8,128)(2,1)S(1)} %get-tuple-element.277), channel_id=1, source_target_pairs={{0,2},{2,0},{16,18},{18,16},{1,3},{3,1},{17,19},{19,17},{4,6},{6,4... | collective-permute-start | bytes 589832 | tf_op jit(solution)/shard_map/ppermute | solution.py:678
  572.4 35.8 %collective-permute-start.46 = (bf16[256,384]{1,0:T(8,128)(2,1)S(1)}, bf16[256,384]{1,0:T(8,128)(2,1)S(1)}, u32[]{:S(2)}, u32[]{:S(2)}) collective-permute-start(bf16[256,384]{1,0:T(8,128)(2,1)S(1)} %get-tuple-element.279), channel_id=1, source_target_pairs={{0,16},{2,18},{16,0},{18,2},{1,17},{3,19},{17,1},{19,3},{4,20},{6,... | collective-permute-start | bytes 589832 | tf_op jit(solution)/shard_map/ppermute | solution.py:678
  573.4 37.4 %collective-permute-start.47 = (bf16[256,384]{1,0:T(8,128)(2,1)S(1)}, bf16[256,384]{1,0:T(8,128)(2,1)S(1)}, u32[]{:S(2)}, u32[]{:S(2)}) collective-permute-start(bf16[256,384]{1,0:T(8,128)(2,1)S(1)} %get-tuple-element.278), channel_id=1, source_target_pairs={{0,18},{2,16},{16,2},{18,0},{1,19},{3,17},{17,3},{19,1},{4,22},{6,... | collective-permute-start | bytes 589832 | tf_op jit(solution)/shard_map/ppermute | solution.py:678
  (75 other events, 468.3 us)
Sparse Core Ops, SparseCore 0:
  74.0 38.3 all-gather.2
  114.8 82.9 all-gather.4
  364.8 71.2 reduce-scatter.1

commit v4 on v3

--- a/solution.py
+++ b/solution.py
@@ -1006,14 +1006,7 @@
     small_core = (own_small.astype(F32) + other_small.astype(F32)).astype(BF)
     grad_one, small_core, q_far, up_zh = together(grad_one, small_core, q_far, up_zh)
     q_zh = sum_axis(q_far, "zh")
-    rows_held = small_core.shape[0] // (far_n * zh_n)
-    small_sum = total_of(
-        [small_core[:rows_held]]
-        + [
-            swap(small_core[d * rows_held : (d + 1) * rows_held], ("far", "zh"), d)
-            for d in range(1, far_n * zh_n)
-        ]
-    ).astype(BF)
+    small_sum = sum_axis(sum_axis(small_core, "far"), "zh")
     merged = to_owner(jnp.concatenate([grad_down, gate_zh, up_zh], axis=1))
     grad_down, grad_gate, grad_up = (
         merged[:, :, :ff], merged[:, :, ff : 2 * ff], merged[:, :, 2 * ff :]

time: 651 us -> 646 us (level)
    ppermute x48 -> x47, waiting for transfers between devices: 240 us -> 237 us  [swap(): return lax.ppermute(block, axes, [(i, i ^ distance) for i in range(size)])]
    ppermute x48 -> x47, starting transfers between devices: 46.3 us -> 45.1 us  [swap(): return lax.ppermute(block, axes, [(i, i ^ distance) for i in range(size)])]
    unnamed x135 -> x137, local copies, waits for them, and re-layouts: 25.1 us -> 25.2 us
  transfers between devices with their start and end apart: 62 -> 61, of which waited for: 26 -> 26; matrix products, arithmetic and copies ran while one was open for 7% -> 7% of each run, Pallas kernels for 18% -> 18%
where the time goes in v4:
time: 646 us; the launch traced here: 636 us
  waiting for transfers between devices  266 us (41%)
  Pallas kernels  166 us (26%)
  starting transfers between devices  101 us (16%)
  local copies, waits for them, and re-layouts  51.1 us (8%)
  other arithmetic  21.4 us (3%)
  between operations  17.7 us (3%)
  blocking collectives  12 us (2%)
    ppermute x47, waiting for transfers between devices, swap(): return lax.ppermute(block, axes, [(i, i ^ distance) for i in range(size)])  237 us
    pallas_call x14, Pallas kernels, call(): pl.pallas_call(kernel, out_shape=tuple((jax.ShapeDtypeStruct(s, d) for s,...  86.9 us
    all_to_all x11, starting transfers between devices, to_team(): return lax.all_to_all(pieces, TEAM, split_axis=0, concat_axis=0, tiled=True)  55.8 us
    pallas_call x14, Pallas kernels, outer(): pl.pallas_call(outer_kernel, out_shape=jax.ShapeDtypeStruct((count * bloc...  49.3 us
    ppermute x47, starting transfers between devices, swap(): return lax.ppermute(block, axes, [(i, i ^ distance) for i in range(size)])  45.1 us
    all_to_all x11, waiting for transfers between devices, to_team(): return lax.all_to_all(pieces, TEAM, split_axis=0, concat_axis=0, tiled=True)  29.3 us
    unnamed x137, local copies, waits for them, and re-layouts  25.2 us
    pallas_call x1, Pallas kernels, attention_backward(): pl.pallas_call(functools.partial(backward_kernel, docs, sizes, run, len(k...  18 us
  transfers between devices with their start and end apart: 61, of which 26 were waited for; matrix products, arithmetic and copies ran while one was open for 7% of the time, Pallas kernels for 18%

profile of v4, /device:TPU:0, one launch (start us, length us, event | category | flops | bytes accessed | tf_op | source)
XLA Modules:
  0.0 635.5 jit_solution(10117383110410418251)
XLA Ops:
  12.8 5.4 all-to-all-start
  22.8 13.3 %all-to-all-done = bf16[4,64,2816]{2,1,0:T(8,128)(2,1)S(1)} async-done(((bf16[4,64,2816]{2,1,0:T(8,128)(2,1)}), bf16[4,64,2816]{2,1,0:T(8,128)(2,1)S(1)}, u32[]{:S(2)}, u32[]{:S(2)}) %all-to-all-start) | async-done | bytes 1441824 | tf_op jit(solution)/shard_map/all_to_all | solution.py:699
  36.0 3.6 all-to-all-start.1
  51.1 20.6 %collective-permute-done.refs_1_ = bf16[256,896]{1,0:T(8,128)(2,1)} collective-permute-done((bf16[256,896]{1,0:T(8,128)(2,1)}, bf16[256,896]{1,0:T(8,128)(2,1)}, u32[]{:S(2)}, u32[]{:S(2)}) %collective-permute-start) | collective-permute-done | bytes 458784 | tf_op jit(solution)/shard_map/ppermute | solution.py:678
  76.2 10.6 %collective-permute-done.2.refs_3_ = bf16[256,896]{1,0:T(8,128)(2,1)} collective-permute-done((bf16[256,896]{1,0:T(8,128)(2,1)}, bf16[256,896]{1,0:T(8,128)(2,1)}, u32[]{:S(2)}, u32[]{:S(2)}) %collective-permute-start.2) | collective-permute-done | bytes 458784 | tf_op jit(solution)/shard_map/ppermute | solution.py:678
  90.4 7.5 %project.1 = (bf16[512,2048]{1,0:T(8,128)(2,1)}, f32[512,1]{1,0:T(8,128)}, f32[512,512]{1,0:T(8,128)}, bf16[512,256]{1,0:T(8,128)(2,1)}, f32[8,2048]{1,0:T(8,128)}) custom-call(bf16[512,2048]{1,0:T(8,128)(2,1)} %bitcast.77, f32[512,128]{1,0:T(8,128)} %pad_maximum_fusion.4.cosine, f32[512,128]{1,0:T(8,128)} %pad_maximum_fusion.5.sine, ...), custom_call_target="tpu_custom_call" | custom-call | flops 1879048192 | bytes 6291456 | tf_op jit(solution)/shard_map/project/pallas_call | solution.py:314
  98.0 6.0 all-to-all-start.2
  112.7 17.7 %collective-permute-done.7.refs_1_ = bf16[512,256]{1,0:T(8,128)(2,1)S(1)} collective-permute-done((bf16[512,256]{1,0:T(8,128)(2,1)S(1)}, bf16[512,256]{1,0:T(8,128)(2,1)S(1)}, u32[]{:S(2)}, u32[]{:S(2)}) %collective-permute-start.7) | collective-permute-done | bytes 262176 | tf_op jit(solution)/shard_map/ppermute | solution.py:678
  132.7 6.3 collective-permute-done.9.refs_3_
  139.7 3.6 all-to-all-start.3
  145.2 3.5 collective-permute-start.14
  150.8 11.7 %attention_forward.1 = (bf16[512,512]{1,0:T(8,128)(2,1)}, bf16[512,512]{1,0:T(8,128)(2,1)}, f32[4,512]{1,0:T(4,128)}) custom-call(s32[10]{0:T(128)} %concatenate.58.meta, f32[512,512]{1,0:T(8,128)} %get-tuple-element.159.q, f32[512,128]{1,0:T(8,128)} %pad_maximum_fusion.4.cosine, f32[512,128]{1,0:T(8,128)} %pad_maximum_fusion.5.sine, s32[1,512]{1,0:T(1,128)} %fusion.28.qpos, ...), custom_call_target="tpu_custom_call" | custom-call | flops 2147483648 | bytes 4194304 | tf_op jit(solution)/shard_map/attention_forward/pallas_call | solution.py:259
  162.6 25.8 %collective-permute-done.14 = bf16[128,1408]{1,0:T(8,128)(2,1)S(1)} collective-permute-done((bf16[128,1408]{1,0:T(8,128)(2,1)S(1)}, bf16[128,1408]{1,0:T(8,128)(2,1)S(1)}, u32[]{:S(2)}, u32[]{:S(2)}) %collective-permute-start.14) | collective-permute-done | bytes 360480 | tf_op jit(solution)/shard_map/ppermute | solution.py:678
  189.1 5.7 proj.1
  194.8 8.0 %all-to-all-start.4 = ((bf16[4,128,2048]{2,1,0:T(8,128)(2,1)}), bf16[4,128,2048]{2,1,0:T(8,128)(2,1)S(1)}, u32[]{:S(2)}, u32[]{:S(2)}) async-start(bf16[4,128,2048]{2,1,0:T(8,128)(2,1)} %bitcast.71), calls=%async_computation.4 | async-start | bytes 4194304 | tf_op jit(solution)/shard_map/all_to_all | solution.py:699
  210.4 23.9 %collective-permute-done.19 = bf16[128,1408]{1,0:T(8,128)(2,1)S(1)} collective-permute-done((bf16[128,1408]{1,0:T(8,128)(2,1)S(1)}, bf16[128,1408]{1,0:T(8,128)(2,1)S(1)}, u32[]{:S(2)}, u32[]{:S(2)}) %collective-permute-start.19) | collective-permute-done | bytes 360480 | tf_op jit(solution)/shard_map/ppermute | solution.py:678
  234.3 4.5 collective-permute-done.17
  250.4 3.9 middle.1
  254.3 3.7 all-to-all-start.5
  270.0 7.9 %collective-permute-done.28 = bf16[128,1408]{1,0:T(8,128)(2,1)S(1)} collective-permute-done((bf16[128,1408]{1,0:T(8,128)(2,1)}, bf16[128,1408]{1,0:T(8,128)(2,1)S(1)}, u32[]{:S(2)}, u32[]{:S(2)}) %collective-permute-start.28) | collective-permute-done | bytes 360480 | tf_op jit(solution)/shard_map/ppermute | solution.py:678
  283.1 32.6 %mlp.1 = (bf16[512,1408]{1,0:T(8,128)(2,1)}, bf16[512,1408]{1,0:T(8,128)(2,1)}, bf16[512,1408]{1,0:T(8,128)(2,1)}, bf16[512,2048]{1,0:T(8,128)(2,1)}, bf16[512,2048]{1,0:T(8,128)(2,1)}) custom-call(s32[10]{0:T(128)} %concatenate.58.meta, bf16[512,2048]{1,0:T(8,128)(2,1)} %bitcast.62, bf16[512,2048]{1,0:T(8,128)(2,1)} %bitcast.67, ...), custom_call_target="tpu_custom_call" | custom-call | flops 17716740096 | bytes 21495848 | tf_op jit(solution)/shard_map/mlp/pallas_call | solution.py:314
  315.7 5.1 all-to-all-start.6
  320.9 4.3 outer.14
  325.4 4.3 outer.18
  330.0 4.3 outer.16
  336.1 5.9 outer.15
  342.0 4.4 all-to-all-done.6.parts
  346.4 4.9 middle_grad.1
  351.3 4.5 all-to-all-start.7
  358.7 5.9 outer.19
  367.2 5.9 outer.17
  373.1 42.2 %collective-permute-done.32 = bf16[512,1408]{1,0:T(8,128)(2,1)S(1)} collective-permute-done((bf16[512,1408]{1,0:T(8,128)(2,1)S(1)}, bf16[512,1408]{1,0:T(8,128)(2,1)S(1)}, u32[]{:S(2)}, u32[]{:S(2)}) %collective-permute-start.32) | collective-permute-done | bytes 1441824 | tf_op jit(solution)/shard_map/ppermute | solution.py:678
  416.7 4.7 all-to-all-start.8
  427.2 18.0 %attention_backward.1 = (bf16[512,512]{1,0:T(8,128)(2,1)}, bf16[4096,256]{1,0:T(8,128)(2,1)}) custom-call(s32[10]{0:T(128)} %concatenate.58.meta, bf16[512,512]{1,0:T(8,128)(2,1)} %get-tuple-element.176.q, bf16[512,512]{1,0:T(8,128)(2,1)} %get-tuple-element.239.attn.o.right, bf16[512,2048]{1,0:T(8,128)(2,1)} %bitcast.18.g_proj.left, ...), custom_call_target="tpu_custom_call" | custom-call | flops 5368709120 | bytes 6291456 | tf_op jit(solution)/shard_map/attention_backward/pallas_call | solution.py:288
  445.2 12.6 %collective-permute-done.33 = bf16[256,1408]{1,0:T(8,128)(2,1)} collective-permute-done((bf16[256,1408]{1,0:T(8,128)(2,1)}, bf16[256,1408]{1,0:T(8,128)(2,1)}, u32[]{:S(2)}, u32[]{:S(2)}) %collective-permute-start.33) | collective-permute-done | bytes 720928 | tf_op jit(solution)/shard_map/ppermute | solution.py:678
  461.4 5.3 all-to-all-done.8.parts
  470.7 3.5 outer.23
  484.7 3.5 outer.21
  490.3 9.2 %collective-permute-done.37 = bf16[512,256]{1,0:T(8,128)(2,1)S(1)} collective-permute-done((bf16[512,256]{1,0:T(8,128)(2,1)S(1)}, bf16[512,256]{1,0:T(8,128)(2,1)S(1)}, u32[]{:S(2)}, u32[]{:S(2)}) %collective-permute-start.37) | collective-permute-done | bytes 262176 | tf_op jit(solution)/shard_map/ppermute | solution.py:678
  499.5 5.1 collective-permute-done.39
  505.8 9.2 %qkv_grad.1 = (bf16[512,2048]{1,0:T(8,128)(2,1)}, bf16[512,2048]{1,0:T(8,128)(2,1)}) custom-call(bf16[512,512]{1,0:T(8,128)(2,1)} %get-tuple-element.237.right.grad_q, bf16[512,256]{1,0:T(8,128)(2,1)} %pad_maximum_fusion.6.grad_kv.right, bf16[512,2048]{1,0:T(8,128)(2,1)} %bitcast.78, f32[512,1]{1,0:T(8,128)} %get-tuple-element.244.scale, ...), custom_call_target="tpu_custom_call" | custom-call | flops 1879048192 | bytes 6555648 | tf_op jit(solution)/shard_map/qkv_grad/pallas_call | solution.py:314
  515.0 4.8 all-to-all-start.9
  532.0 25.7 %collective-permute-done.43 = bf16[256,1408]{1,0:T(8,128)(2,1)S(1)} collective-permute-done((bf16[256,1408]{1,0:T(8,128)(2,1)S(1)}, bf16[256,1408]{1,0:T(8,128)(2,1)S(1)}, u32[]{:S(2)}, u32[]{:S(2)}) %collective-permute-start.43) | collective-permute-done | bytes 720928 | tf_op jit(solution)/shard_map/ppermute | solution.py:678
  561.8 6.4 %all-to-all-start.10 = ((bf16[4,64,4224]{2,1,0:T(8,128)(2,1)}), bf16[4,64,4224]{2,1,0:T(8,128)(2,1)S(1)}, u32[]{:S(2)}, u32[]{:S(2)}) async-start(bf16[4,64,4224]{2,1,0:T(8,128)(2,1)} %bitcast.70), calls=%async_computation.11 | async-start | bytes 4325376 | tf_op jit(solution)/shard_map/all_to_all | solution.py:699
  571.7 3.4 output.1.array
  577.1 3.9 token_grad.1.array
  585.6 18.3 %collective-permute-done.44 = bf16[256,1024]{1,0:T(8,128)(2,1)S(1)} collective-permute-done((bf16[256,1024]{1,0:T(8,128)(2,1)S(1)}, bf16[256,1024]{1,0:T(8,128)(2,1)S(1)}, u32[]{:S(2)}, u32[]{:S(2)}) %collective-permute-start.44) | collective-permute-done | bytes 524320 | tf_op jit(solution)/shard_map/ppermute | solution.py:678
  612.9 12.0 %all_to_all.60 = bf16[4,64,1408]{2,1,0:T(8,128)(2,1)S(1)} all-to-all(bf16[4,64,1408]{2,1,0:T(8,128)(2,1)S(1)} %bitcast.76), channel_id=1, replica_groups=mesh['far'=2,'x'=2,'core'=2,'zh'=2,'zl'=2] {'x','zl'}, dimensions={0} | all-to-all | bytes 1441792 | tf_op jit(solution)/shard_map/all_to_all | solution.py:699
  (331 shorter events, 155.1 us)
Async XLA Ops:
  12.8 23.2 %all-to-all-start = ((bf16[4,64,2816]{2,1,0:T(8,128)(2,1)}), bf16[4,64,2816]{2,1,0:T(8,128)(2,1)S(1)}, u32[]{:S(2)}, u32[]{:S(2)}) async-start(bf16[4,64,2816]{2,1,0:T(8,128)(2,1)} %pack.2), calls=%async_computation | async-start | bytes 2883584 | tf_op jit(solution)/shard_map/all_to_all | solution.py:699
  36.0 37.8 %all-to-all-start.1 = ((bf16[4,128,2048]{2,1,0:T(8,128)(2,1)}), bf16[4,128,2048]{2,1,0:T(8,128)(2,1)S(1)}, u32[]{:S(2)}, u32[]{:S(2)}) async-start(bf16[4,128,2048]{2,1,0:T(8,128)(2,1)} %get-tuple-element.140), calls=%async_computation.1 | async-start | bytes 4194304 | tf_op jit(solution)/shard_map/all_to_all | solution.py:699
  39.7 99.3 %all-gather.3.cloned.1.call-start = ((), (), s32[]{:S(2)}) async-start(), calls=%async_computation.13 | async-start | bytes 2359296 | tf_op jit(solution)/shard_map/all_gather | solution.py:752
  40.5 31.2 %collective-permute-start = (bf16[256,896]{1,0:T(8,128)(2,1)}, bf16[256,896]{1,0:T(8,128)(2,1)}, u32[]{:S(2)}, u32[]{:S(2)}) collective-permute-start(bf16[256,896]{1,0:T(8,128)(2,1)} %slice.222.refs_0_), channel_id=1, source_target_pairs={{0,2},{2,0},{1,3},{3,1},{4,6},{6,4},{5,7},{7,5},{8,10},{10,8},{9,1... | collective-permute-start | bytes 1376264 | tf_op jit(solution)/shard_map/ppermute | solution.py:678
  43.2 28.6 %collective-permute-start.1 = (bf16[256,896]{1,0:T(8,128)(2,1)}, bf16[256,896]{1,0:T(8,128)(2,1)}, u32[]{:S(2)}, u32[]{:S(2)}) collective-permute-start(bf16[256,896]{1,0:T(8,128)(2,1)} %slice.222.refs_0_), channel_id=1, source_target_pairs={{0,16},{16,0},{1,17},{17,1},{2,18},{18,2},{3,19},{19,3},{4,20},{20... | collective-permute-start | bytes 1376264 | tf_op jit(solution)/shard_map/ppermute | solution.py:678
  73.9 167.1 %all-gather.5.cloned.1.call-start = ((), (), s32[]{:S(2)}) async-start(), calls=%async_computation.14 | async-start | bytes 6488064 | tf_op jit(solution)/shard_map/all_gather | solution.py:752
  75.5 14.8 %collective-permute-start.4 = (bf16[256,896]{1,0:T(8,128)(2,1)}, bf16[256,896]{1,0:T(8,128)(2,1)}, u32[]{:S(2)}, u32[]{:S(2)}) collective-permute-start(bf16[256,896]{1,0:T(8,128)(2,1)} %collective-permute-done.refs_1_), channel_id=1, source_target_pairs={{0,4},{4,0},{1,5},{5,1},{2,6},{6,2},{3,7},{7,3},{8,12},{12,8},{9,1... | collective-permute-start | bytes 1376264 | tf_op jit(solution)/shard_map/ppermute | solution.py:678
  75.6 14.8 %collective-permute-start.3 = (bf16[256,896]{1,0:T(8,128)(2,1)}, bf16[256,896]{1,0:T(8,128)(2,1)}, u32[]{:S(2)}, u32[]{:S(2)}) collective-permute-start(bf16[256,896]{1,0:T(8,128)(2,1)} %slice.222.refs_0_), channel_id=1, source_target_pairs={{0,4},{4,0},{1,5},{5,1},{2,6},{6,2},{3,7},{7,3},{8,12},{12,8},{9,1... | collective-permute-start | bytes 1376264 | tf_op jit(solution)/shard_map/ppermute | solution.py:678
  76.1 14.3 %collective-permute-start.5 = (bf16[256,896]{1,0:T(8,128)(2,1)}, bf16[256,896]{1,0:T(8,128)(2,1)}, u32[]{:S(2)}, u32[]{:S(2)}) collective-permute-start(bf16[256,896]{1,0:T(8,128)(2,1)} %collective-permute-done.1.refs_2_), channel_id=1, source_target_pairs={{0,4},{4,0},{1,5},{5,1},{2,6},{6,2},{3,7},{7,3},{8,12},{12,8},{9,1... | collective-permute-start | bytes 1376264 | tf_op jit(solution)/shard_map/ppermute | solution.py:678
  98.0 34.6 %all-to-all-start.2 = ((bf16[4,64,2816]{2,1,0:T(8,128)(2,1)}), bf16[4,64,2816]{2,1,0:T(8,128)(2,1)S(1)}, u32[]{:S(2)}, u32[]{:S(2)}) async-start(bf16[4,64,2816]{2,1,0:T(8,128)(2,1)} %pack.3), calls=%async_computation.2 | async-start | bytes 2883584 | tf_op jit(solution)/shard_map/all_to_all | solution.py:699
  105.3 25.1 %collective-permute-start.7 = (bf16[512,256]{1,0:T(8,128)(2,1)S(1)}, bf16[512,256]{1,0:T(8,128)(2,1)S(1)}, u32[]{:S(2)}, u32[]{:S(2)}) collective-permute-start(bf16[512,256]{1,0:T(8,128)(2,1)S(1)} %copy-done.52), channel_id=1, source_target_pairs={{0,2},{2,0},{1,3},{3,1},{4,6},{6,4},{5,7},{7,5},{8,10},{10,8},{9,1... | collective-permute-start | bytes 786440 | tf_op jit(solution)/shard_map/ppermute | solution.py:678
  105.3 25.1 %collective-permute-start.8 = (bf16[512,256]{1,0:T(8,128)(2,1)S(1)}, bf16[512,256]{1,0:T(8,128)(2,1)S(1)}, u32[]{:S(2)}, u32[]{:S(2)}) collective-permute-start(bf16[512,256]{1,0:T(8,128)(2,1)S(1)} %copy-done.52), channel_id=1, source_target_pairs={{0,16},{16,0},{1,17},{17,1},{2,18},{18,2},{3,19},{19,3},{4,20},{20... | collective-permute-start | bytes 786440 | tf_op jit(solution)/shard_map/ppermute | solution.py:678
  139.7 49.3 %all-to-all-start.3 = ((bf16[4,128,2048]{2,1,0:T(8,128)(2,1)}), bf16[4,128,2048]{2,1,0:T(8,128)(2,1)S(1)}, u32[]{:S(2)}, u32[]{:S(2)}) async-start(bf16[4,128,2048]{2,1,0:T(8,128)(2,1)} %get-tuple-element.180), calls=%async_computation.3 | async-start | bytes 4194304 | tf_op jit(solution)/shard_map/all_to_all | solution.py:699
  145.2 43.1 %collective-permute-start.14 = (bf16[128,1408]{1,0:T(8,128)(2,1)S(1)}, bf16[128,1408]{1,0:T(8,128)(2,1)S(1)}, u32[]{:S(2)}, u32[]{:S(2)}) collective-permute-start(bf16[128,1408]{1,0:T(8,128)(2,1)S(1)} %get-tuple-element.193), channel_id=1, source_target_pairs={{0,2},{2,0},{1,3},{3,1},{4,6},{6,4},{5,7},{7,5},{8,10},{10,8},{9,1... | collective-permute-start | bytes 1081352 | tf_op jit(solution)/shard_map/ppermute | solution.py:678
  148.7 40.3 %collective-permute-start.15 = (bf16[128,1408]{1,0:T(8,128)(2,1)S(1)}, bf16[128,1408]{1,0:T(8,128)(2,1)}, u32[]{:S(2)}, u32[]{:S(2)}) collective-permute-start(bf16[128,1408]{1,0:T(8,128)(2,1)S(1)} %get-tuple-element.193), channel_id=1, source_target_pairs={{0,16},{16,0},{1,17},{17,1},{2,18},{18,2},{3,19},{19,3},{4,20},{20... | collective-permute-start | bytes 1081352 | tf_op jit(solution)/shard_map/ppermute | solution.py:678
  194.8 46.2 %all-to-all-start.4 = ((bf16[4,128,2048]{2,1,0:T(8,128)(2,1)}), bf16[4,128,2048]{2,1,0:T(8,128)(2,1)S(1)}, u32[]{:S(2)}, u32[]{:S(2)}) async-start(bf16[4,128,2048]{2,1,0:T(8,128)(2,1)} %bitcast.71), calls=%async_computation.4 | async-start | bytes 4194304 | tf_op jit(solution)/shard_map/all_to_all | solution.py:699
  202.8 31.5 %collective-permute-start.19 = (bf16[128,1408]{1,0:T(8,128)(2,1)S(1)}, bf16[128,1408]{1,0:T(8,128)(2,1)S(1)}, u32[]{:S(2)}, u32[]{:S(2)}) collective-permute-start(bf16[128,1408]{1,0:T(8,128)(2,1)S(1)} %get-tuple-element.200), channel_id=1, source_target_pairs={{0,2},{2,0},{1,3},{3,1},{4,6},{6,4},{5,7},{7,5},{8,10},{10,8},{9,1... | collective-permute-start | bytes 1081352 | tf_op jit(solution)/shard_map/ppermute | solution.py:678
  202.9 31.4 %collective-permute-start.20 = (bf16[128,1408]{1,0:T(8,128)(2,1)S(1)}, bf16[128,1408]{1,0:T(8,128)(2,1)S(1)}, u32[]{:S(2)}, u32[]{:S(2)}) collective-permute-start(bf16[128,1408]{1,0:T(8,128)(2,1)S(1)} %get-tuple-element.200), channel_id=1, source_target_pairs={{0,16},{16,0},{1,17},{17,1},{2,18},{18,2},{3,19},{19,3},{4,20},{20... | collective-permute-start | bytes 1081352 | tf_op jit(solution)/shard_map/ppermute | solution.py:678
  204.0 34.8 %collective-permute-start.17 = (bf16[128,1408]{1,0:T(8,128)(2,1)S(1)}, bf16[128,1408]{1,0:T(8,128)(2,1)S(1)}, u32[]{:S(2)}, u32[]{:S(2)}) collective-permute-start(bf16[128,1408]{1,0:T(8,128)(2,1)S(1)} %copy-done.29), channel_id=1, source_target_pairs={{0,2},{2,0},{1,3},{3,1},{4,6},{6,4},{5,7},{7,5},{8,10},{10,8},{9,1... | collective-permute-start | bytes 1081352 | tf_op jit(solution)/shard_map/ppermute | solution.py:678
  206.9 32.0 %collective-permute-start.18 = (bf16[128,1408]{1,0:T(8,128)(2,1)S(1)}, bf16[128,1408]{1,0:T(8,128)(2,1)S(1)}, u32[]{:S(2)}, u32[]{:S(2)}) collective-permute-start(bf16[128,1408]{1,0:T(8,128)(2,1)S(1)} %copy-done.29), channel_id=1, source_target_pairs={{0,16},{16,0},{1,17},{17,1},{2,18},{18,2},{3,19},{19,3},{4,20},{20... | collective-permute-start | bytes 1081352 | tf_op jit(solution)/shard_map/ppermute | solution.py:678
  207.8 31.8 %collective-permute-start.16 = (bf16[128,1408]{1,0:T(8,128)(2,1)}, bf16[128,1408]{1,0:T(8,128)(2,1)}, u32[]{:S(2)}, u32[]{:S(2)}) collective-permute-start(bf16[128,1408]{1,0:T(8,128)(2,1)} %copy-done.35), channel_id=1, source_target_pairs={{0,16},{16,0},{1,17},{17,1},{2,18},{18,2},{3,19},{19,3},{4,20},{20... | collective-permute-start | bytes 1081352 | tf_op jit(solution)/shard_map/ppermute | solution.py:678
  241.9 25.0 %collective-permute-start.26 = (bf16[128,1408]{1,0:T(8,128)(2,1)S(1)}, bf16[128,1408]{1,0:T(8,128)(2,1)}, u32[]{:S(2)}, u32[]{:S(2)}) collective-permute-start(bf16[128,1408]{1,0:T(8,128)(2,1)S(1)} %get-tuple-element.203), channel_id=1, source_target_pairs={{0,2},{2,0},{1,3},{3,1},{4,6},{6,4},{5,7},{7,5},{8,10},{10,8},{9,1... | collective-permute-start | bytes 1081352 | tf_op jit(solution)/shard_map/ppermute | solution.py:678
  243.9 25.1 %collective-permute-start.27 = (bf16[128,1408]{1,0:T(8,128)(2,1)S(1)}, bf16[128,1408]{1,0:T(8,128)(2,1)}, u32[]{:S(2)}, u32[]{:S(2)}) collective-permute-start(bf16[128,1408]{1,0:T(8,128)(2,1)S(1)} %get-tuple-element.203), channel_id=1, source_target_pairs={{0,16},{16,0},{1,17},{17,1},{2,18},{18,2},{3,19},{19,3},{4,20},{20... | collective-permute-start | bytes 1081352 | tf_op jit(solution)/shard_map/ppermute | solution.py:678
  245.9 17.3 %collective-permute-start.24 = (bf16[128,1408]{1,0:T(8,128)(2,1)}, bf16[128,1408]{1,0:T(8,128)(2,1)}, u32[]{:S(2)}, u32[]{:S(2)}) collective-permute-start(bf16[128,1408]{1,0:T(8,128)(2,1)} %copy-done.37), channel_id=1, source_target_pairs={{0,16},{16,0},{1,17},{17,1},{2,18},{18,2},{3,19},{19,3},{4,20},{20... | collective-permute-start | bytes 1081352 | tf_op jit(solution)/shard_map/ppermute | solution.py:678
  248.1 18.6 %collective-permute-start.22 = (bf16[128,1408]{1,0:T(8,128)(2,1)S(1)}, bf16[128,1408]{1,0:T(8,128)(2,1)S(1)}, u32[]{:S(2)}, u32[]{:S(2)}) collective-permute-start(bf16[128,1408]{1,0:T(8,128)(2,1)S(1)} %collective-permute-done.17), channel_id=1, source_target_pairs={{0,16},{16,0},{1,17},{17,1},{2,18},{18,2},{3,19},{19,3},{4,20},{20... | collective-permute-start | bytes 1081352 | tf_op jit(solution)/shard_map/ppermute | solution.py:678
  254.3 27.2 %all-to-all-start.5 = ((bf16[4,128,2048]{2,1,0:T(8,128)(2,1)}), bf16[4,128,2048]{2,1,0:T(8,128)(2,1)S(1)}, u32[]{:S(2)}, u32[]{:S(2)}) async-start(bf16[4,128,2048]{2,1,0:T(8,128)(2,1)} %get-tuple-element.192), calls=%async_computation.5 | async-start | bytes 4194304 | tf_op jit(solution)/shard_map/all_to_all | solution.py:699
  262.3 15.7 %collective-permute-start.21 = (bf16[512,1408]{1,0:T(8,128)(2,1)}, bf16[512,1408]{1,0:T(8,128)(2,1)S(1)}, u32[]{:S(2)}, u32[]{:S(2)}) collective-permute-start(bf16[512,1408]{1,0:T(8,128)(2,1)} %constant_dynamic-update-slice_fusion.refs_0_), channel_id=1, source_target_pairs={{0,4},{4,0},{1,5},{5,1},{2,6},{6,2},{3,7},{7,3},{8,12},{12,8},{9,1... | collective-permute-start | bytes 4325384 | tf_op jit(solution)/shard_map/ppermute | solution.py:678
  264.9 13.2 %collective-permute-start.25 = (bf16[512,1408]{1,0:T(8,128)(2,1)}, bf16[512,1408]{1,0:T(8,128)(2,1)S(1)}, u32[]{:S(2)}, u32[]{:S(2)}) collective-permute-start(bf16[512,1408]{1,0:T(8,128)(2,1)} %constant_dynamic-update-slice_fusion.8.refs_4_), channel_id=1, source_target_pairs={{0,4},{4,0},{1,5},{5,1},{2,6},{6,2},{3,7},{7,3},{8,12},{12,8},{9,1... | collective-permute-start | bytes 4325384 | tf_op jit(solution)/shard_map/ppermute | solution.py:678
  315.7 30.7 %all-to-all-start.6 = ((bf16[4,128,2048]{2,1,0:T(8,128)(2,1)}), bf16[4,128,2048]{2,1,0:T(8,128)(2,1)}, u32[]{:S(2)}, u32[]{:S(2)}) async-start(bf16[4,128,2048]{2,1,0:T(8,128)(2,1)} %bitcast.81), calls=%async_computation.6 | async-start | bytes 4194304 | tf_op jit(solution)/shard_map/all_to_all | solution.py:699
  329.7 26.1 %collective-permute-start.35 = (bf16[1024,1408]{1,0:T(8,128)(2,1)}, bf16[1024,1408]{1,0:T(8,128)(2,1)}, u32[]{:S(2)}, u32[]{:S(2)}) collective-permute-start(bf16[1024,1408]{1,0:T(8,128)(2,1)} %outer.18), channel_id=1, source_target_pairs={{0,4},{4,0},{1,5},{5,1},{2,6},{6,2},{3,7},{7,3},{8,12},{12,8},{9,1... | collective-permute-start | bytes 8650760 | tf_op jit(solution)/shard_map/ppermute | solution.py:678
  334.4 32.8 %collective-permute-start.31 = (bf16[1024,1408]{1,0:T(8,128)(2,1)}, bf16[1024,1408]{1,0:T(8,128)(2,1)}, u32[]{:S(2)}, u32[]{:S(2)}) collective-permute-start(bf16[1024,1408]{1,0:T(8,128)(2,1)} %outer.16), channel_id=1, source_target_pairs={{0,4},{4,0},{1,5},{5,1},{2,6},{6,2},{3,7},{7,3},{8,12},{12,8},{9,1... | collective-permute-start | bytes 8650760 | tf_op jit(solution)/shard_map/ppermute | solution.py:678
  351.3 65.4 %all-to-all-start.7 = ((bf16[4,128,2048]{2,1,0:T(8,128)(2,1)}), bf16[4,128,2048]{2,1,0:T(8,128)(2,1)}, u32[]{:S(2)}, u32[]{:S(2)}) async-start(bf16[4,128,2048]{2,1,0:T(8,128)(2,1)} %get-tuple-element.220), calls=%async_computation.7 | async-start | bytes 4194304 | tf_op jit(solution)/shard_map/all_to_all | solution.py:699
  355.7 105.7 %reduce-scatter.2.cloned.1.call-start = ((), (), s32[]{:S(2)}) async-start(), calls=%async_computation.15 | async-start | bytes 3604480 | tf_op jit(solution)/shard_map/reduce_scatter | solution.py:756
  366.2 49.1 %collective-permute-start.32 = (bf16[512,1408]{1,0:T(8,128)(2,1)S(1)}, bf16[512,1408]{1,0:T(8,128)(2,1)S(1)}, u32[]{:S(2)}, u32[]{:S(2)}) collective-permute-start(bf16[512,1408]{1,0:T(8,128)(2,1)S(1)} %slice.183), channel_id=1, source_target_pairs={{0,16},{16,0},{1,17},{17,1},{2,18},{18,2},{3,19},{19,3},{4,20},{20... | collective-permute-start | bytes 4325384 | tf_op jit(solution)/shard_map/ppermute | solution.py:678
  416.7 49.9 %all-to-all-start.8 = ((bf16[4,128,2048]{2,1,0:T(8,128)(2,1)}), bf16[4,128,2048]{2,1,0:T(8,128)(2,1)}, u32[]{:S(2)}, u32[]{:S(2)}) async-start(bf16[4,128,2048]{2,1,0:T(8,128)(2,1)} %bitcast.79), calls=%async_computation.8 | async-start | bytes 4194304 | tf_op jit(solution)/shard_map/all_to_all | solution.py:699
  421.6 38.4 %collective-permute-start.34 = (bf16[512,1408]{1,0:T(8,128)(2,1)S(1)}, bf16[512,1408]{1,0:T(8,128)(2,1)S(1)}, u32[]{:S(2)}, u32[]{:S(2)}) collective-permute-start(bf16[512,1408]{1,0:T(8,128)(2,1)S(1)} %slice.187), channel_id=1, source_target_pairs={{0,16},{16,0},{1,17},{17,1},{2,18},{18,2},{3,19},{19,3},{4,20},{20... | collective-permute-start | bytes 4325384 | tf_op jit(solution)/shard_map/ppermute | solution.py:678
  424.6 33.2 %collective-permute-start.33 = (bf16[256,1408]{1,0:T(8,128)(2,1)}, bf16[256,1408]{1,0:T(8,128)(2,1)}, u32[]{:S(2)}, u32[]{:S(2)}) collective-permute-start(bf16[256,1408]{1,0:T(8,128)(2,1)} %slice.185), channel_id=1, source_target_pairs={{0,2},{2,0},{1,3},{3,1},{4,6},{6,4},{5,7},{7,5},{8,10},{10,8},{9,1... | collective-permute-start | bytes 2162696 | tf_op jit(solution)/shard_map/ppermute | solution.py:678
  478.1 21.3 %collective-permute-start.37 = (bf16[512,256]{1,0:T(8,128)(2,1)S(1)}, bf16[512,256]{1,0:T(8,128)(2,1)S(1)}, u32[]{:S(2)}, u32[]{:S(2)}) collective-permute-start(bf16[512,256]{1,0:T(8,128)(2,1)S(1)} %get-tuple-element.276), channel_id=1, source_target_pairs={{0,2},{2,0},{16,18},{18,16},{1,3},{3,1},{17,19},{19,17},{4,6},{6,4... | collective-permute-start | bytes 786440 | tf_op jit(solution)/shard_map/ppermute | solution.py:678
  479.3 20.2 %collective-permute-start.38 = (bf16[512,256]{1,0:T(8,128)(2,1)S(1)}, bf16[512,256]{1,0:T(8,128)(2,1)S(1)}, u32[]{:S(2)}, u32[]{:S(2)}) collective-permute-start(bf16[512,256]{1,0:T(8,128)(2,1)S(1)} %get-tuple-element.275), channel_id=1, source_target_pairs={{0,16},{2,18},{16,0},{18,2},{1,17},{3,19},{17,1},{19,3},{4,20},{6,... | collective-permute-start | bytes 786440 | tf_op jit(solution)/shard_map/ppermute | solution.py:678
  480.3 24.2 %collective-permute-start.39 = (bf16[512,256]{1,0:T(8,128)(2,1)S(1)}, bf16[512,256]{1,0:T(8,128)(2,1)S(1)}, u32[]{:S(2)}, u32[]{:S(2)}) collective-permute-start(bf16[512,256]{1,0:T(8,128)(2,1)S(1)} %get-tuple-element.274), channel_id=1, source_target_pairs={{0,18},{2,16},{16,2},{18,0},{1,19},{3,17},{17,3},{19,1},{4,22},{6,... | collective-permute-start | bytes 786440 | tf_op jit(solution)/shard_map/ppermute | solution.py:678
  515.0 44.9 %all-to-all-start.9 = ((bf16[4,128,2048]{2,1,0:T(8,128)(2,1)}), bf16[4,128,2048]{2,1,0:T(8,128)(2,1)}, u32[]{:S(2)}, u32[]{:S(2)}) async-start(bf16[4,128,2048]{2,1,0:T(8,128)(2,1)} %bitcast.80), calls=%async_computation.10 | async-start | bytes 4194304 | tf_op jit(solution)/shard_map/all_to_all | solution.py:699
  520.2 37.4 %collective-permute-start.43 = (bf16[256,1408]{1,0:T(8,128)(2,1)S(1)}, bf16[256,1408]{1,0:T(8,128)(2,1)S(1)}, u32[]{:S(2)}, u32[]{:S(2)}) collective-permute-start(bf16[256,1408]{1,0:T(8,128)(2,1)S(1)} %slice.201), channel_id=1, source_target_pairs={{0,2},{2,0},{1,3},{3,1},{4,6},{6,4},{5,7},{7,5},{8,10},{10,8},{9,1... | collective-permute-start | bytes 2162696 | tf_op jit(solution)/shard_map/ppermute | solution.py:678
  527.0 30.9 %collective-permute-start.41 = (bf16[1024,384]{1,0:T(8,128)(2,1)S(1)}, bf16[1024,384]{1,0:T(8,128)(2,1)S(1)}, u32[]{:S(2)}, u32[]{:S(2)}) collective-permute-start(bf16[1024,384]{1,0:T(8,128)(2,1)S(1)} %pad_maximum_fusion.2), channel_id=1, source_target_pairs={{0,4},{4,0},{1,5},{5,1},{2,6},{6,2},{3,7},{7,3},{8,12},{12,8},{9,1... | collective-permute-start | bytes 2359304 | tf_op jit(solution)/shard_map/ppermute | solution.py:678
  527.1 31.8 %collective-permute-start.42 = (bf16[512,1024]{1,0:T(8,128)(2,1)S(1)}, bf16[512,1024]{1,0:T(8,128)(2,1)S(1)}, u32[]{:S(2)}, u32[]{:S(2)}) collective-permute-start(bf16[512,1024]{1,0:T(8,128)(2,1)S(1)} %slice.199), channel_id=1, source_target_pairs={{0,16},{16,0},{1,17},{17,1},{2,18},{18,2},{3,19},{19,3},{4,20},{20... | collective-permute-start | bytes 3145736 | tf_op jit(solution)/shard_map/ppermute | solution.py:678
  561.8 47.1 %all-to-all-start.10 = ((bf16[4,64,4224]{2,1,0:T(8,128)(2,1)}), bf16[4,64,4224]{2,1,0:T(8,128)(2,1)S(1)}, u32[]{:S(2)}, u32[]{:S(2)}) async-start(bf16[4,64,4224]{2,1,0:T(8,128)(2,1)} %bitcast.70), calls=%async_computation.11 | async-start | bytes 4325376 | tf_op jit(solution)/shard_map/all_to_all | solution.py:699
  569.2 14.1 %collective-permute-start.45 = (bf16[512,384]{1,0:T(8,128)(2,1)S(1)}, bf16[512,384]{1,0:T(8,128)(2,1)S(1)}, u32[]{:S(2)}, u32[]{:S(2)}) collective-permute-start(bf16[512,384]{1,0:T(8,128)(2,1)S(1)} %slice.205), channel_id=1, source_target_pairs={{0,16},{16,0},{1,17},{17,1},{2,18},{18,2},{3,19},{19,3},{4,20},{20... | collective-permute-start | bytes 1179656 | tf_op jit(solution)/shard_map/ppermute | solution.py:678
  570.3 33.7 %collective-permute-start.44 = (bf16[256,1024]{1,0:T(8,128)(2,1)S(1)}, bf16[256,1024]{1,0:T(8,128)(2,1)S(1)}, u32[]{:S(2)}, u32[]{:S(2)}) collective-permute-start(bf16[256,1024]{1,0:T(8,128)(2,1)S(1)} %slice.203), channel_id=1, source_target_pairs={{0,2},{2,0},{1,3},{3,1},{4,6},{6,4},{5,7},{7,5},{8,10},{10,8},{9,1... | collective-permute-start | bytes 1572872 | tf_op jit(solution)/shard_map/ppermute | solution.py:678
  583.5 23.2 %collective-permute-start.46 = (bf16[256,384]{1,0:T(8,128)(2,1)S(1)}, bf16[256,384]{1,0:T(8,128)(2,1)S(1)}, u32[]{:S(2)}, u32[]{:S(2)}) collective-permute-start(bf16[256,384]{1,0:T(8,128)(2,1)S(1)} %slice.236), channel_id=1, source_target_pairs={{0,2},{2,0},{1,3},{3,1},{4,6},{6,4},{5,7},{7,5},{8,10},{10,8},{9,1... | collective-permute-start | bytes 589832 | tf_op jit(solution)/shard_map/ppermute | solution.py:678
  (75 other events, 457.5 us)
Sparse Core Ops, SparseCore 0:
  74.0 38.3 all-gather.2
  114.8 83.0 all-gather.4
  364.8 71.2 reduce-scatter.1
